TPU v7x, 32 devices: a whole 2x2x4 slice. The times are simulated.
32 devices in a mesh: dp: 8 (over y, x, core), mp: 4 (over z).
Axes of the slice: x: 2, y: 2, z: 4, core: 2. Of those that a mesh axis runs over, the one named last changes fastest.
Arguments:
- hidden_in: bfloat16 [4096, 2048], P(('dp', 'mp')), may hold values from -6 to 6
- doc_lengths: int32 [16], replicated, may hold values from 1 to 2048, 4096 in all
- attn_norm: float32 [2048], replicated, may hold values from 0.5 to 1.5
- query_weight: bfloat16 [2048, 2048], P('dp', 'mp'), may hold values from -0.125 to 0.125
- key_weight: bfloat16 [2048, 1024], P('dp', 'mp'), may hold values from -0.125 to 0.125
- value_weight: bfloat16 [2048, 1024], P('dp', 'mp'), may hold values from -0.125 to 0.125
- query_gain: float32 [128], replicated, may hold values from 0.1 to 1.9
- key_gain: float32 [128], replicated, may hold values from 0.1 to 1.9
- output_weight: bfloat16 [2048, 2048], P('mp', 'dp'), may hold values from -0.375 to 0.375
- ffn_norm: float32 [2048], replicated, may hold values from 0.5 to 1.5
- gate_weight: bfloat16 [2048, 6144], P('dp', 'mp'), may hold values from -0.125 to 0.125
- up_weight: bfloat16 [2048, 6144], P('dp', 'mp'), may hold values from -0.125 to 0.125
- down_weight: bfloat16 [6144, 2048], P('mp', 'dp'), may hold values from -0.078125 to 0.078125
- grad_out: bfloat16 [4096, 2048], P(('dp', 'mp')), may hold values from -6 to 6
Outputs:
- result: bfloat16 [4096, 2048], P(('dp', 'mp'))
- grad_hidden: float32 [4096, 2048], P(('dp', 'mp'))
- grad_attn_norm: float32 [2048], replicated
- grad_query: float32 [2048, 2048], P('dp', 'mp')
- grad_key: float32 [2048, 1024], P('dp', 'mp')
- grad_value: float32 [2048, 1024], P('dp', 'mp')
- grad_query_gain: float32 [128], replicated
- grad_key_gain: float32 [128], replicated
- grad_output_weight: float32 [2048, 2048], P('mp', 'dp')
- grad_ffn_norm: float32 [2048], replicated
- grad_gate: float32 [2048, 6144], P('dp', 'mp')
- grad_up: float32 [2048, 6144], P('dp', 'mp')
- grad_down: float32 [6144, 2048], P('mp', 'dp')
Inputs may be any that keep to these rules, and one draw needn't show every extreme that they name: `doc_lengths`: the lengths sum to 4096 and one document is exactly 2048 tokens long.
All inputs are finite; a program needn't handle non-finite values.
Results may differ from a plain program's by a relative error of at most 0.022.
Values may be sent and summed in bfloat16 or wider, within the bound.
No kernel may reach another device: no remote copies, remote signals or barrier semaphores. Data moves between devices by JAX's collectives and lax.ppermute only.
A program may use at most 192 MiB of HBM per device.

v0:
```python
import functools

import jax
import jax.numpy as jnp
from jax import lax
from jax.experimental import pallas as pl
from jax.experimental.pallas import tpu as pltpu
from jax.sharding import PartitionSpec as P

eps_norm = 1e-06
rope_base = 1000000.0
log2_e = 1.4426950408889634
bf16 = jnp.bfloat16
f32 = jnp.float32
longest = 2048
light_cost = pl.CostEstimate(flops=1 << 20, bytes_accessed=1 << 16, transcendentals=0)


def rms_scale(values):
    return lax.rsqrt(jnp.mean(values * values, axis=-1, keepdims=True) + eps_norm)


def norm_back(grad_hat, normed, scale_rows):
    return scale_rows * (grad_hat - normed * jnp.mean(grad_hat * normed, axis=-1, keepdims=True))


def mm(left, right):
    return jnp.dot(left, right, preferred_element_type=f32)


def mm_nt(left, right):
    return lax.dot_general(left, right, (((1,), (1,)), ((), ())), preferred_element_type=f32)


def mm_tn(left, right):
    return lax.dot_general(left, right, (((0,), (0,)), ((), ())), preferred_element_type=f32)


def load_pieces(refs, held_ref, sem_ref):
    rows = refs[0].shape[0]
    copies = [
        pltpu.make_async_copy(ref, held_ref.at[pl.ds(i * rows, rows), :], sem_ref.at[i])
        for i, ref in enumerate(refs)
    ]
    for copy in copies:
        copy.start()
    for copy in copies:
        copy.wait()


def gather_rows(src_ref, dst_ref, tok, repeat):
    dim = dst_ref.shape[1]
    for slot in range(src_ref.shape[0] // tok):
        for i in range(repeat):
            at = (slot * repeat + i) * tok
            dst_ref[at:at + tok] = src_ref[slot * tok:(slot + 1) * tok, i * dim:(i + 1) * dim]


def head_lanes(dim):
    head, heads = pl.program_id(0), pl.num_programs(0)
    return pl.ds(pl.multiple_of(head * dim, dim), dim), pl.ds(pl.multiple_of((heads + head) * dim, dim), dim)


def attn_fwd_kernel(flags_ref, base_ref, places_ref, q_ref, *refs, tok, sub, slots, blocks, pieces, repeat, head_dim):
    kv_refs, (o_ref, lse_ref, kv_ref, acc_ref, values_ref, rows_ref, sem_ref) = refs[:pieces], refs[pieces:]
    kb, chunk = tok * sub, tok * repeat
    k_lanes, v_lanes = head_lanes(head_dim)

    @pl.when(pl.program_id(0) == 0)
    def _():
        load_pieces(kv_refs, kv_ref, sem_ref)
        values_ref[:, head_dim:] = jnp.ones((kb, head_dim), bf16)

    gather_rows(q_ref, rows_ref, tok, repeat)
    acc_ref[...] = jnp.zeros_like(acc_ref)

    def run(block, keys, masked):
        values_ref[:, :head_dim] = kv_ref[keys, v_lanes]
        k = kv_ref[keys, k_lanes]
        for slot in range(slots):
            lines = slice(slot * chunk, (slot + 1) * chunk)
            p = jnp.exp2(mm_nt(rows_ref[lines], k))
            if masked:
                start, place = places_ref[lines, 0:1], places_ref[lines, 1:2]
                at = lax.broadcasted_iota(jnp.int32, (chunk, tok), 1)
                bases = [base_ref[block * sub + piece] for piece in range(sub)]
                allowed = jnp.concatenate([(at >= start - base) & (at <= place - base) for base in bases], axis=1)
                p = jnp.where(allowed, p, 0.0)
            acc_ref[lines] += mm(p.astype(bf16), values_ref[...])

    @pl.loop(0, blocks)
    def _(block):
        keys = pl.ds(pl.multiple_of(block * kb, kb), kb)
        pl.when(flags_ref[block] == 1)(lambda: run(block, keys, True))
        pl.when(flags_ref[block] == 2)(lambda: run(block, keys, False))

    for slot in range(slots):
        total = acc_ref[slot * chunk:(slot + 1) * chunk, head_dim:]
        out = acc_ref[slot * chunk:(slot + 1) * chunk, :head_dim] * (1.0 / total)
        for i in range(repeat):
            o_ref[slot * tok:(slot + 1) * tok, i * head_dim:(i + 1) * head_dim] = out[i * tok:(i + 1) * tok].astype(bf16)
        lse_ref[:, slot * chunk:(slot + 1) * chunk] = jnp.log2(total).T[:1]


def attn_bwd_kernel(flags_ref, base_ref, places_ref, q_ref, lse_ref, o_ref, do_ref, *refs, tok, sub, slots, blocks, pieces, repeat, head_dim, dq_scale, dk_scale):
    kv_refs = refs[:pieces]
    dq_ref, near_ref, far_ref, kv_ref, rows_ref, grads_ref, dqt_ref, delta_ref, dka_ref, dva_ref, sem_ref = refs[pieces:]
    kb, chunk = tok * sub, tok * repeat
    k_lanes, v_lanes = head_lanes(head_dim)

    @pl.when(pl.program_id(0) == 0)
    def _():
        load_pieces(kv_refs, kv_ref, sem_ref)

    gather_rows(q_ref, rows_ref, tok, repeat)
    gather_rows(do_ref, grads_ref, tok, repeat)
    dqt_ref[...] = jnp.zeros_like(dqt_ref)
    for slot in range(slots):
        for i in range(repeat):
            lines, lanes = slice(slot * tok, (slot + 1) * tok), slice(i * head_dim, (i + 1) * head_dim)
            prod = do_ref[lines, lanes].astype(f32) * o_ref[lines, lanes].astype(f32)
            at = (slot * repeat + i) * tok
            delta_ref[:, at:at + tok] = jnp.sum(prod.T, axis=0, keepdims=True)

    def run(block, keys, masked):
        k = kv_ref[keys, k_lanes]
        v = kv_ref[keys, v_lanes]
        kt = k.T
        for slot in range(slots):
            lanes = slice(slot * chunk, (slot + 1) * chunk)
            q = rows_ref[lanes]
            do = grads_ref[lanes]
            p = jnp.exp2(mm_nt(k, q) - lse_ref[:, lanes])
            if masked:
                start, place = places_ref[0:1, lanes], places_ref[1:2, lanes]
                at = lax.broadcasted_iota(jnp.int32, (tok, chunk), 0)
                bases = [base_ref[block * sub + piece] for piece in range(sub)]
                allowed = jnp.concatenate([(at >= start - base) & (at <= place - base) for base in bases], axis=0)
                p = jnp.where(allowed, p, 0.0)
            ds = (p * (mm_nt(v, do) - delta_ref[:, lanes])).astype(bf16)
            dva_ref[...] += mm(p.astype(bf16), do)
            dka_ref[...] += mm(ds, q)
            dqt_ref[:, lanes] += mm(kt, ds)

    @pl.loop(0, blocks)
    def _(block):
        keys = pl.ds(pl.multiple_of(block * kb, kb), kb)
        dka_ref[...] = jnp.zeros_like(dka_ref)
        dva_ref[...] = jnp.zeros_like(dva_ref)
        pl.when(flags_ref[block] == 1)(lambda: run(block, keys, True))
        pl.when(flags_ref[block] == 2)(lambda: run(block, keys, False))

        @pl.when(block < blocks // 2)
        def _():
            near_ref[keys, k_lanes] = (dka_ref[...] * dk_scale).astype(bf16)
            near_ref[keys, v_lanes] = dva_ref[...].astype(bf16)

        @pl.when(block >= blocks // 2)
        def _():
            far = pl.ds(pl.multiple_of(block * kb - blocks // 2 * kb, kb), kb)
            far_ref[far, k_lanes] = (dka_ref[...] * dk_scale).astype(bf16)
            far_ref[far, v_lanes] = dva_ref[...].astype(bf16)

    for slot in range(slots):
        out = (dqt_ref[:, slot * chunk:(slot + 1) * chunk] * dq_scale).T
        for i in range(repeat):
            dq_ref[slot * tok:(slot + 1) * tok, i * head_dim:(i + 1) * head_dim] = out[i * tok:(i + 1) * tok]


def turn(values):
    half = values.shape[-1] // 2
    return jnp.concatenate([values[:, half:], values[:, :half]], axis=1)


def ignoring(kernel, at, count):
    def reduced(*refs):
        kernel(*refs[:at], *refs[at + count:])

    return reduced


any_place = pl.BlockSpec(memory_space=pl.ANY)


def rotated_heads(raw, cos_ref, sin_ref, gain_ref, out_ref, head_dim, scale):
    for first in range(0, raw.shape[1], head_dim):
        lanes = slice(first, first + head_dim)
        hat = raw[:, lanes] * rms_scale(raw[:, lanes]) * gain_ref[...]
        out_ref[:, lanes] = ((hat * cos_ref[...] + turn(hat) * sin_ref[...]) * scale).astype(bf16)


def project_kv_kernel(w_ref, cos_ref, sin_ref, gain_ref, norm_ref, *refs, head_dim):
    *slot_refs, x_ref, rows_ref, raw_ref, out_ref = refs
    tok = slot_refs[0].shape[0]
    step = pl.program_id(0)

    @pl.when(step == 0)
    def _():
        for slot, slot_ref in enumerate(slot_refs):
            lines = slice(slot * tok, (slot + 1) * tok)
            values = slot_ref[...].astype(f32)
            scale = rms_scale(values)
            x_ref[lines] = (values * scale * norm_ref[...]).astype(bf16)
            rows_ref[lines] = jnp.broadcast_to(scale, (tok, rows_ref.shape[1]))

    raw = mm(x_ref[...], w_ref[...])

    @pl.when(step == 0)
    def _():
        raw_ref[...] = raw
        rotated_heads(raw, cos_ref, sin_ref, gain_ref, out_ref, head_dim, 1.0)

    @pl.when(step == 1)
    def _():
        out_ref[...] = raw.astype(bf16)


def project_kv(slots, norm, w, cos_table, sin_table, gain, first, tile):
    tok, width = slots[0].shape
    tokens, head_dim = tok * len(slots), gain.shape[1]

    def whole(rows, cols):
        return pl.BlockSpec((rows, cols), lambda j: (0, 0))

    w_spec = pl.BlockSpec((width, tile), lambda j: (0, j + first))
    return pl.pallas_call(
        functools.partial(project_kv_kernel, head_dim=head_dim),
        grid=(2,),
        in_specs=[w_spec, whole(tokens, head_dim), whole(tokens, head_dim), whole(1, head_dim), whole(1, width)]
        + [whole(tok, width)] * len(slots),
        out_specs=[whole(tokens, width), whole(tokens, head_dim), whole(tokens, tile), pl.BlockSpec((tokens, tile), lambda j: (0, j))],
        out_shape=[
            jax.ShapeDtypeStruct((tokens, width), bf16),
            jax.ShapeDtypeStruct((tokens, head_dim), f32),
            jax.ShapeDtypeStruct((tokens, tile), f32),
            jax.ShapeDtypeStruct((tokens, 2 * tile), bf16),
        ],
        cost_estimate=light_cost,
        name="project_kv",
    )(w, cos_table, sin_table, gain, norm, *slots)


def project_q_kernel(x_ref, w_ref, cos_ref, sin_ref, gain_ref, raw_ref, out_ref, *, head_dim, scale):
    raw = mm(x_ref[...], w_ref[...])
    raw_ref[...] = raw
    rotated_heads(raw, cos_ref, sin_ref, gain_ref, out_ref, head_dim, scale)


def project_q(x, w, cos_table, sin_table, gain, cols, tile, scale, after):
    tokens, width = x.shape
    head_dim = gain.shape[1]

    def whole(rows, cols):
        return pl.BlockSpec((rows, cols), lambda j: (0, 0))

    w_spec = pl.BlockSpec((width, tile), lambda j: (0, j))
    out_spec = pl.BlockSpec((tokens, tile), lambda j: (0, j))
    return pl.pallas_call(
        ignoring(functools.partial(project_q_kernel, head_dim=head_dim, scale=scale), 5, len(after)),
        grid=(cols // tile,),
        in_specs=[whole(tokens, width), w_spec, whole(tokens, head_dim), whole(tokens, head_dim), whole(1, head_dim)] + [any_place] * len(after),
        out_specs=[out_spec, out_spec],
        out_shape=[jax.ShapeDtypeStruct((tokens, cols), f32), jax.ShapeDtypeStruct((tokens, cols), bf16)],
        cost_estimate=light_cost,
        name="project_q",
    )(x, w, cos_table, sin_table, gain, *after)


def unproject_kernel(raw_ref, cos_ref, sin_ref, gain_ref, *refs, head_dim, sums):
    grad_refs, (out_ref, part_ref) = refs[:sums], refs[sums:]
    part = jnp.zeros((1, head_dim), f32)
    for first in range(0, out_ref.shape[1], head_dim):
        lanes = slice(first, first + head_dim)
        grad = grad_refs[0][:, lanes].astype(f32)
        for grad_ref in grad_refs[1:]:
            grad = grad + grad_ref[:, lanes].astype(f32)
        if first < raw_ref.shape[1]:
            raw = raw_ref[:, lanes]
            scale = rms_scale(raw)
            hat = raw * scale
            grad = grad * cos_ref[...] - turn(grad) * sin_ref[...]
            part = part + jnp.sum(grad * hat, axis=0, keepdims=True)
            grad = norm_back(grad * gain_ref[...], hat, scale)
        out_ref[:, lanes] = grad.astype(bf16)
    part_ref[...] = part


def unproject(raw, cos_table, sin_table, gain, grads, after, name):
    tokens, cols = raw.shape[0], grads[0].shape[1]
    head_dim = gain.shape[1]

    def first_rows(width):
        return pl.BlockSpec((tokens, width), lambda j: (0, 0))

    gain_spec = pl.BlockSpec((1, head_dim), lambda j: (0, 0))
    return pl.pallas_call(
        ignoring(functools.partial(unproject_kernel, head_dim=head_dim, sums=len(grads)), 4 + len(grads), len(after)),
        grid=(1,),
        in_specs=[first_rows(raw.shape[1]), first_rows(head_dim), first_rows(head_dim), gain_spec]
        + [first_rows(cols)] * len(grads)
        + [any_place] * len(after),
        out_specs=[first_rows(cols), gain_spec],
        out_shape=[
            jax.ShapeDtypeStruct((tokens, cols), bf16),
            jax.ShapeDtypeStruct(gain.shape, f32),
        ],
        cost_estimate=light_cost,
        name=name,
    )(raw, cos_table, sin_table, gain, *grads, *after)


def attn_back_kernel(dq_ref, dkv_ref, w_ref, rows_ref, *refs, slots):
    hidden_refs, out_refs, gain_ref = refs[:slots], refs[slots:-1], refs[-1]
    q_cols = dq_ref.shape[1]
    tok = out_refs[0].shape[0]
    total = mm_nt(dq_ref[...], w_ref[:, :q_cols]) + mm_nt(dkv_ref[...], w_ref[:, q_cols:])
    gain = jnp.zeros((1, total.shape[1]), f32)
    for slot in range(slots):
        lines = slice(slot * tok, (slot + 1) * tok)
        part = total[lines]
        gain = gain + jnp.sum(part * (hidden_refs[slot][...].astype(f32) * rows_ref[lines, :1]), axis=0, keepdims=True)
        out_refs[slot][...] = part.astype(bf16)
    gain_ref[...] = jnp.broadcast_to(gain, gain_ref.shape)


def attn_back_product(dq, dkv, w, row_scales, hidden_slots, after):
    rows, q_cols = dq.shape
    slots = len(hidden_slots)
    tok, width = hidden_slots[0].shape
    tile = min(512, width)
    slot_spec = pl.BlockSpec((tok, tile), lambda t: (0, t))
    return pl.pallas_call(
        ignoring(functools.partial(attn_back_kernel, slots=slots), 4 + slots, len(after)),
        grid=(width // tile,),
        in_specs=[
            pl.BlockSpec((rows, q_cols), lambda t: (0, 0)),
            pl.BlockSpec((rows, dkv.shape[1]), lambda t: (0, 0)),
            pl.BlockSpec((tile, q_cols + dkv.shape[1]), lambda t: (t, 0)),
            pl.BlockSpec(row_scales.shape, lambda t: (0, 0)),
        ]
        + [slot_spec] * slots
        + [any_place] * len(after),
        out_specs=[slot_spec] * slots + [pl.BlockSpec((8, tile), lambda t: (0, t))],
        out_shape=[jax.ShapeDtypeStruct((tok, width), bf16)] * slots + [jax.ShapeDtypeStruct((8, width), f32)],
        cost_estimate=light_cost,
        name="attn_back",
    )(dq, dkv, w, row_scales, *hidden_slots, *after)


def grad_attended_kernel(w_ref, *refs):
    *slot_refs, mid_ref, out_ref = refs
    tok = slot_refs[0].shape[0]
    for slot, slot_ref in enumerate(slot_refs):
        mid_ref[slot * tok:(slot + 1) * tok] = slot_ref[...]
    out_ref[...] = mm(mid_ref[...], w_ref[...]).astype(bf16)


def grad_attended_product(slots, w, cols, after):
    tok, width = slots[0].shape
    rows = tok * len(slots)

    def whole(rows, cols):
        return pl.BlockSpec((rows, cols), lambda j: (0, 0))

    return pl.pallas_call(
        ignoring(grad_attended_kernel, 1 + len(slots), len(after)),
        grid=(1,),
        in_specs=[pl.BlockSpec((width, cols), lambda j: (0, w.shape[1] // cols - 1))] + [whole(tok, width)] * len(slots) + [any_place] * len(after),
        out_specs=[whole(rows, width), whole(rows, cols)],
        out_shape=[jax.ShapeDtypeStruct((rows, width), bf16), jax.ShapeDtypeStruct((rows, cols), bf16)],
        cost_estimate=light_cost,
        name="grad_attended",
    )(w, *slots, *after)


def simple_call(kernel, arrays, shapes, name, after=()):
    vmem = pl.BlockSpec(memory_space=pltpu.VMEM)
    return pl.pallas_call(
        ignoring(kernel, len(arrays), len(after)),
        in_specs=[vmem] * len(arrays) + [any_place] * len(after),
        out_specs=[vmem] * len(shapes),
        out_shape=[jax.ShapeDtypeStruct(shape, dtype) for shape, dtype in shapes],
        cost_estimate=light_cost,
        name=name,
    )(*arrays, *after)


def add_rounded(left, right):
    return (left.astype(f32) + right.astype(f32)).astype(bf16)


def summed(refs):
    count = len(refs) // 2
    return jnp.concatenate(
        [came[...].astype(f32) + part[...].astype(f32) for came, part in zip(refs[:count], refs[count:])],
        axis=0,
    )


def store_halves(values, refs):
    rows = refs[0].shape[0]
    for i, ref in enumerate(refs):
        ref[...] = values[i * rows:(i + 1) * rows].astype(ref.dtype)


def mix_kernel(*refs, halves):
    sum_refs, (hidden_ref, norm_ref, mixed_ref, *input_refs) = refs[:2 * halves], refs[2 * halves:]
    mixed = hidden_ref[...].astype(f32) + summed(sum_refs)
    mixed_ref[...] = mixed
    store_halves(mixed * rms_scale(mixed) * norm_ref[...], input_refs)


def mid_kernel(*refs, halves):
    sum_refs, (mixed_ref, norm_ref, out_ref, grad_ref, gain_ref, *low_refs) = refs[:2 * halves], refs[2 * halves:]
    mixed = mixed_ref[...]
    scale = rms_scale(mixed)
    normed = mixed * scale
    back = summed(sum_refs)
    gain_ref[...] = jnp.sum(back * normed, axis=0, keepdims=True)
    grad = out_ref[...].astype(f32) + norm_back(back * norm_ref[...], normed, scale)
    grad_ref[...] = grad
    store_halves(grad, low_refs)


def last_kernel(*refs, halves):
    sum_refs, (grad_ref, hidden_ref, norm_ref, out_ref) = refs[:2 * halves], refs[2 * halves:]
    hidden = hidden_ref[...].astype(f32)
    scale = rms_scale(hidden)
    out_ref[...] = grad_ref[...] + norm_back(summed(sum_refs) * norm_ref[...], hidden * scale, scale)


def result_kernel(*refs):
    *sum_refs, mixed_ref, out_ref = refs
    total = sum_refs[0][...].astype(f32)
    for sum_ref in sum_refs[1:]:
        total = total + sum_ref[...].astype(f32)
    out_ref[...] = (mixed_ref[...] + total).astype(bf16)


def mark_kernel(out_ref):
    out_ref[...] = jnp.zeros_like(out_ref)


def split_kernel(x_ref, *out_refs):
    at = 0
    for out_ref in out_refs[:-1]:
        out_ref[...] = x_ref[:, at:at + out_ref.shape[1]].astype(f32)
        at += out_ref.shape[1]
    out_refs[-1][...] = x_ref[:, at:].astype(f32).T


def split_columns(x, cols, name):
    rows = x.shape[0]
    shapes = [((rows, c), f32) for c in cols[:-1]] + [((cols[-1], rows), f32)]
    return simple_call(split_kernel, [x], shapes, name)


def ffn_kernel(gate_ref, up_ref, down_ref, *refs, parts, held):
    x_refs, g_refs, refs = refs[:parts], refs[parts:2 * parts], refs[2 * parts + held:]
    grad_ref, x_ref, go_ref, *back_refs, back_ref = refs
    tile = pl.program_id(0)
    tok, size = x_refs[0].shape[0], gate_ref.shape[1]
    ff = grad_ref.shape[1] // 3

    @pl.when(tile == 0)
    def _():
        for i in range(parts):
            x_ref[i * tok:(i + 1) * tok] = x_refs[i][...]
            go_ref[i * tok:(i + 1) * tok] = g_refs[i][...]
        back_ref[...] = jnp.zeros_like(back_ref)

    x = x_ref[...]
    gate_pre = mm(x, gate_ref[...])
    up_value = mm(x, up_ref[...])
    grad_act = mm(go_ref[...], down_ref[...])
    sigmoid_gate = jax.nn.sigmoid(gate_pre)
    gated = gate_pre * sigmoid_gate
    grad_gate_pre = (
        grad_act * up_value * sigmoid_gate * (1.0 + gate_pre * (1.0 - sigmoid_gate))
    ).astype(bf16)
    grad_up_value = (grad_act * gated).astype(bf16)
    for i, values in enumerate([grad_gate_pre, grad_up_value, (gated * up_value).astype(bf16)]):
        grad_ref[:, pl.ds(pl.multiple_of(i * ff + tile * size, size), size)] = values
    back_ref[...] += mm_nt(grad_gate_pre, gate_ref[...]) + mm_nt(grad_up_value, up_ref[...])

    @pl.when(tile == pl.num_programs(0) - 1)
    def _():
        store_halves(back_ref[...], back_refs)


def feed_forward(inputs, grads, w_ffn, held, chunk, chunks):
    parts = len(inputs)
    tok, width = inputs[0].shape
    ff = w_ffn.shape[1] // 3
    size = next(s for s in (512, 384, 256, 128) if ff % s == 0)
    tiles = ff // size
    part_spec = pl.BlockSpec((tok, width), lambda t: (0, 0))

    def rows_spec(cols):
        return pl.BlockSpec((parts * tok, cols), lambda t: (chunk, 0))

    rows = parts * tok * chunks
    return pl.pallas_call(
        functools.partial(ffn_kernel, parts=parts, held=len(held)),
        grid=(tiles,),
        in_specs=[
            pl.BlockSpec((width, size), lambda t: (0, t)),
            pl.BlockSpec((width, size), lambda t: (0, tiles + t)),
            pl.BlockSpec((width, size), lambda t: (0, 2 * tiles + t)),
        ]
        + [part_spec] * (2 * parts)
        + [pl.BlockSpec(memory_space=pl.ANY)] * len(held),
        out_specs=[rows_spec(3 * ff), rows_spec(width), rows_spec(width)] + [part_spec] * parts,
        out_shape=[
            jax.ShapeDtypeStruct((rows, 3 * ff), bf16),
            jax.ShapeDtypeStruct((rows, width), bf16),
            jax.ShapeDtypeStruct((rows, width), bf16),
        ]
        + [jax.ShapeDtypeStruct((tok, width), bf16)] * parts,
        scratch_shapes=[pltpu.VMEM((parts * tok, width), f32)],
        input_output_aliases={3 + 2 * parts + i: i for i in range(len(held))},
        cost_estimate=light_cost,
        name="feed_forward",
    )(w_ffn, w_ffn, w_ffn, *inputs, *grads, *held)


def weight_grads_kernel(*refs, turns):
    *left_refs, right_ref, out_ref, turned_ref = refs
    tile = pl.program_id(0)
    for left_ref, at in zip(left_refs, turns):
        @pl.when(tile == at)
        def _(left_ref=left_ref):
            turned_ref[...] = left_ref[...].T

    rows = min(256, out_ref.shape[0])
    for first in range(0, out_ref.shape[0], rows):
        lines = slice(first, first + rows)
        out_ref[lines] = mm(turned_ref[lines], right_ref[...]).astype(bf16)


def weight_grads(lefts, right, starts, after, name):
    tokens, width = lefts[0].shape
    cols = right.shape[1]
    size = next(s for s in (512, 384, 256, 128) if all(at % s == 0 for at in (cols, *starts)))
    whole = pl.BlockSpec((tokens, width), lambda t: (0, 0))
    return pl.pallas_call(
        ignoring(functools.partial(weight_grads_kernel, turns=[at // size for at in starts]), len(lefts) + 1, len(after)),
        grid=(cols // size,),
        in_specs=[whole] * len(lefts) + [pl.BlockSpec((tokens, size), lambda t: (0, t))] + [any_place] * len(after),
        out_specs=pl.BlockSpec((width, size), lambda t: (0, t)),
        out_shape=jax.ShapeDtypeStruct((width, cols), bf16),
        scratch_shapes=[pltpu.VMEM((width, tokens), bf16)],
        cost_estimate=light_cost,
        name=name,
    )(*lefts, right, *after)


def slot_product_kernel(x_ref, w_ref, *out_refs):
    tok = out_refs[0].shape[0]
    total = mm_nt(x_ref[...], w_ref[...])
    for slot, out_ref in enumerate(out_refs):
        out_ref[...] = total[slot * tok:(slot + 1) * tok].astype(bf16)


def slot_product(x, x_block, w, w_block, depth, slots, after, name):
    rows, width = x.shape[0], w.shape[0]
    tile = min(512, width)
    out_spec = pl.BlockSpec((rows // slots, tile), lambda t: (0, t))
    return pl.pallas_call(
        ignoring(slot_product_kernel, 2, len(after)),
        grid=(width // tile,),
        in_specs=[
            pl.BlockSpec((rows, depth), lambda t: (0, x_block)),
            pl.BlockSpec((tile, depth), lambda t: (t, w_block)),
        ]
        + [any_place] * len(after),
        out_specs=[out_spec] * slots,
        out_shape=[jax.ShapeDtypeStruct((rows // slots, width), bf16)] * slots,
        cost_estimate=light_cost,
        name=name,
    )(x, w, *after)


def more_grads_kernel(left_ref, *refs, rights):
    right_refs, out_ref, turned_ref = refs[:rights], refs[-2], refs[-1]
    tile = pl.program_id(0)

    @pl.when(tile == 0)
    def _():
        turned_ref[...] = left_ref[...].T

    def run(right_ref):
        rows = min(256, out_ref.shape[0])
        for first in range(0, out_ref.shape[0], rows):
            lines = slice(first, first + rows)
            out_ref[lines] = mm(turned_ref[lines], right_ref[...]).astype(bf16)

    for i, right_ref in enumerate(right_refs):
        pl.when(tile == i)(functools.partial(run, right_ref))


def more_grads(left, rights, held, at, blocks, after, name):
    tokens, width = left.shape
    size = rights[0].shape[1]
    return pl.pallas_call(
        ignoring(functools.partial(more_grads_kernel, rights=len(rights)), 1 + len(rights), len(held) + len(after)),
        grid=(len(rights),),
        in_specs=[pl.BlockSpec((tokens, width), lambda t: (0, 0))]
        + [pl.BlockSpec((tokens, size), lambda t: (0, 0))] * len(rights)
        + [any_place] * (len(held) + len(after)),
        out_specs=pl.BlockSpec((width, size), lambda t: (0, at + t)),
        out_shape=jax.ShapeDtypeStruct((width, blocks * size), bf16),
        scratch_shapes=[pltpu.VMEM((width, tokens), bf16)],
        input_output_aliases={1 + len(rights) + i: 0 for i in range(len(held))},
        cost_estimate=light_cost,
        name=name,
    )(left, *rights, *held, *after)


def fold_kernel(near_ref, got_ref, *out_refs):
    rows = out_refs[0].shape[0]
    for i, out_ref in enumerate(out_refs):
        lines = slice((i + 1) * rows, (i + 2) * rows)
        out_ref[...] = (near_ref[lines].astype(f32) + got_ref[lines].astype(f32)).astype(bf16)


def fold_blocks(near, got, count, after):
    vmem = pl.BlockSpec(memory_space=pltpu.VMEM)
    shape = jax.ShapeDtypeStruct((near.shape[0] // count, near.shape[1]), bf16)
    return pl.pallas_call(
        ignoring(fold_kernel, 2, len(after)),
        in_specs=[vmem, vmem] + [any_place] * len(after),
        out_specs=[vmem] * (count - 1),
        out_shape=[shape] * (count - 1),
        cost_estimate=light_cost,
        name="fold_blocks",
    )(near, got, *after)


def body(
    hidden_in,
    doc_lengths,
    attn_norm,
    query_weight,
    key_weight,
    value_weight,
    query_gain,
    key_gain,
    output_weight,
    ffn_norm,
    gate_weight,
    up_weight,
    down_weight,
    grad_out,
):
    dp_count = lax.axis_size("dp")
    mp_count = lax.axis_size("mp")
    slots = mp_count
    tok, width = hidden_in.shape
    group_rows = tok * mp_count
    head_dim = query_gain.shape[0]
    half_dim = head_dim // 2
    q_cols = query_weight.shape[1]
    k_cols = key_weight.shape[1]
    kv_local = k_cols // head_dim
    repeat = q_cols // k_cols
    ff = gate_weight.shape[1]
    group = lax.axis_index("dp")
    my_z = lax.axis_index("mp")
    score_scale = head_dim ** (-0.5)
    ring = [(i, (i + 1) % mp_count) for i in range(mp_count)]
    near_masks = list(range(0, dp_count, 2))
    masks = near_masks + [mask + 1 for mask in near_masks]
    far_masks = near_masks[1:]

    def tie(value, *others):
        return lax.optimization_barrier((value,) + others)[0]

    def shift(values):
        return lax.ppermute(values, "mp", ring)

    def swap(values, mask):
        return lax.ppermute(values, "dp", [(i, i ^ mask) for i in range(dp_count)])

    reach = (min(longest, group_rows * dp_count) - 2) // group_rows + 1

    def needs(reader, owner):
        first = reader // 2 * 2
        return owner <= first + 1 and owner >= first - reach

    def swap_forward(values, mask):
        pairs = [(i, i ^ mask) for i in range(dp_count) if needs(i ^ mask, i)]
        return lax.ppermute(values, "dp", pairs)

    def swap_back(values, mask):
        pairs = [(i, i ^ mask) for i in range(dp_count) if needs(i, i ^ mask)]
        return lax.ppermute(values, "dp", pairs)

    half = dp_count // 2
    halves = 2
    part_rows = tok // halves
    ids = jnp.array(masks, jnp.int32)
    mask_blocks = group ^ ids
    attn_norm = attn_norm.reshape(1, width)
    ffn_norm = ffn_norm.reshape(1, width)
    part_shape = ((part_rows, width), bf16)

    def tie_all(values, *others):
        return list(lax.optimization_barrier((*values, *others)))[:len(values)]

    def order(values, others):
        both = lax.optimization_barrier((*values, *others))
        return list(both[:len(values)]), list(both[len(values):])

    def mark(*operands):
        (tiny,) = simple_call(mark_kernel, [], [((8, 128), f32)], "mark", operands)
        return [swap(tiny, 1)]

    def flat(slot_lists):
        return [part for slot in slot_lists for part in slot]

    def by_slot(parts):
        return [list(parts[i:i + halves]) for i in range(0, len(parts), halves)]

    def shift_all(parts):
        return [shift(part) for part in parts]

    def ring_add(came, own):
        return [shift(add_rounded(one, other)) for one, other in zip(came, own)]

    w_attn_own = jnp.concatenate([query_weight, key_weight, value_weight, output_weight.T], axis=1)
    w_ffn_own = jnp.concatenate([gate_weight, up_weight, down_weight.T], axis=1)
    w_attn = lax.all_gather(w_attn_own, "dp", axis=0, tiled=True)
    w_ffn = tie(lax.all_gather(w_ffn_own, "dp", axis=0, tiled=True), w_attn)

    doc_ends = jnp.cumsum(doc_lengths)
    slot_offset = ((my_z - jnp.arange(slots, dtype=jnp.int32)) % mp_count) * tok
    places = (
        group * group_rows
        + slot_offset[:, None]
        + jnp.arange(tok, dtype=jnp.int32)[None, :]
    )
    before = doc_ends[None, None, :] <= places[:, :, None]
    starts = jnp.sum(jnp.where(before, doc_lengths[None, None, :], 0), axis=-1)
    position = (places - starts).reshape(group_rows)
    inverse = rope_base ** (-(2.0 * jnp.arange(half_dim, dtype=f32)) / head_dim)
    angles = position.astype(f32)[:, None] * inverse[None, :]
    cos_table, sin_table = jnp.cos(angles), jnp.sin(angles)
    cos_table = jnp.concatenate([cos_table, cos_table], axis=1)
    sin_table = jnp.concatenate([-sin_table, sin_table], axis=1)

    sub = min(4, slots)
    key_base = mask_blocks[:, None] * group_rows + slot_offset[None, :]
    blocks = dp_count * slots // sub
    key_base = key_base.reshape(blocks, sub)
    q_first, q_last = places[:, 0], places[:, -1]
    s_first, s_last = starts[:, 0], starts[:, -1]
    piece_lo, piece_hi = key_base[None], key_base[None] + tok - 1
    some = (piece_lo <= q_last[:, None, None]) & (s_first[:, None, None] <= piece_hi)
    every = (piece_hi <= q_first[:, None, None]) & (s_last[:, None, None] <= piece_lo)
    flags = jnp.where(jnp.all(every, -1), 2, jnp.any(some, -1).astype(jnp.int32)).astype(jnp.int32)
    flags = jnp.where(jnp.all(flags == 2, axis=0), 2, jnp.any(flags > 0, axis=0).astype(jnp.int32))
    key_base = key_base.reshape(-1)
    lane_places = jnp.tile(jnp.stack([starts, places]), (1, 1, repeat)).reshape(2, -1)
    row_places = lane_places.T

    hidden_slots = [[hidden_in[i * part_rows:(i + 1) * part_rows] for i in range(halves)]]
    for slot in range(1, slots):
        came = shift_all(hidden_slots[-1])
        if slot == 1:
            came = tie_all(came, cos_table, sin_table, lane_places, w_ffn_own)
        hidden_slots.append(came)
    q_gain, k_gain = query_gain.reshape(1, head_dim), key_gain.reshape(1, head_dim)
    attn_input, row_scales, key_raw, kv_own = project_kv(
        flat(hidden_slots), attn_norm, w_attn, cos_table, sin_table, k_gain, repeat, k_cols
    )
    kv_came = [swap_forward(kv_own, mask) for mask in far_masks]
    grad_slots = [tie_all([grad_out[i * part_rows:(i + 1) * part_rows] for i in range(halves)], *hidden_slots[-1])]
    grad_slots.append(tie_all(shift_all(grad_slots[-1]), kv_own))
    query_raw, query_rot = project_q(
        tie(attn_input, kv_own, *grad_slots[-1]), w_attn, cos_table, sin_table, q_gain, q_cols, k_cols,
        score_scale * log2_e, [],
    )
    for slot in range(2, slots):
        came = shift_all(grad_slots[-1])
        if slot == 2:
            came = tie_all(came, query_rot)
            kv_came = tie_all(kv_came, *came)
        grad_slots.append(came)
    kv_near = [kv_own] + tie_all(kv_came, query_rot)
    kv_pieces = kv_near + [swap(piece, 1) for piece in kv_near]

    keys_total = dp_count * group_rows
    head_rows = repeat * tok
    smem = pl.BlockSpec(memory_space=pltpu.SMEM)
    any_spec = pl.BlockSpec(memory_space=pl.ANY)
    all_rows = slots * head_rows
    lane_spec = pl.BlockSpec((2, all_rows), lambda h: (0, 0))
    row_spec = pl.BlockSpec((all_rows, 2), lambda h: (0, 0))
    q_spec = pl.BlockSpec((group_rows, repeat * head_dim), lambda h: (0, h))
    lse_spec = pl.BlockSpec((None, 1, all_rows), lambda h: (h, 0, 0))
    dims = dict(
        tok=tok, sub=sub, slots=slots, blocks=blocks, pieces=dp_count, repeat=repeat, head_dim=head_dim
    )
    kv_scratch = pltpu.VMEM((keys_total, 2 * k_cols), bf16)
    attended_low, lse = pl.pallas_call(
        functools.partial(attn_fwd_kernel, **dims),
        grid=(kv_local,),
        in_specs=[smem, smem, row_spec, q_spec] + [any_spec] * dp_count,
        out_specs=[q_spec, lse_spec],
        out_shape=[
            jax.ShapeDtypeStruct((group_rows, q_cols), bf16),
            jax.ShapeDtypeStruct((kv_local, 1, all_rows), f32),
        ],
        scratch_shapes=[
            kv_scratch,
            pltpu.VMEM((all_rows, 2 * head_dim), f32),
            pltpu.VMEM((tok * sub, 2 * head_dim), bf16),
            pltpu.VMEM((all_rows, head_dim), bf16),
            pltpu.SemaphoreType.DMA((dp_count,)),
        ],
        cost_estimate=light_cost,
        name="attn_fwd",
    )(flags, key_base, row_places, query_rot, *kv_pieces)

    grad_slots[slots - 1] = tie_all(grad_slots[slots - 1], attended_low)
    parts = by_slot(slot_product(attended_low, 0, w_attn, 2 * k_cols // q_cols + 1, q_cols, slots * halves, [], "attn_out"))
    came = shift_all(tie_all(parts[1], *grad_slots[-1]))
    for slot in range(2, slots):
        came = ring_add(came, parts[slot])
    mixed_rows, *ffn_input = simple_call(
        functools.partial(mix_kernel, halves=halves),
        [*came, *parts[0], hidden_in, ffn_norm],
        [((tok, width), f32)] + [part_shape] * halves,
        "mix",
    )

    ffn_slots = [ffn_input, shift_all(ffn_input)]
    held, parts = [], []
    for first in range(0, slots, 2):
        *held, = feed_forward(
            flat(ffn_slots[first:first + 2]), flat(grad_slots[first:first + 2]), w_ffn, held, first // 2, slots // 2
        )
        held, back = held[:3], held[3:]
        parts += by_slot(back)
        if first + 2 < slots:
            ffn_slots.append(tie_all(shift_all(ffn_slots[-1]), *back))
            ffn_slots.append(shift_all(ffn_slots[-1]))
    ffn_right, ffn_all, grad_all = held

    came = shift_all(tie_all(parts[1], *ffn_slots[-1]))
    ffn_part = weight_grads([ffn_all, grad_all], tie(ffn_right, *came), [0, 2 * ff], [], "ffn_grads")
    for slot in range(2, slots):
        came = ring_add(came, parts[slot])
        if slot == 2:
            came = tie_all(came, ffn_part)
    grad_ffn = lax.psum_scatter(ffn_part, "dp", scatter_dimension=0, tiled=True)
    grad_mixed, grad_ffn_norm, *mid_first = simple_call(
        functools.partial(mid_kernel, halves=halves),
        [*came, *parts[0], mixed_rows, ffn_norm, grad_out],
        [((tok, width), f32), ((1, width), f32)] + [part_shape] * halves,
        "mid",
    )
    mid_slots = [mid_first]
    result_parts = slot_product(ffn_right, 2, w_ffn, 2, ff, slots, [], "ffn_out")
    for slot in range(1, slots):
        came = shift_all(mid_slots[-1])
        mid_slots.append(came)

    result_came = [
        lax.ppermute(result_parts[slot], "mp", [(i, (i - slot) % mp_count) for i in range(mp_count)])
        for slot in range(1, slots)
    ]

    grad_mid, grad_attended = grad_attended_product(flat(mid_slots), w_attn, q_cols, [])
    near_spec = pl.BlockSpec((keys_total // 2, 2 * k_cols), lambda h: (0, 0))
    near_shape = jax.ShapeDtypeStruct((keys_total // 2, 2 * k_cols), bf16)
    dq_rot, dkv_near, dkv_far = pl.pallas_call(
        functools.partial(
            attn_bwd_kernel, **dims, dq_scale=score_scale, dk_scale=1.0 / log2_e
        ),
        grid=(kv_local,),
        in_specs=[smem, smem, lane_spec, q_spec, lse_spec, q_spec, q_spec] + [any_spec] * dp_count,
        out_specs=[q_spec, near_spec, near_spec],
        out_shape=[jax.ShapeDtypeStruct((group_rows, q_cols), f32), near_shape, near_shape],
        scratch_shapes=[
            kv_scratch,
            pltpu.VMEM((all_rows, head_dim), bf16),
            pltpu.VMEM((all_rows, head_dim), bf16),
            pltpu.VMEM((head_dim, all_rows), f32),
            pltpu.VMEM((1, all_rows), f32),
            pltpu.VMEM((tok * sub, head_dim), f32),
            pltpu.VMEM((tok * sub, head_dim), f32),
            pltpu.SemaphoreType.DMA((dp_count,)),
        ],
        cost_estimate=light_cost,
        name="attn_bwd",
    )(flags, key_base, lane_places, query_rot, lse, attended_low, grad_attended, *kv_pieces)

    dkv_got = swap(dkv_far, 1)
    dkv_sent = fold_blocks(dkv_near, dkv_got, half, [])
    dkv_came = [swap_back(sent, mask) for sent, mask in zip(dkv_sent, far_masks)]
    marked = mark(*dkv_sent)
    dq_raw, query_gain_part = unproject(query_raw, cos_table, sin_table, q_gain, [dq_rot], marked, "unproject_q")
    attn_part = more_grads(grad_mid, [attended_low], [], 2, 3, marked, "out_grads")
    attn_part = more_grads(attn_input, [dq_raw], [attn_part], 0, 3, [], "q_grads")
    dkv_raw, key_gain_part = unproject(
        key_raw, cos_table, sin_table, k_gain, [dkv_near, dkv_got] + dkv_came, [attn_part, *result_came], "unproject_kv"
    )

    attn_part = more_grads(attn_input, [dkv_raw], [attn_part], 1, 3, [grad_ffn], "kv_grads")
    grad_attn = lax.psum_scatter(attn_part, "dp", scatter_dimension=0, tiled=True)
    *parts, attn_gain_part = attn_back_product(
        dq_raw, dkv_raw, w_attn, row_scales, flat(hidden_slots), [attn_part]
    )
    parts = by_slot(parts)
    came = shift_all(parts[1])
    came, (attn_gain_part,) = order(came, [attn_gain_part])
    small = jnp.concatenate(
        [attn_gain_part[0], grad_ffn_norm[0], query_gain_part[0], key_gain_part[0]]
    ).reshape(-1, head_dim)
    small = small + swap(small, 1)
    for slot in range(2, slots):
        came = ring_add(came, parts[slot])
        if slot == 2:
            grads = split_columns(grad_ffn, [ff, ff, ff], "split_ffn")
            came, (small, grad_gate, grad_up, grad_down) = order(came, [small, *grads])
            small = small + sum(swap(small, mask) for mask in far_masks)
    came, (small,) = order(came, [small])
    turns = [[(i, (i + by) % mp_count) for i in range(mp_count)] for by in range(1, mp_count)]
    small = small + sum(lax.ppermute(small, "mp", turn) for turn in turns)
    (grad_hidden,) = simple_call(
        functools.partial(last_kernel, halves=halves),
        [*came, *parts[0], grad_mixed, hidden_in, attn_norm],
        [((tok, width), f32)],
        "last",
    )
    (result,) = simple_call(
        result_kernel, [result_parts[0], *result_came, mixed_rows], [((tok, width), bf16)], "result"
    )
    grad_query, grad_key, grad_value, grad_out_weight = split_columns(
        grad_attn, [q_cols, k_cols, k_cols, q_cols], "split_attn"
    )

    small = small.reshape(-1)
    return (
        result,
        grad_hidden,
        small[:width],
        grad_query,
        grad_key,
        grad_value,
        small[2 * width:2 * width + head_dim],
        small[2 * width + head_dim:],
        grad_out_weight,
        small[width:2 * width],
        grad_gate,
        grad_up,
        grad_down,
    )


def solution(mesh):
    rows = P(("dp", "mp"), None)
    placed = (
        rows,
        P(),
        P(),
        P("dp", "mp"),
        P("dp", "mp"),
        P("dp", "mp"),
        P(),
        P(),
        P("mp", "dp"),
        P(),
        P("dp", "mp"),
        P("dp", "mp"),
        P("mp", "dp"),
        rows,
    )
    return jax.shard_map(
        body,
        mesh=mesh,
        in_specs=placed,
        out_specs=(
            rows,
            rows,
            P(),
            P("dp", "mp"),
            P("dp", "mp"),
            P("dp", "mp"),
            P(),
            P(),
            P("mp", "dp"),
            P(),
            P("dp", "mp"),
            P("dp", "mp"),
            P("mp", "dp"),
        ),
        check_vma=False,
    )
```

profile of v0, /device:TPU:0, one launch (start us, length us, event | category | flops | bytes accessed | tf_op | source)
XLA Modules:
  0.0 486.2 jit_solution(10080853309095705886)
XLA Ops:
  13.6 3.1 collective-permute-start.1
  21.6 4.3 collective-permute-done.1.refs_3_.refs_7_
  25.8 4.8 collective-permute-done.refs_2_.refs_6_
  31.9 9.7 %collective-permute-done.2.refs_4_.refs_8_ = bf16[64,2048]{1,0:T(8,128)(2,1)S(1)} collective-permute-done((bf16[64,2048]{1,0:T(8,128)(2,1)S(1)}, bf16[64,2048]{1,0:T(8,128)(2,1)S(1)}, u32[]{:S(2)}, u32[]{:S(2)}) %collective-permute-start.2) | collective-permute-done | bytes 262176 | tf_op jit(solution)/shard_map/ppermute | solution.py:680
  41.7 5.6 %collective-permute-done.3.refs_5_.refs_9_ = bf16[64,2048]{1,0:T(8,128)(2,1)S(1)} collective-permute-done((bf16[64,2048]{1,0:T(8,128)(2,1)S(1)}, bf16[64,2048]{1,0:T(8,128)(2,1)S(1)}, u32[]{:S(2)}, u32[]{:S(2)}) %collective-permute-start.3) | collective-permute-done | bytes 262176 | tf_op jit(solution)/shard_map/ppermute | solution.py:680
  47.4 5.5 %collective-permute-done.4.refs_6_.refs_10_ = bf16[64,2048]{1,0:T(8,128)(2,1)S(1)} collective-permute-done((bf16[64,2048]{1,0:T(8,128)(2,1)S(1)}, bf16[64,2048]{1,0:T(8,128)(2,1)S(1)}, u32[]{:S(2)}, u32[]{:S(2)}) %collective-permute-start.4) | collective-permute-done | bytes 262176 | tf_op jit(solution)/shard_map/ppermute | solution.py:680
  52.9 3.9 collective-permute-done.5.refs_7_.refs_11_
  59.0 6.5 %project_kv.1 = (bf16[512,2048]{1,0:T(8,128)(2,1)}, f32[512,128]{1,0:T(8,128)}, f32[512,256]{1,0:T(8,128)}, bf16[512,512]{1,0:T(8,128)(2,1)}) custom-call(bf16[2048,1536]{1,0:T(8,128)(2,1)} %all-gather.5.cloned.1.call-done.w_ref.refs_1_.refs_0_.refs_2_, f32[512,128]{1,0:T(8,128)} %pad_maximum_fusion.2.cos_ref.refs_2_.refs_1_, ...), custom_call_target="tpu_custom_call" | custom-call | flops 1048576 | bytes 65536 | tf_op jit(solution)/shard_map/project_kv/pallas_call | solution.py:226
  67.8 2.9 collective-permute-done.7.refs_7_
  72.1 3.6 collective-permute-start.9
  75.7 3.4 collective-permute-start.8
  80.0 5.8 %project_q.1 = (f32[512,512]{1,0:T(8,128)}, bf16[512,512]{1,0:T(8,128)(2,1)}) custom-call(bf16[512,2048]{1,0:T(8,128)(2,1)} %get-tuple-element.130.refs_0_, bf16[2048,1536]{1,0:T(8,128)(2,1)} %all-gather.5.cloned.1.call-done.w_ref.refs_1_.refs_0_.refs_2_, f32[512,128]{1,0:T(8,128)} %pad_maximum_fusion.2.cos_ref.refs_2_.refs_1_, ...), custom_call_target="tpu_custom_call" | custom-call | flops 1048576 | bytes 65536 | tf_op jit(solution)/shard_map/project_q/pallas_call | solution.py:258
  85.9 4.4 collective-permute-done.12.refs_5_
  90.3 18.1 %collective-permute-done.9.refs_2_ = bf16[512,512]{1,0:T(8,128)(2,1)S(1)} collective-permute-done((bf16[512,512]{1,0:T(8,128)(2,1)}, bf16[512,512]{1,0:T(8,128)(2,1)S(1)}, u32[]{:S(2)}, u32[]{:S(2)}) %collective-permute-start.9) | collective-permute-done | bytes 524320 | tf_op jit(solution)/shard_map/ppermute | solution.py:693
  114.0 7.8 %attn_fwd.1 = (bf16[512,512]{1,0:T(8,128)(2,1)}, f32[2,1,1024]{2,1,0:T(1,128)}) custom-call(s32[8]{0:T(128)} %convert_select_fusion.1.flags_ref, s32[32]{0:T(128)} %add.167.base_ref, s32[1024,2]{1,0:T(8,128)} %copy.52.places_ref, bf16[512,512]{1,0:T(8,128)(2,1)} %get-tuple-element.131.q_ref, bf16[512,512]{1,0:T(8,128)(2,1)} %get-tuple-element.125.refs_0_, ...), custom_call_target="tpu_custom_call" | custom-call | flops 1048576 | bytes 65536 | tf_op jit(solution)/shard_map/attn_fwd/pallas_call | solution.py:806
  121.8 3.9 collective-permute-done.18.refs_7_
  125.7 5.1 %attn_out.1 = (bf16[64,2048]{1,0:T(8,128)(2,1)}, bf16[64,2048]{1,0:T(8,128)(2,1)}, bf16[64,2048]{1,0:T(8,128)(2,1)}, bf16[64,2048]{1,0:T(8,128)(2,1)}, bf16[64,2...) custom-call(bf16[512,512]{1,0:T(8,128)(2,1)} %get-tuple-element.140.refs_0_.o_r, ...), custom_call_target="tpu_custom_call" | custom-call | flops 1048576 | bytes 65536 | tf_op jit(solution)/shard_map/attn_out/pallas_call | solution.py:569
  130.9 11.1 %collective-permute-done.19 = bf16[64,2048]{1,0:T(8,128)(2,1)S(1)} collective-permute-done((bf16[64,2048]{1,0:T(8,128)(2,1)}, bf16[64,2048]{1,0:T(8,128)(2,1)S(1)}, u32[]{:S(2)}, u32[]{:S(2)}) %collective-permute-start.19) | collective-permute-done | bytes 262176 | tf_op jit(solution)/shard_map/ppermute | solution.py:680
  143.1 4.5 collective-permute-done.22
  148.8 4.5 collective-permute-done.20
  154.3 5.5 %collective-permute-done.23 = bf16[64,2048]{1,0:T(8,128)(2,1)S(1)} collective-permute-done((bf16[64,2048]{1,0:T(8,128)(2,1)S(1)}, bf16[64,2048]{1,0:T(8,128)(2,1)S(1)}, u32[]{:S(2)}, u32[]{:S(2)}) %collective-permute-start.23) | collective-permute-done | bytes 262176 | tf_op jit(solution)/shard_map/ppermute | solution.py:680
  160.1 5.3 %collective-permute-done.21.refs_0_ = bf16[64,2048]{1,0:T(8,128)(2,1)S(1)} collective-permute-done((bf16[64,2048]{1,0:T(8,128)(2,1)S(1)}, bf16[64,2048]{1,0:T(8,128)(2,1)S(1)}, u32[]{:S(2)}, u32[]{:S(2)}) %collective-permute-start.21) | collective-permute-done | bytes 262176 | tf_op jit(solution)/shard_map/ppermute | solution.py:680
  165.4 3.5 collective-permute-done.24.refs_1_
  169.6 2.8 mix.1
  172.4 11.2 %collective-permute-done.25.refs_2_ = bf16[64,2048]{1,0:T(8,128)(2,1)S(1)} collective-permute-done((bf16[64,2048]{1,0:T(8,128)(2,1)}, bf16[64,2048]{1,0:T(8,128)(2,1)S(1)}, u32[]{:S(2)}, u32[]{:S(2)}) %collective-permute-start.25) | collective-permute-done | bytes 262176 | tf_op jit(solution)/shard_map/ppermute | solution.py:680
  183.7 5.6 %collective-permute-done.27.refs_3_ = bf16[64,2048]{1,0:T(8,128)(2,1)S(1)} collective-permute-done((bf16[64,2048]{1,0:T(8,128)(2,1)}, bf16[64,2048]{1,0:T(8,128)(2,1)S(1)}, u32[]{:S(2)}, u32[]{:S(2)}) %collective-permute-start.27) | collective-permute-done | bytes 262176 | tf_op jit(solution)/shard_map/ppermute | solution.py:680
  190.0 16.4 %feed_forward.2 = (bf16[512,4608]{1,0:T(8,128)(2,1)}, bf16[512,2048]{1,0:T(8,128)(2,1)}, bf16[512,2048]{1,0:T(8,128)(2,1)}, bf16[64,2048]{1,0:T(8,128)(2,1)}, bf...) custom-call(bf16[2048,4608]{1,0:T(8,128)(2,1)} %all-gather.3.cloned.1.call-done.gate_ref.up_ref.down_ref.r, ...), custom_call_target="tpu_custom_call" | custom-call | flops 1048576 | bytes 65536 | tf_op jit(solution)/shard_map/feed_forward/pallas_call | solution.py:503
  206.6 8.1 %collective-permute-done.29.refs_2_ = bf16[64,2048]{1,0:T(8,128)(2,1)S(1)} collective-permute-done((bf16[64,2048]{1,0:T(8,128)(2,1)S(1)}, bf16[64,2048]{1,0:T(8,128)(2,1)S(1)}, u32[]{:S(2)}, u32[]{:S(2)}) %collective-permute-start.29) | collective-permute-done | bytes 262176 | tf_op jit(solution)/shard_map/ppermute | solution.py:680
  214.6 5.4 %collective-permute-done.30.refs_3_ = bf16[64,2048]{1,0:T(8,128)(2,1)S(1)} collective-permute-done((bf16[64,2048]{1,0:T(8,128)(2,1)S(1)}, bf16[64,2048]{1,0:T(8,128)(2,1)S(1)}, u32[]{:S(2)}, u32[]{:S(2)}) %collective-permute-start.30) | collective-permute-done | bytes 262176 | tf_op jit(solution)/shard_map/ppermute | solution.py:680
  222.1 16.4 %feed_forward.3 = (bf16[512,4608]{1,0:T(8,128)(2,1)}, bf16[512,2048]{1,0:T(8,128)(2,1)}, bf16[512,2048]{1,0:T(8,128)(2,1)}, bf16[64,2048]{1,0:T(8,128)(2,1)}, bf...) custom-call(bf16[2048,4608]{1,0:T(8,128)(2,1)} %all-gather.3.cloned., ...), custom_call_target="tpu_custom_call", output_to_operand_aliasing={{0}: (11, {}), {1}: (12, {}), {2}: (13, {})} | custom-call | flops 1048576 | bytes 65536 | tf_op jit(solution)/shard_map/feed_forward/pallas_call | solution.py:503
  238.5 17.2 %ffn_grads.1 = bf16[2048,4608]{1,0:T(8,128)(2,1)} custom-call(bf16[512,2048]{1,0:T(8,128)(2,1)} %get-tuple-element.176.refs_0_, bf16[512,2048]{1,0:T(8,128)(2,1)} %get-tuple-element.177.refs_1_, bf16[512,4608]{1,0:T(8,128)(2,1)} %get-tuple-element.178.refs_0_.refs_2_), custom_call_target="tpu_custom_call" | custom-call | flops 1048576 | bytes 65536 | tf_op jit(solution)/shard_map/ffn_grads/pallas_call | solution.py:546
  259.8 8.0 %collective-permute-done.35 = bf16[64,2048]{1,0:T(8,128)(2,1)S(1)} collective-permute-done((bf16[64,2048]{1,0:T(8,128)(2,1)S(1)}, bf16[64,2048]{1,0:T(8,128)(2,1)S(1)}, u32[]{:S(2)}, u32[]{:S(2)}) %collective-permute-start.35) | collective-permute-done | bytes 262176 | tf_op jit(solution)/shard_map/ppermute | solution.py:680
  267.8 4.0 collective-permute-done.37
  272.1 8.2 %collective-permute-done.39.refs_1_ = bf16[64,2048]{1,0:T(8,128)(2,1)S(1)} collective-permute-done((bf16[64,2048]{1,0:T(8,128)(2,1)S(1)}, bf16[64,2048]{1,0:T(8,128)(2,1)S(1)}, u32[]{:S(2)}, u32[]{:S(2)}) %collective-permute-start.39) | collective-permute-done | bytes 262176 | tf_op jit(solution)/shard_map/ppermute | solution.py:680
  280.3 5.6 %collective-permute-done.38.refs_0_ = bf16[64,2048]{1,0:T(8,128)(2,1)S(1)} collective-permute-done((bf16[64,2048]{1,0:T(8,128)(2,1)S(1)}, bf16[64,2048]{1,0:T(8,128)(2,1)S(1)}, u32[]{:S(2)}, u32[]{:S(2)}) %collective-permute-start.38) | collective-permute-done | bytes 262176 | tf_op jit(solution)/shard_map/ppermute | solution.py:680
  286.6 3.9 mid.1
  290.5 10.1 %collective-permute-done.40.refs_3_ = bf16[64,2048]{1,0:T(8,128)(2,1)S(1)} collective-permute-done((bf16[64,2048]{1,0:T(8,128)(2,1)}, bf16[64,2048]{1,0:T(8,128)(2,1)S(1)}, u32[]{:S(2)}, u32[]{:S(2)}) %collective-permute-start.40) | collective-permute-done | bytes 262176 | tf_op jit(solution)/shard_map/ppermute | solution.py:680
  300.6 5.6 %collective-permute-done.41.refs_4_ = bf16[64,2048]{1,0:T(8,128)(2,1)S(1)} collective-permute-done((bf16[64,2048]{1,0:T(8,128)(2,1)}, bf16[64,2048]{1,0:T(8,128)(2,1)S(1)}, u32[]{:S(2)}, u32[]{:S(2)}) %collective-permute-start.41) | collective-permute-done | bytes 262176 | tf_op jit(solution)/shard_map/ppermute | solution.py:680
  306.2 3.9 collective-permute-done.42.refs_5_
  310.1 4.3 collective-permute-done.43.refs_6_
  314.6 3.7 collective-permute-done.44.refs_7_
  318.3 4.5 collective-permute-done.45.refs_8_
  323.5 5.0 %grad_attended.1 = (bf16[512,2048]{1,0:T(8,128)(2,1)}, bf16[512,512]{1,0:T(8,128)(2,1)}) custom-call(bf16[2048,1536]{1,0:T(8,128)(2,1)} %all-gather.5.cloned.1.call-done.w_ref.refs_1_.refs_0_.refs_2_, bf16[64,2048]{1,0:T(8,128)(2,1)} %get-tuple-element.183.refs_1_, bf16[64,2048]{1,0:T(8,128)(2,1)} %get-tuple-element.184.refs_2_, ...), custom_call_target="tpu_custom_call" | custom-call | flops 1048576 | bytes 65536 | tf_op jit(solution)/shard_map/grad_attended/pallas_call | solution.py:365
  328.5 11.8 %attn_bwd.1 = (f32[512,512]{1,0:T(8,128)}, bf16[2048,512]{1,0:T(8,128)(2,1)}, bf16[2048,512]{1,0:T(8,128)(2,1)}) custom-call(s32[8]{0:T(128)} %convert_select_fusion.1.flags_ref, s32[32]{0:T(128)} %add.167.base_ref, s32[2,1024]{1,0:T(2,128)} %copy-done.57, bf16[512,512]{1,0:T(8,128)(2,1)} %get-tuple-element.131.q_ref, ...), custom_call_target="tpu_custom_call" | custom-call | flops 1048576 | bytes 65536 | tf_op jit(solution)/shard_map/attn_bwd/pallas_call | solution.py:878
  340.4 7.3 %ffn_out.1 = (bf16[128,2048]{1,0:T(8,128)(2,1)}, bf16[128,2048]{1,0:T(8,128)(2,1)}, bf16[128,2048]{1,0:T(8,128)(2,1)}, bf16[128,2048]{1,0:T(8,128)(2,1)}) custom-call(bf16[512,4608]{1,0:T(8,128)(2,1)} %get-tuple-element.178.refs_0_.refs_2_, bf16[2048,4608]{1,0:T(8,128)(2,1)} %all-gather.3.cloned.1.call-done.gate_ref.up_ref.down_ref.refs_1_), custom_call_target="tpu_custom_call" | custom-call | flops 1048576 | bytes 65536 | tf_op jit(solution)/shard_map/ffn_out/pallas_call | solution.py:569
  349.1 3.6 fold_blocks.1
  356.7 6.0 %collective-permute-done.31.refs_1_.refs_10_ = bf16[128,2048]{1,0:T(8,128)(2,1)S(1)} collective-permute-done((bf16[128,2048]{1,0:T(8,128)(2,1)}, bf16[128,2048]{1,0:T(8,128)(2,1)S(1)}, u32[]{:S(2)}, u32[]{:S(2)}) %collective-permute-start.31) | collective-permute-done | bytes 524320 | tf_op jit(solution)/shard_map/ppermute | solution.py:871
  364.7 4.4 out_grads.1.refs_2_
  369.1 3.6 unproject_q.1
  372.7 4.3 q_grads.1.refs_9_.refs_2_
  377.0 16.5 %collective-permute-done.32.refs_2_.refs_11_ = bf16[128,2048]{1,0:T(8,128)(2,1)S(1)} collective-permute-done((bf16[128,2048]{1,0:T(8,128)(2,1)}, bf16[128,2048]{1,0:T(8,128)(2,1)S(1)}, u32[]{:S(2)}, u32[]{:S(2)}) %collective-permute-start.32) | collective-permute-done | bytes 524320 | tf_op jit(solution)/shard_map/ppermute | solution.py:871
  394.9 3.7 unproject_kv.1
  398.7 4.4 kv_grads.1.refs_12_
  403.1 6.5 %attn_back.1 = (bf16[64,2048]{1,0:T(8,128)(2,1)}, bf16[64,2048]{1,0:T(8,128)(2,1)}, bf16[64,2048]{1,0:T(8,128)(2,1)}, bf16[64,2048]{1,0:T(8,128)(2,1)}, bf16[64,...) custom-call(bf16[512,512]{1,0:T(8,128)(2,1)} %get-tuple-element.192., ...), custom_call_target="tpu_custom_call" | custom-call | flops 1048576 | bytes 65536 | tf_op jit(solution)/shard_map/attn_back/pallas_call | solution.py:332
  409.6 9.4 %collective-permute-start.51 = (bf16[64,2048]{1,0:T(8,128)(2,1)}, bf16[64,2048]{1,0:T(8,128)(2,1)S(1)}, u32[]{:S(2)}, u32[]{:S(2)}) collective-permute-start(bf16[64,2048]{1,0:T(8,128)(2,1)} %get-tuple-element.197), channel_id=1, source_target_pairs={{0,1},{1,2},{2,3},{3,0},{4,5},{5,6},{6,7},{7,4},{8,9},{9,10},{10,1... | collective-permute-start | bytes 786440 | tf_op jit(solution)/shard_map/ppermute | solution.py:680
  419.0 4.1 collective-permute-done.51
  423.2 4.2 collective-permute-done.52
  432.3 4.2 split_ffn.1
  437.7 2.8 collective-permute-done.53
  441.6 11.6 %collective-permute-start.60 = (f32[34,128]{1,0:T(8,128)S(1)}, f32[34,128]{1,0:T(8,128)S(1)}, u32[]{:S(2)}, u32[]{:S(2)}) collective-permute-start(f32[34,128]{1,0:T(8,128)S(1)} %fusion.7), channel_id=1, source_target_pairs={{0,24},{4,28},{8,16},{12,20},{16,8},{20,12},{24,0},{28,4},{1,25},{... | collective-permute-start | bytes 52232 | tf_op jit(solution)/shard_map/ppermute | solution.py:683
  459.7 3.9 collective-permute-start.63
  466.1 2.9 result.1
  469.0 3.3 last.1
  473.5 3.3 reduce-scatter.5.cloned.1.call-done.refs_0_
  (279 shorter events, 66.6 us)
Async XLA Ops:
  7.2 51.7 %all-gather.5.cloned.1.call-start = ((), (), s32[]{:S(2)}) async-start(), calls=%async_computation.3 | async-start | bytes 7077888 | tf_op jit(solution)/shard_map/all_gather | solution.py:733
  10.5 178.8 %all-gather.3.cloned.1.call-start = ((), (), s32[]{:S(2)}) async-start(), calls=%async_computation.2 | async-start | bytes 21233664 | tf_op jit(solution)/shard_map/all_gather | solution.py:734
  12.5 386.1 %reduce-scatter.3.cloned.1.call-start = ((), (), s32[]{:S(2)}) async-start(), calls=%async_computation.4 | async-start | bytes 21233664 | tf_op jit(solution)/shard_map/reduce_scatter | solution.py:857
  13.6 12.2 %collective-permute-start.1 = (bf16[64,2048]{1,0:T(8,128)(2,1)S(1)}, bf16[64,2048]{1,0:T(8,128)(2,1)S(1)}, u32[]{:S(2)}, u32[]{:S(2)}) collective-permute-start(bf16[64,2048]{1,0:T(8,128)(2,1)S(1)} %get-tuple-element.239.refs_1_.refs_5_), channel_id=1, source_target_pairs={{0,1},{1,2},{2,3},{3,0},{4,5},{5,6},{6,7},{7,4},{8,9},{9,10},{10,1... | collective-permute-start | bytes 786440 | tf_op jit(solution)/shard_map/ppermute | solution.py:680
  16.7 13.9 %collective-permute-start = (bf16[64,2048]{1,0:T(8,128)(2,1)S(1)}, bf16[64,2048]{1,0:T(8,128)(2,1)S(1)}, u32[]{:S(2)}, u32[]{:S(2)}) collective-permute-start(bf16[64,2048]{1,0:T(8,128)(2,1)S(1)} %get-tuple-element.240.refs_0_.refs_4_), channel_id=1, source_target_pairs={{0,1},{1,2},{2,3},{3,0},{4,5},{5,6},{6,7},{7,4},{8,9},{9,10},{10,1... | collective-permute-start | bytes 786440 | tf_op jit(solution)/shard_map/ppermute | solution.py:680
  30.6 11.0 %collective-permute-start.2 = (bf16[64,2048]{1,0:T(8,128)(2,1)S(1)}, bf16[64,2048]{1,0:T(8,128)(2,1)S(1)}, u32[]{:S(2)}, u32[]{:S(2)}) collective-permute-start(bf16[64,2048]{1,0:T(8,128)(2,1)S(1)} %collective-permute-done.refs_2_.refs_6_), channel_id=1, source_target_pairs={{0,1},{1,2},{2,3},{3,0},{4,5},{5,6},{6,7},{7,4},{8,9},{9,10},{10,1... | collective-permute-start | bytes 786440 | tf_op jit(solution)/shard_map/ppermute | solution.py:680
  30.6 16.7 %collective-permute-start.3 = (bf16[64,2048]{1,0:T(8,128)(2,1)S(1)}, bf16[64,2048]{1,0:T(8,128)(2,1)S(1)}, u32[]{:S(2)}, u32[]{:S(2)}) collective-permute-start(bf16[64,2048]{1,0:T(8,128)(2,1)S(1)} %collective-permute-done.1.refs_3_.refs_7_), channel_id=1, source_target_pairs={{0,1},{1,2},{2,3},{3,0},{4,5},{5,6},{6,7},{7,4},{8,9},{9,10},{10,1... | collective-permute-start | bytes 786440 | tf_op jit(solution)/shard_map/ppermute | solution.py:680
  41.7 11.2 %collective-permute-start.4 = (bf16[64,2048]{1,0:T(8,128)(2,1)S(1)}, bf16[64,2048]{1,0:T(8,128)(2,1)S(1)}, u32[]{:S(2)}, u32[]{:S(2)}) collective-permute-start(bf16[64,2048]{1,0:T(8,128)(2,1)S(1)} %collective-permute-done.2.refs_4_.refs_8_), channel_id=1, source_target_pairs={{0,1},{1,2},{2,3},{3,0},{4,5},{5,6},{6,7},{7,4},{8,9},{9,10},{10,1... | collective-permute-start | bytes 786440 | tf_op jit(solution)/shard_map/ppermute | solution.py:680
  47.3 9.5 %collective-permute-start.5 = (bf16[64,2048]{1,0:T(8,128)(2,1)S(1)}, bf16[64,2048]{1,0:T(8,128)(2,1)S(1)}, u32[]{:S(2)}, u32[]{:S(2)}) collective-permute-start(bf16[64,2048]{1,0:T(8,128)(2,1)S(1)} %collective-permute-done.3.refs_5_.refs_9_), channel_id=1, source_target_pairs={{0,1},{1,2},{2,3},{3,0},{4,5},{5,6},{6,7},{7,4},{8,9},{9,10},{10,1... | collective-permute-start | bytes 786440 | tf_op jit(solution)/shard_map/ppermute | solution.py:680
  56.8 11.0 %collective-permute-start.6 = (bf16[64,2048]{1,0:T(8,128)(2,1)S(1)}, bf16[64,2048]{1,0:T(8,128)(2,1)S(1)}, u32[]{:S(2)}, u32[]{:S(2)}) collective-permute-start(bf16[64,2048]{1,0:T(8,128)(2,1)S(1)} %get-tuple-element.126.refs_4_), channel_id=1, source_target_pairs={{0,1},{1,2},{2,3},{3,0},{4,5},{5,6},{6,7},{7,4},{8,9},{9,10},{10,1... | collective-permute-start | bytes 786440 | tf_op jit(solution)/shard_map/ppermute | solution.py:680
  56.8 14.0 %collective-permute-start.7 = (bf16[64,2048]{1,0:T(8,128)(2,1)S(1)}, bf16[64,2048]{1,0:T(8,128)(2,1)S(1)}, u32[]{:S(2)}, u32[]{:S(2)}) collective-permute-start(bf16[64,2048]{1,0:T(8,128)(2,1)S(1)} %get-tuple-element.127.refs_5_), channel_id=1, source_target_pairs={{0,1},{1,2},{2,3},{3,0},{4,5},{5,6},{6,7},{7,4},{8,9},{9,10},{10,1... | collective-permute-start | bytes 786440 | tf_op jit(solution)/shard_map/ppermute | solution.py:680
  71.5 8.2 %collective-permute-start.11 = (bf16[64,2048]{1,0:T(8,128)(2,1)S(1)}, bf16[64,2048]{1,0:T(8,128)(2,1)S(1)}, u32[]{:S(2)}, u32[]{:S(2)}) collective-permute-start(bf16[64,2048]{1,0:T(8,128)(2,1)S(1)} %collective-permute-done.6.refs_6_), channel_id=1, source_target_pairs={{0,1},{1,2},{2,3},{3,0},{4,5},{5,6},{6,7},{7,4},{8,9},{9,10},{10,1... | collective-permute-start | bytes 786440 | tf_op jit(solution)/shard_map/ppermute | solution.py:680
  71.5 18.8 %collective-permute-start.10 = (bf16[512,512]{1,0:T(8,128)(2,1)}, bf16[512,512]{1,0:T(8,128)(2,1)S(1)}, u32[]{:S(2)}, u32[]{:S(2)}) collective-permute-start(bf16[512,512]{1,0:T(8,128)(2,1)} %get-tuple-element.125.refs_0_), channel_id=1, source_target_pairs={{8,16},{12,20},{9,17},{13,21},{10,18},{14,22},{11,19},{15,23}} | collective-permute-start | bytes 1572872 | tf_op jit(solution)/shard_map/ppermute | solution.py:693
  72.1 36.2 %collective-permute-start.9 = (bf16[512,512]{1,0:T(8,128)(2,1)}, bf16[512,512]{1,0:T(8,128)(2,1)S(1)}, u32[]{:S(2)}, u32[]{:S(2)}) collective-permute-start(bf16[512,512]{1,0:T(8,128)(2,1)} %get-tuple-element.125.refs_0_), channel_id=1, source_target_pairs={{0,16},{4,20},{8,24},{12,28},{1,17},{5,21},{9,25},{13,29},{2,18},{... | collective-permute-start | bytes 1572872 | tf_op jit(solution)/shard_map/ppermute | solution.py:693
  75.7 32.6 %collective-permute-start.8 = (bf16[512,512]{1,0:T(8,128)(2,1)}, bf16[512,512]{1,0:T(8,128)(2,1)S(1)}, u32[]{:S(2)}, u32[]{:S(2)}) collective-permute-start(bf16[512,512]{1,0:T(8,128)(2,1)} %get-tuple-element.125.refs_0_), channel_id=1, source_target_pairs={{0,8},{4,12},{16,24},{20,28},{1,9},{5,13},{17,25},{21,29},{2,10},{... | collective-permute-start | bytes 1572872 | tf_op jit(solution)/shard_map/ppermute | solution.py:693
  79.2 30.2 %collective-permute-start.13 = (bf16[512,512]{1,0:T(8,128)(2,1)}, bf16[512,512]{1,0:T(8,128)(2,1)S(1)}, u32[]{:S(2)}, u32[]{:S(2)}) collective-permute-start(bf16[512,512]{1,0:T(8,128)(2,1)} %get-tuple-element.125.refs_0_), channel_id=1, source_target_pairs={{0,4},{4,0},{8,12},{12,8},{16,20},{20,16},{24,28},{28,24},{1,5},{5... | collective-permute-start | bytes 1572872 | tf_op jit(solution)/shard_map/ppermute | solution.py:683
  79.6 10.6 %collective-permute-start.12 = (bf16[64,2048]{1,0:T(8,128)(2,1)}, bf16[64,2048]{1,0:T(8,128)(2,1)S(1)}, u32[]{:S(2)}, u32[]{:S(2)}) collective-permute-start(bf16[64,2048]{1,0:T(8,128)(2,1)} %copy-done.30), channel_id=1, source_target_pairs={{0,1},{1,2},{2,3},{3,0},{4,5},{5,6},{6,7},{7,4},{8,9},{9,10},{10,1... | collective-permute-start | bytes 786440 | tf_op jit(solution)/shard_map/ppermute | solution.py:680
  108.4 4.7 collective-permute-start.14
  109.3 12.5 %collective-permute-start.17 = (bf16[64,2048]{1,0:T(8,128)(2,1)S(1)}, bf16[64,2048]{1,0:T(8,128)(2,1)}, u32[]{:S(2)}, u32[]{:S(2)}) collective-permute-start(bf16[64,2048]{1,0:T(8,128)(2,1)S(1)} %collective-permute-done.11.refs_4_), channel_id=1, source_target_pairs={{0,1},{1,2},{2,3},{3,0},{4,5},{5,6},{6,7},{7,4},{8,9},{9,10},{10,1... | collective-permute-start | bytes 786440 | tf_op jit(solution)/shard_map/ppermute | solution.py:680
  109.4 16.3 %collective-permute-start.18 = (bf16[64,2048]{1,0:T(8,128)(2,1)}, bf16[64,2048]{1,0:T(8,128)(2,1)}, u32[]{:S(2)}, u32[]{:S(2)}) collective-permute-start(bf16[64,2048]{1,0:T(8,128)(2,1)} %copy-done.31), channel_id=1, source_target_pairs={{0,1},{1,2},{2,3},{3,0},{4,5},{5,6},{6,7},{7,4},{8,9},{9,10},{10,1... | collective-permute-start | bytes 786440 | tf_op jit(solution)/shard_map/ppermute | solution.py:680
  130.8 11.3 %collective-permute-start.19 = (bf16[64,2048]{1,0:T(8,128)(2,1)}, bf16[64,2048]{1,0:T(8,128)(2,1)S(1)}, u32[]{:S(2)}, u32[]{:S(2)}) collective-permute-start(bf16[64,2048]{1,0:T(8,128)(2,1)} %get-tuple-element.145), channel_id=1, source_target_pairs={{0,1},{1,2},{2,3},{3,0},{4,5},{5,6},{6,7},{7,4},{8,9},{9,10},{10,1... | collective-permute-start | bytes 786440 | tf_op jit(solution)/shard_map/ppermute | solution.py:680
  130.8 16.8 %collective-permute-start.22 = (bf16[64,2048]{1,0:T(8,128)(2,1)}, bf16[64,2048]{1,0:T(8,128)(2,1)S(1)}, u32[]{:S(2)}, u32[]{:S(2)}) collective-permute-start(bf16[64,2048]{1,0:T(8,128)(2,1)} %get-tuple-element.148), channel_id=1, source_target_pairs={{0,1},{1,2},{2,3},{3,0},{4,5},{5,6},{6,7},{7,4},{8,9},{9,10},{10,1... | collective-permute-start | bytes 786440 | tf_op jit(solution)/shard_map/ppermute | solution.py:680
  143.1 10.2 %collective-permute-start.20 = (bf16[64,2048]{1,0:T(8,128)(2,1)S(1)}, bf16[64,2048]{1,0:T(8,128)(2,1)S(1)}, u32[]{:S(2)}, u32[]{:S(2)}) collective-permute-start(bf16[64,2048]{1,0:T(8,128)(2,1)S(1)} %add_convert_fusion.11), channel_id=1, source_target_pairs={{0,1},{1,2},{2,3},{3,0},{4,5},{5,6},{6,7},{7,4},{8,9},{9,10},{10,1... | collective-permute-start | bytes 786440 | tf_op jit(solution)/shard_map/ppermute | solution.py:680
  148.7 11.1 %collective-permute-start.23 = (bf16[64,2048]{1,0:T(8,128)(2,1)S(1)}, bf16[64,2048]{1,0:T(8,128)(2,1)S(1)}, u32[]{:S(2)}, u32[]{:S(2)}) collective-permute-start(bf16[64,2048]{1,0:T(8,128)(2,1)S(1)} %add_convert_fusion.9), channel_id=1, source_target_pairs={{0,1},{1,2},{2,3},{3,0},{4,5},{5,6},{6,7},{7,4},{8,9},{9,10},{10,1... | collective-permute-start | bytes 786440 | tf_op jit(solution)/shard_map/ppermute | solution.py:680
  154.3 11.1 %collective-permute-start.21 = (bf16[64,2048]{1,0:T(8,128)(2,1)S(1)}, bf16[64,2048]{1,0:T(8,128)(2,1)S(1)}, u32[]{:S(2)}, u32[]{:S(2)}) collective-permute-start(bf16[64,2048]{1,0:T(8,128)(2,1)S(1)} %add_convert_fusion.10), channel_id=1, source_target_pairs={{0,1},{1,2},{2,3},{3,0},{4,5},{5,6},{6,7},{7,4},{8,9},{9,10},{10,1... | collective-permute-start | bytes 786440 | tf_op jit(solution)/shard_map/ppermute | solution.py:680
  159.9 9.1 %collective-permute-start.24 = (bf16[64,2048]{1,0:T(8,128)(2,1)S(1)}, bf16[64,2048]{1,0:T(8,128)(2,1)S(1)}, u32[]{:S(2)}, u32[]{:S(2)}) collective-permute-start(bf16[64,2048]{1,0:T(8,128)(2,1)S(1)} %add_convert_fusion.8), channel_id=1, source_target_pairs={{0,1},{1,2},{2,3},{3,0},{4,5},{5,6},{6,7},{7,4},{8,9},{9,10},{10,1... | collective-permute-start | bytes 786440 | tf_op jit(solution)/shard_map/ppermute | solution.py:680
  172.4 11.3 %collective-permute-start.25 = (bf16[64,2048]{1,0:T(8,128)(2,1)}, bf16[64,2048]{1,0:T(8,128)(2,1)S(1)}, u32[]{:S(2)}, u32[]{:S(2)}) collective-permute-start(bf16[64,2048]{1,0:T(8,128)(2,1)} %get-tuple-element.153.refs_0_), channel_id=1, source_target_pairs={{0,1},{1,2},{2,3},{3,0},{4,5},{5,6},{6,7},{7,4},{8,9},{9,10},{10,1... | collective-permute-start | bytes 786440 | tf_op jit(solution)/shard_map/ppermute | solution.py:680
  172.4 16.9 %collective-permute-start.27 = (bf16[64,2048]{1,0:T(8,128)(2,1)}, bf16[64,2048]{1,0:T(8,128)(2,1)S(1)}, u32[]{:S(2)}, u32[]{:S(2)}) collective-permute-start(bf16[64,2048]{1,0:T(8,128)(2,1)} %get-tuple-element.154.refs_1_), channel_id=1, source_target_pairs={{0,1},{1,2},{2,3},{3,0},{4,5},{5,6},{6,7},{7,4},{8,9},{9,10},{10,1... | collective-permute-start | bytes 786440 | tf_op jit(solution)/shard_map/ppermute | solution.py:680
  183.7 22.7 %collective-permute-start.26 = (bf16[64,2048]{1,0:T(8,128)(2,1)S(1)}, bf16[64,2048]{1,0:T(8,128)(2,1)S(1)}, u32[]{:S(2)}, u32[]{:S(2)}) collective-permute-start(bf16[64,2048]{1,0:T(8,128)(2,1)S(1)} %collective-permute-done.25.refs_2_), channel_id=1, source_target_pairs={{0,1},{1,2},{2,3},{3,0},{4,5},{5,6},{6,7},{7,4},{8,9},{9,10},{10,1... | collective-permute-start | bytes 786440 | tf_op jit(solution)/shard_map/ppermute | solution.py:680
  189.3 17.1 %collective-permute-start.28 = (bf16[64,2048]{1,0:T(8,128)(2,1)S(1)}, bf16[64,2048]{1,0:T(8,128)(2,1)S(1)}, u32[]{:S(2)}, u32[]{:S(2)}) collective-permute-start(bf16[64,2048]{1,0:T(8,128)(2,1)S(1)} %collective-permute-done.27.refs_3_), channel_id=1, source_target_pairs={{0,1},{1,2},{2,3},{3,0},{4,5},{5,6},{6,7},{7,4},{8,9},{9,10},{10,1... | collective-permute-start | bytes 786440 | tf_op jit(solution)/shard_map/ppermute | solution.py:680
  206.4 8.2 %collective-permute-start.29 = (bf16[64,2048]{1,0:T(8,128)(2,1)S(1)}, bf16[64,2048]{1,0:T(8,128)(2,1)S(1)}, u32[]{:S(2)}, u32[]{:S(2)}) collective-permute-start(bf16[64,2048]{1,0:T(8,128)(2,1)S(1)} %collective-permute-done.26.refs_0_), channel_id=1, source_target_pairs={{0,1},{1,2},{2,3},{3,0},{4,5},{5,6},{6,7},{7,4},{8,9},{9,10},{10,1... | collective-permute-start | bytes 786440 | tf_op jit(solution)/shard_map/ppermute | solution.py:680
  206.5 13.6 %collective-permute-start.30 = (bf16[64,2048]{1,0:T(8,128)(2,1)S(1)}, bf16[64,2048]{1,0:T(8,128)(2,1)S(1)}, u32[]{:S(2)}, u32[]{:S(2)}) collective-permute-start(bf16[64,2048]{1,0:T(8,128)(2,1)S(1)} %collective-permute-done.28.refs_1_), channel_id=1, source_target_pairs={{0,1},{1,2},{2,3},{3,0},{4,5},{5,6},{6,7},{7,4},{8,9},{9,10},{10,1... | collective-permute-start | bytes 786440 | tf_op jit(solution)/shard_map/ppermute | solution.py:680
  220.0 18.5 %collective-permute-start.34 = (bf16[64,2048]{1,0:T(8,128)(2,1)}, bf16[64,2048]{1,0:T(8,128)(2,1)S(1)}, u32[]{:S(2)}, u32[]{:S(2)}) collective-permute-start(bf16[64,2048]{1,0:T(8,128)(2,1)} %get-tuple-element.172), channel_id=1, source_target_pairs={{0,1},{1,2},{2,3},{3,0},{4,5},{5,6},{6,7},{7,4},{8,9},{9,10},{10,1... | collective-permute-start | bytes 786440 | tf_op jit(solution)/shard_map/ppermute | solution.py:680
  220.0 18.5 %collective-permute-start.36 = (bf16[64,2048]{1,0:T(8,128)(2,1)}, bf16[64,2048]{1,0:T(8,128)(2,1)S(1)}, u32[]{:S(2)}, u32[]{:S(2)}) collective-permute-start(bf16[64,2048]{1,0:T(8,128)(2,1)} %get-tuple-element.174), channel_id=1, source_target_pairs={{0,1},{1,2},{2,3},{3,0},{4,5},{5,6},{6,7},{7,4},{8,9},{9,10},{10,1... | collective-permute-start | bytes 786440 | tf_op jit(solution)/shard_map/ppermute | solution.py:680
  255.8 221.1 %reduce-scatter.5.cloned.1.call-start = ((), (), s32[]{:S(2)}) async-start(), calls=%async_computation.5 | async-start | bytes 7077888 | tf_op jit(solution)/shard_map/reduce_scatter | solution.py:912
  256.7 11.1 %collective-permute-start.35 = (bf16[64,2048]{1,0:T(8,128)(2,1)S(1)}, bf16[64,2048]{1,0:T(8,128)(2,1)S(1)}, u32[]{:S(2)}, u32[]{:S(2)}) collective-permute-start(bf16[64,2048]{1,0:T(8,128)(2,1)S(1)} %add_convert_fusion.7), channel_id=1, source_target_pairs={{0,1},{1,2},{2,3},{3,0},{4,5},{5,6},{6,7},{7,4},{8,9},{9,10},{10,1... | collective-permute-start | bytes 786440 | tf_op jit(solution)/shard_map/ppermute | solution.py:680
  259.3 12.5 %collective-permute-start.37 = (bf16[64,2048]{1,0:T(8,128)(2,1)S(1)}, bf16[64,2048]{1,0:T(8,128)(2,1)S(1)}, u32[]{:S(2)}, u32[]{:S(2)}) collective-permute-start(bf16[64,2048]{1,0:T(8,128)(2,1)S(1)} %add_convert_fusion.6), channel_id=1, source_target_pairs={{0,1},{1,2},{2,3},{3,0},{4,5},{5,6},{6,7},{7,4},{8,9},{9,10},{10,1... | collective-permute-start | bytes 786440 | tf_op jit(solution)/shard_map/ppermute | solution.py:680
  271.9 8.4 %collective-permute-start.39 = (bf16[64,2048]{1,0:T(8,128)(2,1)S(1)}, bf16[64,2048]{1,0:T(8,128)(2,1)S(1)}, u32[]{:S(2)}, u32[]{:S(2)}) collective-permute-start(bf16[64,2048]{1,0:T(8,128)(2,1)S(1)} %add_convert_fusion.4), channel_id=1, source_target_pairs={{0,1},{1,2},{2,3},{3,0},{4,5},{5,6},{6,7},{7,4},{8,9},{9,10},{10,1... | collective-permute-start | bytes 786440 | tf_op jit(solution)/shard_map/ppermute | solution.py:680
  272.1 13.8 %collective-permute-start.38 = (bf16[64,2048]{1,0:T(8,128)(2,1)S(1)}, bf16[64,2048]{1,0:T(8,128)(2,1)S(1)}, u32[]{:S(2)}, u32[]{:S(2)}) collective-permute-start(bf16[64,2048]{1,0:T(8,128)(2,1)S(1)} %add_convert_fusion.5), channel_id=1, source_target_pairs={{0,1},{1,2},{2,3},{3,0},{4,5},{5,6},{6,7},{7,4},{8,9},{9,10},{10,1... | collective-permute-start | bytes 786440 | tf_op jit(solution)/shard_map/ppermute | solution.py:680
  290.5 10.1 %collective-permute-start.40 = (bf16[64,2048]{1,0:T(8,128)(2,1)}, bf16[64,2048]{1,0:T(8,128)(2,1)S(1)}, u32[]{:S(2)}, u32[]{:S(2)}) collective-permute-start(bf16[64,2048]{1,0:T(8,128)(2,1)} %get-tuple-element.183.refs_1_), channel_id=1, source_target_pairs={{0,1},{1,2},{2,3},{3,0},{4,5},{5,6},{6,7},{7,4},{8,9},{9,10},{10,1... | collective-permute-start | bytes 786440 | tf_op jit(solution)/shard_map/ppermute | solution.py:680
  290.5 15.7 %collective-permute-start.41 = (bf16[64,2048]{1,0:T(8,128)(2,1)}, bf16[64,2048]{1,0:T(8,128)(2,1)S(1)}, u32[]{:S(2)}, u32[]{:S(2)}) collective-permute-start(bf16[64,2048]{1,0:T(8,128)(2,1)} %get-tuple-element.184.refs_2_), channel_id=1, source_target_pairs={{0,1},{1,2},{2,3},{3,0},{4,5},{5,6},{6,7},{7,4},{8,9},{9,10},{10,1... | collective-permute-start | bytes 786440 | tf_op jit(solution)/shard_map/ppermute | solution.py:680
  300.6 9.5 %collective-permute-start.42 = (bf16[64,2048]{1,0:T(8,128)(2,1)S(1)}, bf16[64,2048]{1,0:T(8,128)(2,1)S(1)}, u32[]{:S(2)}, u32[]{:S(2)}) collective-permute-start(bf16[64,2048]{1,0:T(8,128)(2,1)S(1)} %collective-permute-done.40.refs_3_), channel_id=1, source_target_pairs={{0,1},{1,2},{2,3},{3,0},{4,5},{5,6},{6,7},{7,4},{8,9},{9,10},{10,1... | collective-permute-start | bytes 786440 | tf_op jit(solution)/shard_map/ppermute | solution.py:680
  306.2 8.2 %collective-permute-start.43 = (bf16[64,2048]{1,0:T(8,128)(2,1)S(1)}, bf16[64,2048]{1,0:T(8,128)(2,1)S(1)}, u32[]{:S(2)}, u32[]{:S(2)}) collective-permute-start(bf16[64,2048]{1,0:T(8,128)(2,1)S(1)} %collective-permute-done.41.refs_4_), channel_id=1, source_target_pairs={{0,1},{1,2},{2,3},{3,0},{4,5},{5,6},{6,7},{7,4},{8,9},{9,10},{10,1... | collective-permute-start | bytes 786440 | tf_op jit(solution)/shard_map/ppermute | solution.py:680
  310.1 8.2 %collective-permute-start.44 = (bf16[64,2048]{1,0:T(8,128)(2,1)S(1)}, bf16[64,2048]{1,0:T(8,128)(2,1)S(1)}, u32[]{:S(2)}, u32[]{:S(2)}) collective-permute-start(bf16[64,2048]{1,0:T(8,128)(2,1)S(1)} %collective-permute-done.42.refs_5_), channel_id=1, source_target_pairs={{0,1},{1,2},{2,3},{3,0},{4,5},{5,6},{6,7},{7,4},{8,9},{9,10},{10,1... | collective-permute-start | bytes 786440 | tf_op jit(solution)/shard_map/ppermute | solution.py:680
  314.4 8.4 %collective-permute-start.45 = (bf16[64,2048]{1,0:T(8,128)(2,1)S(1)}, bf16[64,2048]{1,0:T(8,128)(2,1)S(1)}, u32[]{:S(2)}, u32[]{:S(2)}) collective-permute-start(bf16[64,2048]{1,0:T(8,128)(2,1)S(1)} %collective-permute-done.43.refs_6_), channel_id=1, source_target_pairs={{0,1},{1,2},{2,3},{3,0},{4,5},{5,6},{6,7},{7,4},{8,9},{9,10},{10,1... | collective-permute-start | bytes 786440 | tf_op jit(solution)/shard_map/ppermute | solution.py:680
  340.3 7.4 %collective-permute-start.46 = (bf16[2048,512]{1,0:T(8,128)(2,1)}, bf16[2048,512]{1,0:T(8,128)(2,1)S(1)}, u32[]{:S(2)}, u32[]{:S(2)}) collective-permute-start(bf16[2048,512]{1,0:T(8,128)(2,1)} %get-tuple-element.188), channel_id=1, source_target_pairs={{0,4},{4,0},{8,12},{12,8},{16,20},{20,16},{24,28},{28,24},{1,5},{5... | collective-permute-start | bytes 6291464 | tf_op jit(solution)/shard_map/ppermute | solution.py:683
  347.7 14.9 %collective-permute-start.31 = (bf16[128,2048]{1,0:T(8,128)(2,1)}, bf16[128,2048]{1,0:T(8,128)(2,1)S(1)}, u32[]{:S(2)}, u32[]{:S(2)}) collective-permute-start(bf16[128,2048]{1,0:T(8,128)(2,1)} %get-tuple-element.166), channel_id=1, source_target_pairs={{0,3},{1,0},{2,1},{3,2},{4,7},{5,4},{6,5},{7,6},{8,11},{9,8},{10,9... | collective-permute-start | bytes 1572872 | tf_op jit(solution)/shard_map/ppermute | solution.py:871
  353.3 10.7 %collective-permute-start.47 = (f32[8,128]{1,0:T(8,128)}, f32[8,128]{1,0:T(8,128)S(1)}, u32[]{:S(2)}, u32[]{:S(2)}) collective-permute-start(f32[8,128]{1,0:T(8,128)} %mark.1), channel_id=1, source_target_pairs={{0,4},{4,0},{8,12},{12,8},{16,20},{20,16},{24,28},{28,24},{1,5},{5... | collective-permute-start | bytes 12296 | tf_op jit(solution)/shard_map/ppermute | solution.py:683
  353.6 39.8 %collective-permute-start.32 = (bf16[128,2048]{1,0:T(8,128)(2,1)}, bf16[128,2048]{1,0:T(8,128)(2,1)S(1)}, u32[]{:S(2)}, u32[]{:S(2)}) collective-permute-start(bf16[128,2048]{1,0:T(8,128)(2,1)} %get-tuple-element.167), channel_id=1, source_target_pairs={{0,2},{1,3},{2,0},{3,1},{4,6},{5,7},{6,4},{7,5},{8,10},{9,11},{10,... | collective-permute-start | bytes 1572872 | tf_op jit(solution)/shard_map/ppermute | solution.py:871
  353.6 39.8 %collective-permute-start.33 = (bf16[128,2048]{1,0:T(8,128)(2,1)}, bf16[128,2048]{1,0:T(8,128)(2,1)S(1)}, u32[]{:S(2)}, u32[]{:S(2)}) collective-permute-start(bf16[128,2048]{1,0:T(8,128)(2,1)} %get-tuple-element.168), channel_id=1, source_target_pairs={{0,1},{1,2},{2,3},{3,0},{4,5},{5,6},{6,7},{7,4},{8,9},{9,10},{10,1... | collective-permute-start | bytes 1572872 | tf_op jit(solution)/shard_map/ppermute | solution.py:871
  355.4 38.1 %collective-permute-start.48 = (bf16[512,512]{1,0:T(8,128)(2,1)}, bf16[512,512]{1,0:T(8,128)(2,1)S(1)}, u32[]{:S(2)}, u32[]{:S(2)}) collective-permute-start(bf16[512,512]{1,0:T(8,128)(2,1)} %get-tuple-element.189.refs_0_), channel_id=1, source_target_pairs={{8,0},{12,4},{24,16},{28,20},{9,1},{13,5},{25,17},{29,21},{10,2},{... | collective-permute-start | bytes 1572872 | tf_op jit(solution)/shard_map/ppermute | solution.py:697
  362.7 31.3 %collective-permute-start.49 = (bf16[512,512]{1,0:T(8,128)(2,1)}, bf16[512,512]{1,0:T(8,128)(2,1)S(1)}, u32[]{:S(2)}, u32[]{:S(2)}) collective-permute-start(bf16[512,512]{1,0:T(8,128)(2,1)} %get-tuple-element.190.refs_1_), channel_id=1, source_target_pairs={{16,0},{20,4},{24,8},{28,12},{17,1},{21,5},{25,9},{29,13},{18,2},{... | collective-permute-start | bytes 1572872 | tf_op jit(solution)/shard_map/ppermute | solution.py:697
  364.0 30.0 %collective-permute-start.50 = (bf16[512,512]{1,0:T(8,128)(2,1)}, bf16[512,512]{1,0:T(8,128)(2,1)S(1)}, u32[]{:S(2)}, u32[]{:S(2)}) collective-permute-start(bf16[512,512]{1,0:T(8,128)(2,1)} %get-tuple-element.191.refs_2_), channel_id=1, source_target_pairs={{16,8},{20,12},{17,9},{21,13},{18,10},{22,14},{19,11},{23,15}} | collective-permute-start | bytes 1572872 | tf_op jit(solution)/shard_map/ppermute | solution.py:697
  409.6 13.6 %collective-permute-start.51 = (bf16[64,2048]{1,0:T(8,128)(2,1)}, bf16[64,2048]{1,0:T(8,128)(2,1)S(1)}, u32[]{:S(2)}, u32[]{:S(2)}) collective-permute-start(bf16[64,2048]{1,0:T(8,128)(2,1)} %get-tuple-element.197), channel_id=1, source_target_pairs={{0,1},{1,2},{2,3},{3,0},{4,5},{5,6},{6,7},{7,4},{8,9},{9,10},{10,1... | collective-permute-start | bytes 786440 | tf_op jit(solution)/shard_map/ppermute | solution.py:680
  419.0 8.4 %collective-permute-start.52 = (bf16[64,2048]{1,0:T(8,128)(2,1)}, bf16[64,2048]{1,0:T(8,128)(2,1)S(1)}, u32[]{:S(2)}, u32[]{:S(2)}) collective-permute-start(bf16[64,2048]{1,0:T(8,128)(2,1)} %get-tuple-element.198), channel_id=1, source_target_pairs={{0,1},{1,2},{2,3},{3,0},{4,5},{5,6},{6,7},{7,4},{8,9},{9,10},{10,1... | collective-permute-start | bytes 786440 | tf_op jit(solution)/shard_map/ppermute | solution.py:680
  429.3 8.4 %collective-permute-start.54 = (bf16[64,2048]{1,0:T(8,128)(2,1)S(1)}, bf16[64,2048]{1,0:T(8,128)(2,1)S(1)}, u32[]{:S(2)}, u32[]{:S(2)}) collective-permute-start(bf16[64,2048]{1,0:T(8,128)(2,1)S(1)} %add_convert_fusion.2), channel_id=1, source_target_pairs={{0,1},{1,2},{2,3},{3,0},{4,5},{5,6},{6,7},{7,4},{8,9},{9,10},{10,1... | collective-permute-start | bytes 786440 | tf_op jit(solution)/shard_map/ppermute | solution.py:680
  432.1 8.4 %collective-permute-start.53 = (bf16[64,2048]{1,0:T(8,128)(2,1)S(1)}, bf16[64,2048]{1,0:T(8,128)(2,1)S(1)}, u32[]{:S(2)}, u32[]{:S(2)}) collective-permute-start(bf16[64,2048]{1,0:T(8,128)(2,1)S(1)} %add_convert_fusion.3), channel_id=1, source_target_pairs={{0,1},{1,2},{2,3},{3,0},{4,5},{5,6},{6,7},{7,4},{8,9},{9,10},{10,1... | collective-permute-start | bytes 786440 | tf_op jit(solution)/shard_map/ppermute | solution.py:680
  440.6 19.1 %collective-permute-start.57 = (bf16[64,2048]{1,0:T(8,128)(2,1)S(1)}, bf16[64,2048]{1,0:T(8,128)(2,1)S(1)}, u32[]{:S(2)}, u32[]{:S(2)}) collective-permute-start(bf16[64,2048]{1,0:T(8,128)(2,1)S(1)} %add_convert_fusion), channel_id=1, source_target_pairs={{0,1},{1,2},{2,3},{3,0},{4,5},{5,6},{6,7},{7,4},{8,9},{9,10},{10,1... | collective-permute-start | bytes 786440 | tf_op jit(solution)/shard_map/ppermute | solution.py:680
  440.7 19.0 %collective-permute-start.56 = (bf16[64,2048]{1,0:T(8,128)(2,1)S(1)}, bf16[64,2048]{1,0:T(8,128)(2,1)S(1)}, u32[]{:S(2)}, u32[]{:S(2)}) collective-permute-start(bf16[64,2048]{1,0:T(8,128)(2,1)S(1)} %add_convert_fusion.1), channel_id=1, source_target_pairs={{0,1},{1,2},{2,3},{3,0},{4,5},{5,6},{6,7},{7,4},{8,9},{9,10},{10,1... | collective-permute-start | bytes 786440 | tf_op jit(solution)/shard_map/ppermute | solution.py:680
  441.6 14.3 %collective-permute-start.60 = (f32[34,128]{1,0:T(8,128)S(1)}, f32[34,128]{1,0:T(8,128)S(1)}, u32[]{:S(2)}, u32[]{:S(2)}) collective-permute-start(f32[34,128]{1,0:T(8,128)S(1)} %fusion.7), channel_id=1, source_target_pairs={{0,24},{4,28},{8,16},{12,20},{16,8},{20,12},{24,0},{28,4},{1,25},{... | collective-permute-start | bytes 52232 | tf_op jit(solution)/shard_map/ppermute | solution.py:683
  453.2 4.7 collective-permute-start.59
  459.7 12.7 %collective-permute-start.63 = (f32[34,128]{1,0:T(8,128)S(1)}, f32[34,128]{1,0:T(8,128)S(1)}, u32[]{:S(2)}, u32[]{:S(2)}) collective-permute-start(f32[34,128]{1,0:T(8,128)S(1)} %add_add_fusion.1), channel_id=1, source_target_pairs={{0,3},{1,0},{2,1},{3,2},{4,7},{5,4},{6,5},{7,6},{8,11},{9,8},{10,9... | collective-permute-start | bytes 52232 | tf_op jit(solution)/shard_map/ppermute | solution.py:931
  463.6 8.8 %collective-permute-start.62 = (f32[34,128]{1,0:T(8,128)S(1)}, f32[34,128]{1,0:T(8,128)S(1)}, u32[]{:S(2)}, u32[]{:S(2)}) collective-permute-start(f32[34,128]{1,0:T(8,128)S(1)} %add_add_fusion.1), channel_id=1, source_target_pairs={{0,2},{1,3},{2,0},{3,1},{4,6},{5,7},{6,4},{7,5},{8,10},{9,11},{10,... | collective-permute-start | bytes 52232 | tf_op jit(solution)/shard_map/ppermute | solution.py:931
  464.1 8.2 %collective-permute-start.61 = (f32[34,128]{1,0:T(8,128)S(1)}, f32[34,128]{1,0:T(8,128)S(1)}, u32[]{:S(2)}, u32[]{:S(2)}) collective-permute-start(f32[34,128]{1,0:T(8,128)S(1)} %add_add_fusion.1), channel_id=1, source_target_pairs={{0,1},{1,2},{2,3},{3,0},{4,5},{5,6},{6,7},{7,4},{8,9},{9,10},{10,1... | collective-permute-start | bytes 52232 | tf_op jit(solution)/shard_map/ppermute | solution.py:931
  (68 other events, 862.4 us)
Sparse Core Ops, SparseCore 0:
  10.7 48.2 all-gather.4
  60.8 120.2 all-gather.2
  255.9 139.5 reduce-scatter.2
  403.2 73.6 reduce-scatter.4
where the time goes:
time: 494 us; the launch traced here: 486 us
  waiting for transfers between devices  233 us (47%)
  Pallas kernels  150 us (30%)
  starting transfers between devices  60.5 us (12%)
  between operations  15.1 us (3%)
  local copies, waits for them, and re-layouts  14.6 us (3%)
  other arithmetic  13.1 us (3%)
    ppermute x42, waiting for transfers between devices, shift(): return lax.ppermute(values, 'mp', ring)  183 us
    pallas_call x2, Pallas kernels, feed_forward(): pl.pallas_call(functools.partial(ffn_kernel, parts=parts, held=len(held))...  32.7 us
    ppermute x42, starting transfers between devices, shift(): return lax.ppermute(values, 'mp', ring)  25.8 us
    ppermute x3, waiting for transfers between devices, body(): lax.ppermute(result_parts[slot], 'mp', [(i, (i - slot) % mp_count) for i...  22.5 us
    pallas_call x7, Pallas kernels, simple_call(): pl.pallas_call(ignoring(kernel, len(arrays), len(after)), in_specs=[vmem]...  20.1 us
    ppermute x3, waiting for transfers between devices, swap_forward(): return lax.ppermute(values, 'dp', pairs)  18.1 us
    pallas_call x1, Pallas kernels, weight_grads(): pl.pallas_call(ignoring(functools.partial(weight_grads_kernel, turns=[at...  17.2 us
    ppermute x10, starting transfers between devices, swap(): return lax.ppermute(values, 'dp', [(i, i ^ mask) for i in range(dp_count)])  15.5 us
  transfers between devices with their start and end apart: 68, of which 43 were waited for; matrix products, arithmetic and copies ran while one was open for 3% of the time, Pallas kernels for 26%

commit v1 on v0

--- a/solution.py
+++ b/solution.py
@@ -779,8 +779,9 @@
     grad_slots.append(tie_all(shift_all(grad_slots[-1]), kv_own))
     query_raw, query_rot = project_q(
         tie(attn_input, kv_own, *grad_slots[-1]), w_attn, cos_table, sin_table, q_gain, q_cols, k_cols,
-        score_scale * log2_e, [],
-    )
+        score_scale * log2_e, [flags, key_base, row_places],
+    )
+    (query_rot,), grad_slots[-1] = order([query_rot], grad_slots[-1])
     for slot in range(2, slots):
         came = shift_all(grad_slots[-1])
         if slot == 2:
@@ -865,6 +866,8 @@
     result_parts = slot_product(ffn_right, 2, w_ffn, 2, ff, slots, [], "ffn_out")
     for slot in range(1, slots):
         came = shift_all(mid_slots[-1])
+        if slot == 1:
+            came[1:], result_parts = order(came[1:], result_parts)
         mid_slots.append(came)
 
     result_came = [

time: 494 us -> 490 us (level)
  waiting for transfers between devices: 233 us -> 215 us
  starting transfers between devices: 60.5 us -> 77.7 us
    ppermute x42, starting transfers between devices: 25.8 us -> 47.9 us  [shift(): return lax.ppermute(values, 'mp', ring)]
    ppermute x42, waiting for transfers between devices: 183 us -> 163 us  [shift(): return lax.ppermute(values, 'mp', ring)]
    ppermute x3, waiting for transfers between devices: 0.46 us -> 10.9 us  [swap_back(): return lax.ppermute(values, 'dp', pairs)]
    ppermute x3, waiting for transfers between devices: 18.1 us -> 8.94 us  [swap_forward(): return lax.ppermute(values, 'dp', pairs)]
  transfers between devices with their start and end apart: 68 -> 68, of which waited for: 43 -> 39; matrix products, arithmetic and copies ran while one was open for 3% -> 3% of each run, Pallas kernels for 26% -> 26%
where the time goes in v1:
time: 490 us; the launch traced here: 485 us
  waiting for transfers between devices  215 us (44%)
  Pallas kernels  150 us (31%)
  starting transfers between devices  77.7 us (16%)
  between operations  15.1 us (3%)
  local copies, waits for them, and re-layouts  13.9 us (3%)
  other arithmetic  13.1 us (3%)
    ppermute x42, waiting for transfers between devices, shift(): return lax.ppermute(values, 'mp', ring)  163 us
    ppermute x42, starting transfers between devices, shift(): return lax.ppermute(values, 'mp', ring)  47.9 us
    pallas_call x2, Pallas kernels, feed_forward(): pl.pallas_call(functools.partial(ffn_kernel, parts=parts, held=len(held))...  32.8 us
    ppermute x3, waiting for transfers between devices, body(): lax.ppermute(result_parts[slot], 'mp', [(i, (i - slot) % mp_count) for i...  20.8 us
    pallas_call x7, Pallas kernels, simple_call(): pl.pallas_call(ignoring(kernel, len(arrays), len(after)), in_specs=[vmem]...  20.7 us
    pallas_call x1, Pallas kernels, weight_grads(): pl.pallas_call(ignoring(functools.partial(weight_grads_kernel, turns=[at...  17.2 us
    pallas_call x3, Pallas kernels, more_grads(): pl.pallas_call(ignoring(functools.partial(more_grads_kernel, rights=len(r...  13.1 us
    pallas_call x2, Pallas kernels, slot_product(): pl.pallas_call(ignoring(slot_product_kernel, 2, len(after)), grid=(width...  12.2 us
  transfers between devices with their start and end apart: 68, of which 39 were waited for; matrix products, arithmetic and copies ran while one was open for 3% of the time, Pallas kernels for 26%

profile of v1, /device:TPU:0, one launch (start us, length us, event | category | flops | bytes accessed | tf_op | source)
XLA Modules:
  0.0 485.2 jit_solution(8982141915526641326)
XLA Ops:
  13.6 3.1 collective-permute-start.1
  21.6 4.2 collective-permute-done.1.refs_3_.refs_7_
  25.8 4.8 collective-permute-done.refs_2_.refs_6_
  32.0 9.7 %collective-permute-done.2.refs_4_.refs_8_ = bf16[64,2048]{1,0:T(8,128)(2,1)S(1)} collective-permute-done((bf16[64,2048]{1,0:T(8,128)(2,1)S(1)}, bf16[64,2048]{1,0:T(8,128)(2,1)S(1)}, u32[]{:S(2)}, u32[]{:S(2)}) %collective-permute-start.2) | collective-permute-done | bytes 262176 | tf_op jit(solution)/shard_map/ppermute | solution.py:680
  41.7 5.6 %collective-permute-done.3.refs_5_.refs_9_ = bf16[64,2048]{1,0:T(8,128)(2,1)S(1)} collective-permute-done((bf16[64,2048]{1,0:T(8,128)(2,1)S(1)}, bf16[64,2048]{1,0:T(8,128)(2,1)S(1)}, u32[]{:S(2)}, u32[]{:S(2)}) %collective-permute-start.3) | collective-permute-done | bytes 262176 | tf_op jit(solution)/shard_map/ppermute | solution.py:680
  47.9 5.0 %collective-permute-done.4.refs_6_.refs_10_ = bf16[64,2048]{1,0:T(8,128)(2,1)S(1)} collective-permute-done((bf16[64,2048]{1,0:T(8,128)(2,1)S(1)}, bf16[64,2048]{1,0:T(8,128)(2,1)S(1)}, u32[]{:S(2)}, u32[]{:S(2)}) %collective-permute-start.4) | collective-permute-done | bytes 262176 | tf_op jit(solution)/shard_map/ppermute | solution.py:680
  52.9 3.9 collective-permute-done.5.refs_7_.refs_11_
  59.0 6.5 %project_kv.1 = (bf16[512,2048]{1,0:T(8,128)(2,1)}, f32[512,128]{1,0:T(8,128)}, f32[512,256]{1,0:T(8,128)}, bf16[512,512]{1,0:T(8,128)(2,1)}) custom-call(bf16[2048,1536]{1,0:T(8,128)(2,1)} %all-gather.5.cloned.1.call-done.w_ref.refs_1_.refs_0_.refs_2_, f32[512,128]{1,0:T(8,128)} %pad_maximum_fusion.2.cos_ref.refs_2_.refs_1_, ...), custom_call_target="tpu_custom_call" | custom-call | flops 1048576 | bytes 65536 | tf_op jit(solution)/shard_map/project_kv/pallas_call | solution.py:226
  66.2 3.8 collective-permute-start.9
  70.0 3.4 collective-permute-start.8
  73.5 5.9 %project_q.1 = (f32[512,512]{1,0:T(8,128)}, bf16[512,512]{1,0:T(8,128)(2,1)}) custom-call(bf16[512,2048]{1,0:T(8,128)(2,1)} %get-tuple-element.138.refs_0_, bf16[2048,1536]{1,0:T(8,128)(2,1)} %all-gather.5.cloned.1.call-done.w_ref.refs_1_.refs_0_.refs_2_, f32[512,128]{1,0:T(8,128)} %pad_maximum_fusion.2.cos_ref.refs_2_.refs_1_, ...), custom_call_target="tpu_custom_call" | custom-call | flops 1048576 | bytes 65536 | tf_op jit(solution)/shard_map/project_q/pallas_call | solution.py:258
  80.8 3.5 collective-permute-start.12
  84.3 6.3 %collective-permute-done.11.refs_4_ = bf16[64,2048]{1,0:T(8,128)(2,1)S(1)} collective-permute-done((bf16[64,2048]{1,0:T(8,128)(2,1)}, bf16[64,2048]{1,0:T(8,128)(2,1)S(1)}, u32[]{:S(2)}, u32[]{:S(2)}) %collective-permute-start.11) | collective-permute-done | bytes 262176 | tf_op jit(solution)/shard_map/ppermute | solution.py:680
  90.6 4.3 collective-permute-done.12.refs_5_
  95.0 8.9 %collective-permute-done.9.refs_2_ = bf16[512,512]{1,0:T(8,128)(2,1)S(1)} collective-permute-done((bf16[512,512]{1,0:T(8,128)(2,1)}, bf16[512,512]{1,0:T(8,128)(2,1)S(1)}, u32[]{:S(2)}, u32[]{:S(2)}) %collective-permute-start.9) | collective-permute-done | bytes 524320 | tf_op jit(solution)/shard_map/ppermute | solution.py:693
  108.7 7.8 %attn_fwd.1 = (bf16[512,512]{1,0:T(8,128)(2,1)}, f32[2,1,1024]{2,1,0:T(1,128)}) custom-call(s32[8]{0:T(128)} %convert_select_fusion.1.refs_5_.flags_ref, s32[32]{0:T(128)} %add.167.refs_6_.base_ref, s32[1024,2]{1,0:T(8,128)} %copy.56.refs_7_.places_ref, bf16[512,512]{1,0:T(8,128)(2,1)} %get-tuple-element.140.q_ref, ...), custom_call_target="tpu_custom_call" | custom-call | flops 1048576 | bytes 65536 | tf_op jit(solution)/shard_map/attn_fwd/pallas_call | solution.py:807
  116.6 4.0 collective-permute-done.18.refs_7_
  120.6 4.7 attn_out.1
  126.8 9.7 %collective-permute-done.19 = bf16[64,2048]{1,0:T(8,128)(2,1)S(1)} collective-permute-done((bf16[64,2048]{1,0:T(8,128)(2,1)}, bf16[64,2048]{1,0:T(8,128)(2,1)S(1)}, u32[]{:S(2)}, u32[]{:S(2)}) %collective-permute-start.19) | collective-permute-done | bytes 262176 | tf_op jit(solution)/shard_map/ppermute | solution.py:680
  137.6 4.5 collective-permute-done.22
  143.3 4.4 collective-permute-done.20
  148.8 5.5 %collective-permute-done.23 = bf16[64,2048]{1,0:T(8,128)(2,1)S(1)} collective-permute-done((bf16[64,2048]{1,0:T(8,128)(2,1)S(1)}, bf16[64,2048]{1,0:T(8,128)(2,1)S(1)}, u32[]{:S(2)}, u32[]{:S(2)}) %collective-permute-start.23) | collective-permute-done | bytes 262176 | tf_op jit(solution)/shard_map/ppermute | solution.py:680
  154.6 5.3 %collective-permute-done.21.refs_0_ = bf16[64,2048]{1,0:T(8,128)(2,1)S(1)} collective-permute-done((bf16[64,2048]{1,0:T(8,128)(2,1)S(1)}, bf16[64,2048]{1,0:T(8,128)(2,1)S(1)}, u32[]{:S(2)}, u32[]{:S(2)}) %collective-permute-start.21) | collective-permute-done | bytes 262176 | tf_op jit(solution)/shard_map/ppermute | solution.py:680
  159.9 3.4 collective-permute-done.24.refs_1_
  167.0 11.0 %collective-permute-done.25.refs_2_ = bf16[64,2048]{1,0:T(8,128)(2,1)S(1)} collective-permute-done((bf16[64,2048]{1,0:T(8,128)(2,1)}, bf16[64,2048]{1,0:T(8,128)(2,1)S(1)}, u32[]{:S(2)}, u32[]{:S(2)}) %collective-permute-start.25) | collective-permute-done | bytes 262176 | tf_op jit(solution)/shard_map/ppermute | solution.py:680
  178.0 5.6 %collective-permute-done.26.refs_3_ = bf16[64,2048]{1,0:T(8,128)(2,1)S(1)} collective-permute-done((bf16[64,2048]{1,0:T(8,128)(2,1)}, bf16[64,2048]{1,0:T(8,128)(2,1)S(1)}, u32[]{:S(2)}, u32[]{:S(2)}) %collective-permute-start.26) | collective-permute-done | bytes 262176 | tf_op jit(solution)/shard_map/ppermute | solution.py:680
  184.3 16.4 %feed_forward.2 = (bf16[512,4608]{1,0:T(8,128)(2,1)}, bf16[512,2048]{1,0:T(8,128)(2,1)}, bf16[512,2048]{1,0:T(8,128)(2,1)}, bf16[64,2048]{1,0:T(8,128)(2,1)}, bf...) custom-call(bf16[2048,4608]{1,0:T(8,128)(2,1)} %all-gather.3.cloned.1.call-done.gate_ref.up_ref.down_ref.r, ...), custom_call_target="tpu_custom_call" | custom-call | flops 1048576 | bytes 65536 | tf_op jit(solution)/shard_map/feed_forward/pallas_call | solution.py:503
  200.9 8.4 %collective-permute-done.29.refs_2_ = bf16[64,2048]{1,0:T(8,128)(2,1)S(1)} collective-permute-done((bf16[64,2048]{1,0:T(8,128)(2,1)S(1)}, bf16[64,2048]{1,0:T(8,128)(2,1)S(1)}, u32[]{:S(2)}, u32[]{:S(2)}) %collective-permute-start.29) | collective-permute-done | bytes 262176 | tf_op jit(solution)/shard_map/ppermute | solution.py:680
  209.3 3.3 collective-permute-done.30.refs_3_
  213.4 16.4 %feed_forward.3 = (bf16[512,4608]{1,0:T(8,128)(2,1)}, bf16[512,2048]{1,0:T(8,128)(2,1)}, bf16[512,2048]{1,0:T(8,128)(2,1)}, bf16[64,2048]{1,0:T(8,128)(2,1)}, bf...) custom-call(bf16[2048,4608]{1,0:T(8,128)(2,1)} %all-gather.3.cloned., ...), custom_call_target="tpu_custom_call", output_to_operand_aliasing={{0}: (11, {}), {1}: (12, {}), {2}: (13, {})} | custom-call | flops 1048576 | bytes 65536 | tf_op jit(solution)/shard_map/feed_forward/pallas_call | solution.py:503
  229.8 17.2 %ffn_grads.1 = bf16[2048,4608]{1,0:T(8,128)(2,1)} custom-call(bf16[512,2048]{1,0:T(8,128)(2,1)} %get-tuple-element.179.refs_0_, bf16[512,2048]{1,0:T(8,128)(2,1)} %get-tuple-element.180.refs_1_, bf16[512,4608]{1,0:T(8,128)(2,1)} %get-tuple-element.182.refs_2_.refs_0_), custom_call_target="tpu_custom_call" | custom-call | flops 1048576 | bytes 65536 | tf_op jit(solution)/shard_map/ffn_grads/pallas_call | solution.py:546
  252.4 5.5 %collective-permute-done.32 = bf16[64,2048]{1,0:T(8,128)(2,1)S(1)} collective-permute-done((bf16[64,2048]{1,0:T(8,128)(2,1)S(1)}, bf16[64,2048]{1,0:T(8,128)(2,1)S(1)}, u32[]{:S(2)}, u32[]{:S(2)}) %collective-permute-start.32) | collective-permute-done | bytes 262176 | tf_op jit(solution)/shard_map/ppermute | solution.py:680
  266.1 3.9 collective-permute-done.36.refs_1_
  273.4 4.3 mid.1
  280.5 7.5 %ffn_out.1 = (bf16[128,2048]{1,0:T(8,128)(2,1)}, bf16[128,2048]{1,0:T(8,128)(2,1)}, bf16[128,2048]{1,0:T(8,128)(2,1)}, bf16[128,2048]{1,0:T(8,128)(2,1)}) custom-call(bf16[512,4608]{1,0:T(8,128)(2,1)} %get-tuple-element.182.refs_2_.refs_0_, bf16[2048,4608]{1,0:T(8,128)(2,1)} %all-gather.3.cloned.1.call-done.gate_ref.up_ref.down_ref.refs_1_), custom_call_target="tpu_custom_call" | custom-call | flops 1048576 | bytes 65536 | tf_op jit(solution)/shard_map/ffn_out/pallas_call | solution.py:569
  288.1 3.9 collective-permute-done.41.refs_3_
  292.0 6.7 %collective-permute-done.43.refs_6_ = bf16[64,2048]{1,0:T(8,128)(2,1)S(1)} collective-permute-done((bf16[64,2048]{1,0:T(8,128)(2,1)S(1)}, bf16[64,2048]{1,0:T(8,128)(2,1)S(1)}, u32[]{:S(2)}, u32[]{:S(2)}) %collective-permute-start.43) | collective-permute-done | bytes 262176 | tf_op jit(solution)/shard_map/ppermute | solution.py:680
  298.7 5.6 %collective-permute-done.42.refs_5_ = bf16[64,2048]{1,0:T(8,128)(2,1)S(1)} collective-permute-done((bf16[64,2048]{1,0:T(8,128)(2,1)S(1)}, bf16[64,2048]{1,0:T(8,128)(2,1)S(1)}, u32[]{:S(2)}, u32[]{:S(2)}) %collective-permute-start.42) | collective-permute-done | bytes 262176 | tf_op jit(solution)/shard_map/ppermute | solution.py:680
  304.6 4.0 collective-permute-done.45.refs_8_
  308.6 4.1 collective-permute-done.44.refs_7_
  313.5 4.8 grad_attended.1
  318.3 11.8 %attn_bwd.1 = (f32[512,512]{1,0:T(8,128)}, bf16[2048,512]{1,0:T(8,128)(2,1)}, bf16[2048,512]{1,0:T(8,128)(2,1)}) custom-call(s32[8]{0:T(128)} %convert_select_fusion.1.refs_5_.flags_ref, s32[32]{0:T(128)} %add.167.refs_6_.base_ref, s32[2,1024]{1,0:T(2,128)} %copy-done.56, bf16[512,512]{1,0:T(8,128)(2,1)} %get-tuple-element.140.q_ref, ...), custom_call_target="tpu_custom_call" | custom-call | flops 1048576 | bytes 65536 | tf_op jit(solution)/shard_map/attn_bwd/pallas_call | solution.py:881
  330.2 4.3 collective-permute-done.46.refs_1_.refs_5_
  335.9 3.6 fold_blocks.1
  341.5 3.0 collective-permute-done.38.refs_1_.refs_10_
  346.5 4.4 out_grads.1.refs_2_
  351.0 3.6 unproject_q.1
  354.5 4.3 q_grads.1.refs_9_.refs_2_
  358.8 17.8 %collective-permute-done.39.refs_2_.refs_11_ = bf16[128,2048]{1,0:T(8,128)(2,1)S(1)} collective-permute-done((bf16[128,2048]{1,0:T(8,128)(2,1)}, bf16[128,2048]{1,0:T(8,128)(2,1)S(1)}, u32[]{:S(2)}, u32[]{:S(2)}) %collective-permute-start.39) | collective-permute-done | bytes 524320 | tf_op jit(solution)/shard_map/ppermute | solution.py:874
  376.7 10.9 %collective-permute-done.49.refs_7_ = bf16[512,512]{1,0:T(8,128)(2,1)S(1)} collective-permute-done((bf16[512,512]{1,0:T(8,128)(2,1)}, bf16[512,512]{1,0:T(8,128)(2,1)S(1)}, u32[]{:S(2)}, u32[]{:S(2)}) %collective-permute-start.49) | collective-permute-done | bytes 524320 | tf_op jit(solution)/shard_map/ppermute | solution.py:697
  388.5 3.7 unproject_kv.1
  392.2 4.4 kv_grads.1.refs_12_
  396.6 6.5 %attn_back.1 = (bf16[64,2048]{1,0:T(8,128)(2,1)}, bf16[64,2048]{1,0:T(8,128)(2,1)}, bf16[64,2048]{1,0:T(8,128)(2,1)}, bf16[64,2048]{1,0:T(8,128)(2,1)}, bf16[64,...) custom-call(bf16[512,512]{1,0:T(8,128)(2,1)} %get-tuple-element.208., ...), custom_call_target="tpu_custom_call" | custom-call | flops 1048576 | bytes 65536 | tf_op jit(solution)/shard_map/attn_back/pallas_call | solution.py:332
  403.2 14.7 %collective-permute-start.51 = (bf16[64,2048]{1,0:T(8,128)(2,1)}, bf16[64,2048]{1,0:T(8,128)(2,1)S(1)}, u32[]{:S(2)}, u32[]{:S(2)}) collective-permute-start(bf16[64,2048]{1,0:T(8,128)(2,1)} %get-tuple-element.213), channel_id=1, source_target_pairs={{0,1},{1,2},{2,3},{3,0},{4,5},{5,6},{6,7},{7,4},{8,9},{9,10},{10,1... | collective-permute-start | bytes 786440 | tf_op jit(solution)/shard_map/ppermute | solution.py:680
  418.0 6.9 %collective-permute-done.51 = bf16[64,2048]{1,0:T(8,128)(2,1)S(1)} collective-permute-done((bf16[64,2048]{1,0:T(8,128)(2,1)}, bf16[64,2048]{1,0:T(8,128)(2,1)S(1)}, u32[]{:S(2)}, u32[]{:S(2)}) %collective-permute-start.51) | collective-permute-done | bytes 262176 | tf_op jit(solution)/shard_map/ppermute | solution.py:680
  424.9 4.6 collective-permute-done.52
  435.7 4.3 split_ffn.1
  440.0 3.4 collective-permute-done.53
  443.7 3.9 collective-permute-start.60
  447.6 5.9 %collective-permute-start.59 = (f32[34,128]{1,0:T(8,128)S(1)}, f32[34,128]{1,0:T(8,128)S(1)}, u32[]{:S(2)}, u32[]{:S(2)}) collective-permute-start(f32[34,128]{1,0:T(8,128)S(1)} %fusion.7), channel_id=1, source_target_pairs={{0,16},{4,20},{8,24},{12,28},{16,0},{20,4},{24,8},{28,12},{1,17},{... | collective-permute-start | bytes 52232 | tf_op jit(solution)/shard_map/ppermute | solution.py:683
  457.4 3.9 collective-permute-start.63
  463.6 3.1 result.1
  466.8 3.3 last.1
  471.2 4.6 reduce-scatter.5.cloned.1.call-done.refs_0_
  (279 shorter events, 76.2 us)
Async XLA Ops:
  7.2 51.7 %all-gather.5.cloned.1.call-start = ((), (), s32[]{:S(2)}) async-start(), calls=%async_computation.3 | async-start | bytes 7077888 | tf_op jit(solution)/shard_map/all_gather | solution.py:733
  10.5 173.1 %all-gather.3.cloned.1.call-start = ((), (), s32[]{:S(2)}) async-start(), calls=%async_computation.2 | async-start | bytes 21233664 | tf_op jit(solution)/shard_map/all_gather | solution.py:734
  12.5 379.7 %reduce-scatter.3.cloned.1.call-start = ((), (), s32[]{:S(2)}) async-start(), calls=%async_computation.4 | async-start | bytes 21233664 | tf_op jit(solution)/shard_map/reduce_scatter | solution.py:858
  13.6 12.2 %collective-permute-start.1 = (bf16[64,2048]{1,0:T(8,128)(2,1)S(1)}, bf16[64,2048]{1,0:T(8,128)(2,1)S(1)}, u32[]{:S(2)}, u32[]{:S(2)}) collective-permute-start(bf16[64,2048]{1,0:T(8,128)(2,1)S(1)} %get-tuple-element.255.refs_1_.refs_5_), channel_id=1, source_target_pairs={{0,1},{1,2},{2,3},{3,0},{4,5},{5,6},{6,7},{7,4},{8,9},{9,10},{10,1... | collective-permute-start | bytes 786440 | tf_op jit(solution)/shard_map/ppermute | solution.py:680
  16.7 13.9 %collective-permute-start = (bf16[64,2048]{1,0:T(8,128)(2,1)S(1)}, bf16[64,2048]{1,0:T(8,128)(2,1)S(1)}, u32[]{:S(2)}, u32[]{:S(2)}) collective-permute-start(bf16[64,2048]{1,0:T(8,128)(2,1)S(1)} %get-tuple-element.256.refs_0_.refs_4_), channel_id=1, source_target_pairs={{0,1},{1,2},{2,3},{3,0},{4,5},{5,6},{6,7},{7,4},{8,9},{9,10},{10,1... | collective-permute-start | bytes 786440 | tf_op jit(solution)/shard_map/ppermute | solution.py:680
  30.6 11.0 %collective-permute-start.2 = (bf16[64,2048]{1,0:T(8,128)(2,1)S(1)}, bf16[64,2048]{1,0:T(8,128)(2,1)S(1)}, u32[]{:S(2)}, u32[]{:S(2)}) collective-permute-start(bf16[64,2048]{1,0:T(8,128)(2,1)S(1)} %collective-permute-done.refs_2_.refs_6_), channel_id=1, source_target_pairs={{0,1},{1,2},{2,3},{3,0},{4,5},{5,6},{6,7},{7,4},{8,9},{9,10},{10,1... | collective-permute-start | bytes 786440 | tf_op jit(solution)/shard_map/ppermute | solution.py:680
  30.6 16.7 %collective-permute-start.3 = (bf16[64,2048]{1,0:T(8,128)(2,1)S(1)}, bf16[64,2048]{1,0:T(8,128)(2,1)S(1)}, u32[]{:S(2)}, u32[]{:S(2)}) collective-permute-start(bf16[64,2048]{1,0:T(8,128)(2,1)S(1)} %collective-permute-done.1.refs_3_.refs_7_), channel_id=1, source_target_pairs={{0,1},{1,2},{2,3},{3,0},{4,5},{5,6},{6,7},{7,4},{8,9},{9,10},{10,1... | collective-permute-start | bytes 786440 | tf_op jit(solution)/shard_map/ppermute | solution.py:680
  41.7 11.2 %collective-permute-start.4 = (bf16[64,2048]{1,0:T(8,128)(2,1)S(1)}, bf16[64,2048]{1,0:T(8,128)(2,1)S(1)}, u32[]{:S(2)}, u32[]{:S(2)}) collective-permute-start(bf16[64,2048]{1,0:T(8,128)(2,1)S(1)} %collective-permute-done.2.refs_4_.refs_8_), channel_id=1, source_target_pairs={{0,1},{1,2},{2,3},{3,0},{4,5},{5,6},{6,7},{7,4},{8,9},{9,10},{10,1... | collective-permute-start | bytes 786440 | tf_op jit(solution)/shard_map/ppermute | solution.py:680
  47.3 9.5 %collective-permute-start.5 = (bf16[64,2048]{1,0:T(8,128)(2,1)S(1)}, bf16[64,2048]{1,0:T(8,128)(2,1)S(1)}, u32[]{:S(2)}, u32[]{:S(2)}) collective-permute-start(bf16[64,2048]{1,0:T(8,128)(2,1)S(1)} %collective-permute-done.3.refs_5_.refs_9_), channel_id=1, source_target_pairs={{0,1},{1,2},{2,3},{3,0},{4,5},{5,6},{6,7},{7,4},{8,9},{9,10},{10,1... | collective-permute-start | bytes 786440 | tf_op jit(solution)/shard_map/ppermute | solution.py:680
  56.8 16.7 %collective-permute-start.6 = (bf16[64,2048]{1,0:T(8,128)(2,1)S(1)}, bf16[64,2048]{1,0:T(8,128)(2,1)}, u32[]{:S(2)}, u32[]{:S(2)}) collective-permute-start(bf16[64,2048]{1,0:T(8,128)(2,1)S(1)} %get-tuple-element.134.refs_4_), channel_id=1, source_target_pairs={{0,1},{1,2},{2,3},{3,0},{4,5},{5,6},{6,7},{7,4},{8,9},{9,10},{10,1... | collective-permute-start | bytes 786440 | tf_op jit(solution)/shard_map/ppermute | solution.py:680
  56.8 16.7 %collective-permute-start.7 = (bf16[64,2048]{1,0:T(8,128)(2,1)S(1)}, bf16[64,2048]{1,0:T(8,128)(2,1)}, u32[]{:S(2)}, u32[]{:S(2)}) collective-permute-start(bf16[64,2048]{1,0:T(8,128)(2,1)S(1)} %get-tuple-element.135.refs_5_), channel_id=1, source_target_pairs={{0,1},{1,2},{2,3},{3,0},{4,5},{5,6},{6,7},{7,4},{8,9},{9,10},{10,1... | collective-permute-start | bytes 786440 | tf_op jit(solution)/shard_map/ppermute | solution.py:680
  65.5 29.5 %collective-permute-start.10 = (bf16[512,512]{1,0:T(8,128)(2,1)}, bf16[512,512]{1,0:T(8,128)(2,1)S(1)}, u32[]{:S(2)}, u32[]{:S(2)}) collective-permute-start(bf16[512,512]{1,0:T(8,128)(2,1)} %get-tuple-element.133.refs_0_), channel_id=1, source_target_pairs={{8,16},{12,20},{9,17},{13,21},{10,18},{14,22},{11,19},{15,23}} | collective-permute-start | bytes 1572872 | tf_op jit(solution)/shard_map/ppermute | solution.py:693
  66.2 37.7 %collective-permute-start.9 = (bf16[512,512]{1,0:T(8,128)(2,1)}, bf16[512,512]{1,0:T(8,128)(2,1)S(1)}, u32[]{:S(2)}, u32[]{:S(2)}) collective-permute-start(bf16[512,512]{1,0:T(8,128)(2,1)} %get-tuple-element.133.refs_0_), channel_id=1, source_target_pairs={{0,16},{4,20},{8,24},{12,28},{1,17},{5,21},{9,25},{13,29},{2,18},{... | collective-permute-start | bytes 1572872 | tf_op jit(solution)/shard_map/ppermute | solution.py:693
  70.0 33.9 %collective-permute-start.8 = (bf16[512,512]{1,0:T(8,128)(2,1)}, bf16[512,512]{1,0:T(8,128)(2,1)S(1)}, u32[]{:S(2)}, u32[]{:S(2)}) collective-permute-start(bf16[512,512]{1,0:T(8,128)(2,1)} %get-tuple-element.133.refs_0_), channel_id=1, source_target_pairs={{0,8},{4,12},{16,24},{20,28},{1,9},{5,13},{17,25},{21,29},{2,10},{... | collective-permute-start | bytes 1572872 | tf_op jit(solution)/shard_map/ppermute | solution.py:693
  79.4 11.3 %collective-permute-start.11 = (bf16[64,2048]{1,0:T(8,128)(2,1)}, bf16[64,2048]{1,0:T(8,128)(2,1)S(1)}, u32[]{:S(2)}, u32[]{:S(2)}) collective-permute-start(bf16[64,2048]{1,0:T(8,128)(2,1)} %collective-permute-done.6.refs_6_), channel_id=1, source_target_pairs={{0,1},{1,2},{2,3},{3,0},{4,5},{5,6},{6,7},{7,4},{8,9},{9,10},{10,1... | collective-permute-start | bytes 786440 | tf_op jit(solution)/shard_map/ppermute | solution.py:680
  80.8 14.2 %collective-permute-start.12 = (bf16[64,2048]{1,0:T(8,128)(2,1)}, bf16[64,2048]{1,0:T(8,128)(2,1)}, u32[]{:S(2)}, u32[]{:S(2)}) collective-permute-start(bf16[64,2048]{1,0:T(8,128)(2,1)} %collective-permute-done.7.refs_7_), channel_id=1, source_target_pairs={{0,1},{1,2},{2,3},{3,0},{4,5},{5,6},{6,7},{7,4},{8,9},{9,10},{10,1... | collective-permute-start | bytes 786440 | tf_op jit(solution)/shard_map/ppermute | solution.py:680
  90.6 15.3 %collective-permute-start.13 = (bf16[512,512]{1,0:T(8,128)(2,1)S(1)}, bf16[512,512]{1,0:T(8,128)(2,1)S(1)}, u32[]{:S(2)}, u32[]{:S(2)}) collective-permute-start(bf16[512,512]{1,0:T(8,128)(2,1)S(1)} %copy-done.8), channel_id=1, source_target_pairs={{0,4},{4,0},{8,12},{12,8},{16,20},{20,16},{24,28},{28,24},{1,5},{5... | collective-permute-start | bytes 1572872 | tf_op jit(solution)/shard_map/ppermute | solution.py:683
  104.5 12.1 %collective-permute-start.17 = (bf16[64,2048]{1,0:T(8,128)(2,1)S(1)}, bf16[64,2048]{1,0:T(8,128)(2,1)}, u32[]{:S(2)}, u32[]{:S(2)}) collective-permute-start(bf16[64,2048]{1,0:T(8,128)(2,1)S(1)} %collective-permute-done.11.refs_4_), channel_id=1, source_target_pairs={{0,1},{1,2},{2,3},{3,0},{4,5},{5,6},{6,7},{7,4},{8,9},{9,10},{10,1... | collective-permute-start | bytes 786440 | tf_op jit(solution)/shard_map/ppermute | solution.py:680
  106.0 14.6 %collective-permute-start.18 = (bf16[64,2048]{1,0:T(8,128)(2,1)}, bf16[64,2048]{1,0:T(8,128)(2,1)S(1)}, u32[]{:S(2)}, u32[]{:S(2)}) collective-permute-start(bf16[64,2048]{1,0:T(8,128)(2,1)} %collective-permute-done.12.refs_5_), channel_id=1, source_target_pairs={{0,1},{1,2},{2,3},{3,0},{4,5},{5,6},{6,7},{7,4},{8,9},{9,10},{10,1... | collective-permute-start | bytes 786440 | tf_op jit(solution)/shard_map/ppermute | solution.py:680
  125.3 11.3 %collective-permute-start.19 = (bf16[64,2048]{1,0:T(8,128)(2,1)}, bf16[64,2048]{1,0:T(8,128)(2,1)S(1)}, u32[]{:S(2)}, u32[]{:S(2)}) collective-permute-start(bf16[64,2048]{1,0:T(8,128)(2,1)} %get-tuple-element.156), channel_id=1, source_target_pairs={{0,1},{1,2},{2,3},{3,0},{4,5},{5,6},{6,7},{7,4},{8,9},{9,10},{10,1... | collective-permute-start | bytes 786440 | tf_op jit(solution)/shard_map/ppermute | solution.py:680
  125.3 16.8 %collective-permute-start.22 = (bf16[64,2048]{1,0:T(8,128)(2,1)}, bf16[64,2048]{1,0:T(8,128)(2,1)S(1)}, u32[]{:S(2)}, u32[]{:S(2)}) collective-permute-start(bf16[64,2048]{1,0:T(8,128)(2,1)} %get-tuple-element.159), channel_id=1, source_target_pairs={{0,1},{1,2},{2,3},{3,0},{4,5},{5,6},{6,7},{7,4},{8,9},{9,10},{10,1... | collective-permute-start | bytes 786440 | tf_op jit(solution)/shard_map/ppermute | solution.py:680
  137.6 10.1 %collective-permute-start.20 = (bf16[64,2048]{1,0:T(8,128)(2,1)S(1)}, bf16[64,2048]{1,0:T(8,128)(2,1)S(1)}, u32[]{:S(2)}, u32[]{:S(2)}) collective-permute-start(bf16[64,2048]{1,0:T(8,128)(2,1)S(1)} %add_convert_fusion.11), channel_id=1, source_target_pairs={{0,1},{1,2},{2,3},{3,0},{4,5},{5,6},{6,7},{7,4},{8,9},{9,10},{10,1... | collective-permute-start | bytes 786440 | tf_op jit(solution)/shard_map/ppermute | solution.py:680
  143.2 11.1 %collective-permute-start.23 = (bf16[64,2048]{1,0:T(8,128)(2,1)S(1)}, bf16[64,2048]{1,0:T(8,128)(2,1)S(1)}, u32[]{:S(2)}, u32[]{:S(2)}) collective-permute-start(bf16[64,2048]{1,0:T(8,128)(2,1)S(1)} %add_convert_fusion.9), channel_id=1, source_target_pairs={{0,1},{1,2},{2,3},{3,0},{4,5},{5,6},{6,7},{7,4},{8,9},{9,10},{10,1... | collective-permute-start | bytes 786440 | tf_op jit(solution)/shard_map/ppermute | solution.py:680
  148.7 11.2 %collective-permute-start.21 = (bf16[64,2048]{1,0:T(8,128)(2,1)S(1)}, bf16[64,2048]{1,0:T(8,128)(2,1)S(1)}, u32[]{:S(2)}, u32[]{:S(2)}) collective-permute-start(bf16[64,2048]{1,0:T(8,128)(2,1)S(1)} %add_convert_fusion.10), channel_id=1, source_target_pairs={{0,1},{1,2},{2,3},{3,0},{4,5},{5,6},{6,7},{7,4},{8,9},{9,10},{10,1... | collective-permute-start | bytes 786440 | tf_op jit(solution)/shard_map/ppermute | solution.py:680
  154.4 8.9 %collective-permute-start.24 = (bf16[64,2048]{1,0:T(8,128)(2,1)S(1)}, bf16[64,2048]{1,0:T(8,128)(2,1)S(1)}, u32[]{:S(2)}, u32[]{:S(2)}) collective-permute-start(bf16[64,2048]{1,0:T(8,128)(2,1)S(1)} %add_convert_fusion.8), channel_id=1, source_target_pairs={{0,1},{1,2},{2,3},{3,0},{4,5},{5,6},{6,7},{7,4},{8,9},{9,10},{10,1... | collective-permute-start | bytes 786440 | tf_op jit(solution)/shard_map/ppermute | solution.py:680
  166.7 11.3 %collective-permute-start.25 = (bf16[64,2048]{1,0:T(8,128)(2,1)}, bf16[64,2048]{1,0:T(8,128)(2,1)S(1)}, u32[]{:S(2)}, u32[]{:S(2)}) collective-permute-start(bf16[64,2048]{1,0:T(8,128)(2,1)} %get-tuple-element.164.refs_0_), channel_id=1, source_target_pairs={{0,1},{1,2},{2,3},{3,0},{4,5},{5,6},{6,7},{7,4},{8,9},{9,10},{10,1... | collective-permute-start | bytes 786440 | tf_op jit(solution)/shard_map/ppermute | solution.py:680
  166.8 16.9 %collective-permute-start.26 = (bf16[64,2048]{1,0:T(8,128)(2,1)}, bf16[64,2048]{1,0:T(8,128)(2,1)S(1)}, u32[]{:S(2)}, u32[]{:S(2)}) collective-permute-start(bf16[64,2048]{1,0:T(8,128)(2,1)} %get-tuple-element.165.refs_1_), channel_id=1, source_target_pairs={{0,1},{1,2},{2,3},{3,0},{4,5},{5,6},{6,7},{7,4},{8,9},{9,10},{10,1... | collective-permute-start | bytes 786440 | tf_op jit(solution)/shard_map/ppermute | solution.py:680
  178.0 22.7 %collective-permute-start.27 = (bf16[64,2048]{1,0:T(8,128)(2,1)S(1)}, bf16[64,2048]{1,0:T(8,128)(2,1)S(1)}, u32[]{:S(2)}, u32[]{:S(2)}) collective-permute-start(bf16[64,2048]{1,0:T(8,128)(2,1)S(1)} %collective-permute-done.25.refs_2_), channel_id=1, source_target_pairs={{0,1},{1,2},{2,3},{3,0},{4,5},{5,6},{6,7},{7,4},{8,9},{9,10},{10,1... | collective-permute-start | bytes 786440 | tf_op jit(solution)/shard_map/ppermute | solution.py:680
  183.6 17.1 %collective-permute-start.28 = (bf16[64,2048]{1,0:T(8,128)(2,1)S(1)}, bf16[64,2048]{1,0:T(8,128)(2,1)S(1)}, u32[]{:S(2)}, u32[]{:S(2)}) collective-permute-start(bf16[64,2048]{1,0:T(8,128)(2,1)S(1)} %collective-permute-done.26.refs_3_), channel_id=1, source_target_pairs={{0,1},{1,2},{2,3},{3,0},{4,5},{5,6},{6,7},{7,4},{8,9},{9,10},{10,1... | collective-permute-start | bytes 786440 | tf_op jit(solution)/shard_map/ppermute | solution.py:680
  200.7 8.6 %collective-permute-start.29 = (bf16[64,2048]{1,0:T(8,128)(2,1)S(1)}, bf16[64,2048]{1,0:T(8,128)(2,1)S(1)}, u32[]{:S(2)}, u32[]{:S(2)}) collective-permute-start(bf16[64,2048]{1,0:T(8,128)(2,1)S(1)} %collective-permute-done.27.refs_0_), channel_id=1, source_target_pairs={{0,1},{1,2},{2,3},{3,0},{4,5},{5,6},{6,7},{7,4},{8,9},{9,10},{10,1... | collective-permute-start | bytes 786440 | tf_op jit(solution)/shard_map/ppermute | solution.py:680
  200.8 11.9 %collective-permute-start.30 = (bf16[64,2048]{1,0:T(8,128)(2,1)S(1)}, bf16[64,2048]{1,0:T(8,128)(2,1)S(1)}, u32[]{:S(2)}, u32[]{:S(2)}) collective-permute-start(bf16[64,2048]{1,0:T(8,128)(2,1)S(1)} %collective-permute-done.28.refs_1_), channel_id=1, source_target_pairs={{0,1},{1,2},{2,3},{3,0},{4,5},{5,6},{6,7},{7,4},{8,9},{9,10},{10,1... | collective-permute-start | bytes 786440 | tf_op jit(solution)/shard_map/ppermute | solution.py:680
  212.7 17.1 %collective-permute-start.31 = (bf16[64,2048]{1,0:T(8,128)(2,1)}, bf16[64,2048]{1,0:T(8,128)(2,1)S(1)}, u32[]{:S(2)}, u32[]{:S(2)}) collective-permute-start(bf16[64,2048]{1,0:T(8,128)(2,1)} %get-tuple-element.172), channel_id=1, source_target_pairs={{0,1},{1,2},{2,3},{3,0},{4,5},{5,6},{6,7},{7,4},{8,9},{9,10},{10,1... | collective-permute-start | bytes 786440 | tf_op jit(solution)/shard_map/ppermute | solution.py:680
  212.7 17.1 %collective-permute-start.33 = (bf16[64,2048]{1,0:T(8,128)(2,1)}, bf16[64,2048]{1,0:T(8,128)(2,1)S(1)}, u32[]{:S(2)}, u32[]{:S(2)}) collective-permute-start(bf16[64,2048]{1,0:T(8,128)(2,1)} %get-tuple-element.177), channel_id=1, source_target_pairs={{0,1},{1,2},{2,3},{3,0},{4,5},{5,6},{6,7},{7,4},{8,9},{9,10},{10,1... | collective-permute-start | bytes 786440 | tf_op jit(solution)/shard_map/ppermute | solution.py:680
  247.0 228.8 %reduce-scatter.5.cloned.1.call-start = ((), (), s32[]{:S(2)}) async-start(), calls=%async_computation.5 | async-start | bytes 7077888 | tf_op jit(solution)/shard_map/reduce_scatter | solution.py:915
  248.0 10.0 %collective-permute-start.32 = (bf16[64,2048]{1,0:T(8,128)(2,1)S(1)}, bf16[64,2048]{1,0:T(8,128)(2,1)S(1)}, u32[]{:S(2)}, u32[]{:S(2)}) collective-permute-start(bf16[64,2048]{1,0:T(8,128)(2,1)S(1)} %add_convert_fusion.7), channel_id=1, source_target_pairs={{0,1},{1,2},{2,3},{3,0},{4,5},{5,6},{6,7},{7,4},{8,9},{9,10},{10,1... | collective-permute-start | bytes 786440 | tf_op jit(solution)/shard_map/ppermute | solution.py:680
  250.2 10.6 %collective-permute-start.34 = (bf16[64,2048]{1,0:T(8,128)(2,1)S(1)}, bf16[64,2048]{1,0:T(8,128)(2,1)S(1)}, u32[]{:S(2)}, u32[]{:S(2)}) collective-permute-start(bf16[64,2048]{1,0:T(8,128)(2,1)S(1)} %add_convert_fusion.6), channel_id=1, source_target_pairs={{0,1},{1,2},{2,3},{3,0},{4,5},{5,6},{6,7},{7,4},{8,9},{9,10},{10,1... | collective-permute-start | bytes 786440 | tf_op jit(solution)/shard_map/ppermute | solution.py:680
  260.9 9.1 %collective-permute-start.36 = (bf16[64,2048]{1,0:T(8,128)(2,1)S(1)}, bf16[64,2048]{1,0:T(8,128)(2,1)S(1)}, u32[]{:S(2)}, u32[]{:S(2)}) collective-permute-start(bf16[64,2048]{1,0:T(8,128)(2,1)S(1)} %add_convert_fusion.4), channel_id=1, source_target_pairs={{0,1},{1,2},{2,3},{3,0},{4,5},{5,6},{6,7},{7,4},{8,9},{9,10},{10,1... | collective-permute-start | bytes 786440 | tf_op jit(solution)/shard_map/ppermute | solution.py:680
  263.5 9.2 %collective-permute-start.35 = (bf16[64,2048]{1,0:T(8,128)(2,1)S(1)}, bf16[64,2048]{1,0:T(8,128)(2,1)S(1)}, u32[]{:S(2)}, u32[]{:S(2)}) collective-permute-start(bf16[64,2048]{1,0:T(8,128)(2,1)S(1)} %add_convert_fusion.5), channel_id=1, source_target_pairs={{0,1},{1,2},{2,3},{3,0},{4,5},{5,6},{6,7},{7,4},{8,9},{9,10},{10,1... | collective-permute-start | bytes 786440 | tf_op jit(solution)/shard_map/ppermute | solution.py:680
  277.8 10.2 %collective-permute-start.37 = (bf16[64,2048]{1,0:T(8,128)(2,1)}, bf16[64,2048]{1,0:T(8,128)(2,1)S(1)}, u32[]{:S(2)}, u32[]{:S(2)}) collective-permute-start(bf16[64,2048]{1,0:T(8,128)(2,1)} %get-tuple-element.188.refs_2_), channel_id=1, source_target_pairs={{0,1},{1,2},{2,3},{3,0},{4,5},{5,6},{6,7},{7,4},{8,9},{9,10},{10,1... | collective-permute-start | bytes 786440 | tf_op jit(solution)/shard_map/ppermute | solution.py:680
  278.1 14.0 %collective-permute-start.41 = (bf16[64,2048]{1,0:T(8,128)(2,1)}, bf16[64,2048]{1,0:T(8,128)(2,1)S(1)}, u32[]{:S(2)}, u32[]{:S(2)}) collective-permute-start(bf16[64,2048]{1,0:T(8,128)(2,1)} %get-tuple-element.199.refs_1_), channel_id=1, source_target_pairs={{0,1},{1,2},{2,3},{3,0},{4,5},{5,6},{6,7},{7,4},{8,9},{9,10},{10,1... | collective-permute-start | bytes 786440 | tf_op jit(solution)/shard_map/ppermute | solution.py:680
  288.0 10.7 %collective-permute-start.43 = (bf16[64,2048]{1,0:T(8,128)(2,1)S(1)}, bf16[64,2048]{1,0:T(8,128)(2,1)S(1)}, u32[]{:S(2)}, u32[]{:S(2)}) collective-permute-start(bf16[64,2048]{1,0:T(8,128)(2,1)S(1)} %collective-permute-done.37.refs_4_), channel_id=1, source_target_pairs={{0,1},{1,2},{2,3},{3,0},{4,5},{5,6},{6,7},{7,4},{8,9},{9,10},{10,1... | collective-permute-start | bytes 786440 | tf_op jit(solution)/shard_map/ppermute | solution.py:680
  292.0 12.3 %collective-permute-start.42 = (bf16[64,2048]{1,0:T(8,128)(2,1)S(1)}, bf16[64,2048]{1,0:T(8,128)(2,1)S(1)}, u32[]{:S(2)}, u32[]{:S(2)}) collective-permute-start(bf16[64,2048]{1,0:T(8,128)(2,1)S(1)} %collective-permute-done.41.refs_3_), channel_id=1, source_target_pairs={{0,1},{1,2},{2,3},{3,0},{4,5},{5,6},{6,7},{7,4},{8,9},{9,10},{10,1... | collective-permute-start | bytes 786440 | tf_op jit(solution)/shard_map/ppermute | solution.py:680
  298.7 9.9 %collective-permute-start.45 = (bf16[64,2048]{1,0:T(8,128)(2,1)S(1)}, bf16[64,2048]{1,0:T(8,128)(2,1)S(1)}, u32[]{:S(2)}, u32[]{:S(2)}) collective-permute-start(bf16[64,2048]{1,0:T(8,128)(2,1)S(1)} %collective-permute-done.43.refs_6_), channel_id=1, source_target_pairs={{0,1},{1,2},{2,3},{3,0},{4,5},{5,6},{6,7},{7,4},{8,9},{9,10},{10,1... | collective-permute-start | bytes 786440 | tf_op jit(solution)/shard_map/ppermute | solution.py:680
  304.3 8.4 %collective-permute-start.44 = (bf16[64,2048]{1,0:T(8,128)(2,1)S(1)}, bf16[64,2048]{1,0:T(8,128)(2,1)S(1)}, u32[]{:S(2)}, u32[]{:S(2)}) collective-permute-start(bf16[64,2048]{1,0:T(8,128)(2,1)S(1)} %collective-permute-done.42.refs_5_), channel_id=1, source_target_pairs={{0,1},{1,2},{2,3},{3,0},{4,5},{5,6},{6,7},{7,4},{8,9},{9,10},{10,1... | collective-permute-start | bytes 786440 | tf_op jit(solution)/shard_map/ppermute | solution.py:680
  330.1 4.4 collective-permute-start.46
  330.2 14.3 %collective-permute-start.38 = (bf16[128,2048]{1,0:T(8,128)(2,1)S(1)}, bf16[128,2048]{1,0:T(8,128)(2,1)S(1)}, u32[]{:S(2)}, u32[]{:S(2)}) collective-permute-start(bf16[128,2048]{1,0:T(8,128)(2,1)S(1)} %copy-done.62), channel_id=1, source_target_pairs={{0,3},{1,0},{2,1},{3,2},{4,7},{5,4},{6,5},{7,6},{8,11},{9,8},{10,9... | collective-permute-start | bytes 1572872 | tf_op jit(solution)/shard_map/ppermute | solution.py:874
  340.1 5.7 %collective-permute-start.47 = (f32[8,128]{1,0:T(8,128)}, f32[8,128]{1,0:T(8,128)S(1)}, u32[]{:S(2)}, u32[]{:S(2)}) collective-permute-start(f32[8,128]{1,0:T(8,128)} %mark.1), channel_id=1, source_target_pairs={{0,4},{4,0},{8,12},{12,8},{16,20},{20,16},{24,28},{28,24},{1,5},{5... | collective-permute-start | bytes 12296 | tf_op jit(solution)/shard_map/ppermute | solution.py:683
  340.2 36.4 %collective-permute-start.39 = (bf16[128,2048]{1,0:T(8,128)(2,1)}, bf16[128,2048]{1,0:T(8,128)(2,1)S(1)}, u32[]{:S(2)}, u32[]{:S(2)}) collective-permute-start(bf16[128,2048]{1,0:T(8,128)(2,1)} %get-tuple-element.195), channel_id=1, source_target_pairs={{0,2},{1,3},{2,0},{3,1},{4,6},{5,7},{6,4},{7,5},{8,10},{9,11},{10,... | collective-permute-start | bytes 1572872 | tf_op jit(solution)/shard_map/ppermute | solution.py:874
  340.2 36.4 %collective-permute-start.40 = (bf16[128,2048]{1,0:T(8,128)(2,1)}, bf16[128,2048]{1,0:T(8,128)(2,1)S(1)}, u32[]{:S(2)}, u32[]{:S(2)}) collective-permute-start(bf16[128,2048]{1,0:T(8,128)(2,1)} %get-tuple-element.196), channel_id=1, source_target_pairs={{0,1},{1,2},{2,3},{3,0},{4,5},{5,6},{6,7},{7,4},{8,9},{9,10},{10,1... | collective-permute-start | bytes 1572872 | tf_op jit(solution)/shard_map/ppermute | solution.py:874
  340.2 36.4 %collective-permute-start.48 = (bf16[512,512]{1,0:T(8,128)(2,1)}, bf16[512,512]{1,0:T(8,128)(2,1)S(1)}, u32[]{:S(2)}, u32[]{:S(2)}) collective-permute-start(bf16[512,512]{1,0:T(8,128)(2,1)} %get-tuple-element.205.refs_0_), channel_id=1, source_target_pairs={{8,0},{12,4},{24,16},{28,20},{9,1},{13,5},{25,17},{29,21},{10,2},{... | collective-permute-start | bytes 1572872 | tf_op jit(solution)/shard_map/ppermute | solution.py:697
  344.5 43.0 %collective-permute-start.49 = (bf16[512,512]{1,0:T(8,128)(2,1)}, bf16[512,512]{1,0:T(8,128)(2,1)S(1)}, u32[]{:S(2)}, u32[]{:S(2)}) collective-permute-start(bf16[512,512]{1,0:T(8,128)(2,1)} %get-tuple-element.206.refs_1_), channel_id=1, source_target_pairs={{16,0},{20,4},{24,8},{28,12},{17,1},{21,5},{25,9},{29,13},{18,2},{... | collective-permute-start | bytes 1572872 | tf_op jit(solution)/shard_map/ppermute | solution.py:697
  345.8 41.7 %collective-permute-start.50 = (bf16[512,512]{1,0:T(8,128)(2,1)}, bf16[512,512]{1,0:T(8,128)(2,1)S(1)}, u32[]{:S(2)}, u32[]{:S(2)}) collective-permute-start(bf16[512,512]{1,0:T(8,128)(2,1)} %get-tuple-element.207.refs_2_), channel_id=1, source_target_pairs={{16,8},{20,12},{17,9},{21,13},{18,10},{22,14},{19,11},{23,15}} | collective-permute-start | bytes 1572872 | tf_op jit(solution)/shard_map/ppermute | solution.py:697
  403.2 21.7 %collective-permute-start.51 = (bf16[64,2048]{1,0:T(8,128)(2,1)}, bf16[64,2048]{1,0:T(8,128)(2,1)S(1)}, u32[]{:S(2)}, u32[]{:S(2)}) collective-permute-start(bf16[64,2048]{1,0:T(8,128)(2,1)} %get-tuple-element.213), channel_id=1, source_target_pairs={{0,1},{1,2},{2,3},{3,0},{4,5},{5,6},{6,7},{7,4},{8,9},{9,10},{10,1... | collective-permute-start | bytes 786440 | tf_op jit(solution)/shard_map/ppermute | solution.py:680
  417.9 11.7 %collective-permute-start.52 = (bf16[64,2048]{1,0:T(8,128)(2,1)}, bf16[64,2048]{1,0:T(8,128)(2,1)S(1)}, u32[]{:S(2)}, u32[]{:S(2)}) collective-permute-start(bf16[64,2048]{1,0:T(8,128)(2,1)} %get-tuple-element.214), channel_id=1, source_target_pairs={{0,1},{1,2},{2,3},{3,0},{4,5},{5,6},{6,7},{7,4},{8,9},{9,10},{10,1... | collective-permute-start | bytes 786440 | tf_op jit(solution)/shard_map/ppermute | solution.py:680
  431.4 8.5 %collective-permute-start.54 = (bf16[64,2048]{1,0:T(8,128)(2,1)S(1)}, bf16[64,2048]{1,0:T(8,128)(2,1)S(1)}, u32[]{:S(2)}, u32[]{:S(2)}) collective-permute-start(bf16[64,2048]{1,0:T(8,128)(2,1)S(1)} %add_convert_fusion.2), channel_id=1, source_target_pairs={{0,1},{1,2},{2,3},{3,0},{4,5},{5,6},{6,7},{7,4},{8,9},{9,10},{10,1... | collective-permute-start | bytes 786440 | tf_op jit(solution)/shard_map/ppermute | solution.py:680
  434.9 8.5 %collective-permute-start.53 = (bf16[64,2048]{1,0:T(8,128)(2,1)S(1)}, bf16[64,2048]{1,0:T(8,128)(2,1)S(1)}, u32[]{:S(2)}, u32[]{:S(2)}) collective-permute-start(bf16[64,2048]{1,0:T(8,128)(2,1)S(1)} %add_convert_fusion.3), channel_id=1, source_target_pairs={{0,1},{1,2},{2,3},{3,0},{4,5},{5,6},{6,7},{7,4},{8,9},{9,10},{10,1... | collective-permute-start | bytes 786440 | tf_op jit(solution)/shard_map/ppermute | solution.py:680
  435.6 4.4 collective-permute-start.55
  443.4 13.9 %collective-permute-start.57 = (bf16[64,2048]{1,0:T(8,128)(2,1)S(1)}, bf16[64,2048]{1,0:T(8,128)(2,1)S(1)}, u32[]{:S(2)}, u32[]{:S(2)}) collective-permute-start(bf16[64,2048]{1,0:T(8,128)(2,1)S(1)} %add_convert_fusion), channel_id=1, source_target_pairs={{0,1},{1,2},{2,3},{3,0},{4,5},{5,6},{6,7},{7,4},{8,9},{9,10},{10,1... | collective-permute-start | bytes 786440 | tf_op jit(solution)/shard_map/ppermute | solution.py:680
  443.6 13.7 %collective-permute-start.56 = (bf16[64,2048]{1,0:T(8,128)(2,1)S(1)}, bf16[64,2048]{1,0:T(8,128)(2,1)S(1)}, u32[]{:S(2)}, u32[]{:S(2)}) collective-permute-start(bf16[64,2048]{1,0:T(8,128)(2,1)S(1)} %add_convert_fusion.1), channel_id=1, source_target_pairs={{0,1},{1,2},{2,3},{3,0},{4,5},{5,6},{6,7},{7,4},{8,9},{9,10},{10,1... | collective-permute-start | bytes 786440 | tf_op jit(solution)/shard_map/ppermute | solution.py:680
  443.7 11.2 %collective-permute-start.60 = (f32[34,128]{1,0:T(8,128)S(1)}, f32[34,128]{1,0:T(8,128)S(1)}, u32[]{:S(2)}, u32[]{:S(2)}) collective-permute-start(f32[34,128]{1,0:T(8,128)S(1)} %fusion.7), channel_id=1, source_target_pairs={{0,24},{4,28},{8,16},{12,20},{16,8},{20,12},{24,0},{28,4},{1,25},{... | collective-permute-start | bytes 52232 | tf_op jit(solution)/shard_map/ppermute | solution.py:683
  447.6 8.1 %collective-permute-start.59 = (f32[34,128]{1,0:T(8,128)S(1)}, f32[34,128]{1,0:T(8,128)S(1)}, u32[]{:S(2)}, u32[]{:S(2)}) collective-permute-start(f32[34,128]{1,0:T(8,128)S(1)} %fusion.7), channel_id=1, source_target_pairs={{0,16},{4,20},{8,24},{12,28},{16,0},{20,4},{24,8},{28,12},{1,17},{... | collective-permute-start | bytes 52232 | tf_op jit(solution)/shard_map/ppermute | solution.py:683
  457.4 12.7 %collective-permute-start.63 = (f32[34,128]{1,0:T(8,128)S(1)}, f32[34,128]{1,0:T(8,128)S(1)}, u32[]{:S(2)}, u32[]{:S(2)}) collective-permute-start(f32[34,128]{1,0:T(8,128)S(1)} %add_add_fusion.1), channel_id=1, source_target_pairs={{0,3},{1,0},{2,1},{3,2},{4,7},{5,4},{6,5},{7,6},{8,11},{9,8},{10,9... | collective-permute-start | bytes 52232 | tf_op jit(solution)/shard_map/ppermute | solution.py:934
  461.2 8.9 %collective-permute-start.62 = (f32[34,128]{1,0:T(8,128)S(1)}, f32[34,128]{1,0:T(8,128)S(1)}, u32[]{:S(2)}, u32[]{:S(2)}) collective-permute-start(f32[34,128]{1,0:T(8,128)S(1)} %add_add_fusion.1), channel_id=1, source_target_pairs={{0,2},{1,3},{2,0},{3,1},{4,6},{5,7},{6,4},{7,5},{8,10},{9,11},{10,... | collective-permute-start | bytes 52232 | tf_op jit(solution)/shard_map/ppermute | solution.py:934
  461.7 8.4 %collective-permute-start.61 = (f32[34,128]{1,0:T(8,128)S(1)}, f32[34,128]{1,0:T(8,128)S(1)}, u32[]{:S(2)}, u32[]{:S(2)}) collective-permute-start(f32[34,128]{1,0:T(8,128)S(1)} %add_add_fusion.1), channel_id=1, source_target_pairs={{0,1},{1,2},{2,3},{3,0},{4,5},{5,6},{6,7},{7,4},{8,9},{9,10},{10,1... | collective-permute-start | bytes 52232 | tf_op jit(solution)/shard_map/ppermute | solution.py:934
  (68 other events, 918.1 us)
Sparse Core Ops, SparseCore 0:
  10.7 48.2 all-gather.4
  60.8 118.9 all-gather.2
  247.1 141.9 reduce-scatter.2
  396.7 79.1 reduce-scatter.4

commit v2 on v1

--- a/solution.py
+++ b/solution.py
@@ -327,7 +327,7 @@
     rows, q_cols = dq.shape
     slots = len(hidden_slots)
     tok, width = hidden_slots[0].shape
-    tile = min(512, width)
+    tile = min(1024, width)
     slot_spec = pl.BlockSpec((tok, tile), lambda t: (0, t))
     return pl.pallas_call(
         ignoring(functools.partial(attn_back_kernel, slots=slots), 4 + slots, len(after)),
@@ -564,7 +564,7 @@
 
 def slot_product(x, x_block, w, w_block, depth, slots, after, name):
     rows, width = x.shape[0], w.shape[0]
-    tile = min(512, width)
+    tile = min(1024, width)
     out_spec = pl.BlockSpec((rows // slots, tile), lambda t: (0, t))
     return pl.pallas_call(
         ignoring(slot_product_kernel, 2, len(after)),

time: 490 us -> 491 us (level)
  starting transfers between devices: 77.7 us -> 61.2 us
  waiting for transfers between devices: 215 us -> 228 us
    ppermute x42, starting transfers between devices: 47.9 us -> 27.6 us  [shift(): return lax.ppermute(values, 'mp', ring)]
    ppermute x42, waiting for transfers between devices: 163 us -> 177 us  [shift(): return lax.ppermute(values, 'mp', ring)]
  transfers between devices with their start and end apart: 68 -> 68, of which waited for: 39 -> 41; matrix products, arithmetic and copies ran while one was open for 3% -> 3% of each run, Pallas kernels for 26% -> 26%
where the time goes in v2:
time: 491 us; the launch traced here: 481 us
  waiting for transfers between devices  228 us (46%)
  Pallas kernels  150 us (31%)
  starting transfers between devices  61.2 us (12%)
  between operations  15.1 us (3%)
  local copies, waits for them, and re-layouts  13.8 us (3%)
  other arithmetic  13.1 us (3%)
    ppermute x42, waiting for transfers between devices, shift(): return lax.ppermute(values, 'mp', ring)  177 us
    pallas_call x2, Pallas kernels, feed_forward(): pl.pallas_call(functools.partial(ffn_kernel, parts=parts, held=len(held))...  32.8 us
    ppermute x42, starting transfers between devices, shift(): return lax.ppermute(values, 'mp', ring)  27.6 us
    pallas_call x7, Pallas kernels, simple_call(): pl.pallas_call(ignoring(kernel, len(arrays), len(after)), in_specs=[vmem]...  20.7 us
    ppermute x3, waiting for transfers between devices, body(): lax.ppermute(result_parts[slot], 'mp', [(i, (i - slot) % mp_count) for i...  20.1 us
    pallas_call x1, Pallas kernels, weight_grads(): pl.pallas_call(ignoring(functools.partial(weight_grads_kernel, turns=[at...  17.2 us
    ppermute x10, starting transfers between devices, swap(): return lax.ppermute(values, 'dp', [(i, i ^ mask) for i in range(dp_count)])  15.3 us
    pallas_call x3, Pallas kernels, more_grads(): pl.pallas_call(ignoring(functools.partial(more_grads_kernel, rights=len(r...  13.1 us
  transfers between devices with their start and end apart: 68, of which 41 were waited for; matrix products, arithmetic and copies ran while one was open for 3% of the time, Pallas kernels for 26%

profile of v2, /device:TPU:0, one launch (start us, length us, event | category | flops | bytes accessed | tf_op | source)
XLA Modules:
  0.0 481.3 jit_solution(756247444855320866)
XLA Ops:
  13.6 3.1 collective-permute-start.1
  21.6 4.2 collective-permute-done.1.refs_3_.refs_7_
  25.8 4.8 collective-permute-done.refs_2_.refs_6_
  32.0 9.7 %collective-permute-done.2.refs_4_.refs_8_ = bf16[64,2048]{1,0:T(8,128)(2,1)S(1)} collective-permute-done((bf16[64,2048]{1,0:T(8,128)(2,1)S(1)}, bf16[64,2048]{1,0:T(8,128)(2,1)S(1)}, u32[]{:S(2)}, u32[]{:S(2)}) %collective-permute-start.2) | collective-permute-done | bytes 262176 | tf_op jit(solution)/shard_map/ppermute | solution.py:680
  41.7 5.6 %collective-permute-done.3.refs_5_.refs_9_ = bf16[64,2048]{1,0:T(8,128)(2,1)S(1)} collective-permute-done((bf16[64,2048]{1,0:T(8,128)(2,1)S(1)}, bf16[64,2048]{1,0:T(8,128)(2,1)S(1)}, u32[]{:S(2)}, u32[]{:S(2)}) %collective-permute-start.3) | collective-permute-done | bytes 262176 | tf_op jit(solution)/shard_map/ppermute | solution.py:680
  47.9 5.0 %collective-permute-done.4.refs_6_.refs_10_ = bf16[64,2048]{1,0:T(8,128)(2,1)S(1)} collective-permute-done((bf16[64,2048]{1,0:T(8,128)(2,1)S(1)}, bf16[64,2048]{1,0:T(8,128)(2,1)S(1)}, u32[]{:S(2)}, u32[]{:S(2)}) %collective-permute-start.4) | collective-permute-done | bytes 262176 | tf_op jit(solution)/shard_map/ppermute | solution.py:680
  52.9 3.9 collective-permute-done.5.refs_7_.refs_11_
  59.0 6.5 %project_kv.1 = (bf16[512,2048]{1,0:T(8,128)(2,1)}, f32[512,128]{1,0:T(8,128)}, f32[512,256]{1,0:T(8,128)}, bf16[512,512]{1,0:T(8,128)(2,1)}) custom-call(bf16[2048,1536]{1,0:T(8,128)(2,1)} %all-gather.5.cloned.1.call-done.w_ref.refs_1_.refs_0_.refs_2_, f32[512,128]{1,0:T(8,128)} %pad_maximum_fusion.2.cos_ref.refs_2_.refs_1_, ...), custom_call_target="tpu_custom_call" | custom-call | flops 1048576 | bytes 65536 | tf_op jit(solution)/shard_map/project_kv/pallas_call | solution.py:226
  66.2 3.8 collective-permute-start.9
  70.0 3.4 collective-permute-start.8
  73.5 5.9 %project_q.1 = (f32[512,512]{1,0:T(8,128)}, bf16[512,512]{1,0:T(8,128)(2,1)}) custom-call(bf16[512,2048]{1,0:T(8,128)(2,1)} %get-tuple-element.138.refs_0_, bf16[2048,1536]{1,0:T(8,128)(2,1)} %all-gather.5.cloned.1.call-done.w_ref.refs_1_.refs_0_.refs_2_, f32[512,128]{1,0:T(8,128)} %pad_maximum_fusion.2.cos_ref.refs_2_.refs_1_, ...), custom_call_target="tpu_custom_call" | custom-call | flops 1048576 | bytes 65536 | tf_op jit(solution)/shard_map/project_q/pallas_call | solution.py:258
  80.8 3.5 collective-permute-start.12
  84.3 6.3 %collective-permute-done.11.refs_4_ = bf16[64,2048]{1,0:T(8,128)(2,1)S(1)} collective-permute-done((bf16[64,2048]{1,0:T(8,128)(2,1)}, bf16[64,2048]{1,0:T(8,128)(2,1)S(1)}, u32[]{:S(2)}, u32[]{:S(2)}) %collective-permute-start.11) | collective-permute-done | bytes 262176 | tf_op jit(solution)/shard_map/ppermute | solution.py:680
  90.6 4.3 collective-permute-done.12.refs_5_
  95.0 8.9 %collective-permute-done.9.refs_2_ = bf16[512,512]{1,0:T(8,128)(2,1)S(1)} collective-permute-done((bf16[512,512]{1,0:T(8,128)(2,1)}, bf16[512,512]{1,0:T(8,128)(2,1)S(1)}, u32[]{:S(2)}, u32[]{:S(2)}) %collective-permute-start.9) | collective-permute-done | bytes 524320 | tf_op jit(solution)/shard_map/ppermute | solution.py:693
  108.7 7.8 %attn_fwd.1 = (bf16[512,512]{1,0:T(8,128)(2,1)}, f32[2,1,1024]{2,1,0:T(1,128)}) custom-call(s32[8]{0:T(128)} %convert_select_fusion.1.refs_5_.flags_ref, s32[32]{0:T(128)} %add.167.refs_6_.base_ref, s32[1024,2]{1,0:T(8,128)} %copy.56.refs_7_.places_ref, bf16[512,512]{1,0:T(8,128)(2,1)} %get-tuple-element.140.q_ref, ...), custom_call_target="tpu_custom_call" | custom-call | flops 1048576 | bytes 65536 | tf_op jit(solution)/shard_map/attn_fwd/pallas_call | solution.py:807
  116.6 4.0 collective-permute-done.18.refs_7_
  120.6 3.9 attn_out.1
  126.0 9.7 %collective-permute-done.19 = bf16[64,2048]{1,0:T(8,128)(2,1)S(1)} collective-permute-done((bf16[64,2048]{1,0:T(8,128)(2,1)}, bf16[64,2048]{1,0:T(8,128)(2,1)S(1)}, u32[]{:S(2)}, u32[]{:S(2)}) %collective-permute-start.19) | collective-permute-done | bytes 262176 | tf_op jit(solution)/shard_map/ppermute | solution.py:680
  136.8 4.5 collective-permute-done.22
  142.4 4.5 collective-permute-done.20
  148.0 5.4 %collective-permute-done.23 = bf16[64,2048]{1,0:T(8,128)(2,1)S(1)} collective-permute-done((bf16[64,2048]{1,0:T(8,128)(2,1)S(1)}, bf16[64,2048]{1,0:T(8,128)(2,1)S(1)}, u32[]{:S(2)}, u32[]{:S(2)}) %collective-permute-start.23) | collective-permute-done | bytes 262176 | tf_op jit(solution)/shard_map/ppermute | solution.py:680
  153.8 5.3 %collective-permute-done.21.refs_0_ = bf16[64,2048]{1,0:T(8,128)(2,1)S(1)} collective-permute-done((bf16[64,2048]{1,0:T(8,128)(2,1)S(1)}, bf16[64,2048]{1,0:T(8,128)(2,1)S(1)}, u32[]{:S(2)}, u32[]{:S(2)}) %collective-permute-start.21) | collective-permute-done | bytes 262176 | tf_op jit(solution)/shard_map/ppermute | solution.py:680
  159.1 3.4 collective-permute-done.24.refs_1_
  166.1 11.0 %collective-permute-done.25.refs_2_ = bf16[64,2048]{1,0:T(8,128)(2,1)S(1)} collective-permute-done((bf16[64,2048]{1,0:T(8,128)(2,1)}, bf16[64,2048]{1,0:T(8,128)(2,1)S(1)}, u32[]{:S(2)}, u32[]{:S(2)}) %collective-permute-start.25) | collective-permute-done | bytes 262176 | tf_op jit(solution)/shard_map/ppermute | solution.py:680
  177.2 5.6 %collective-permute-done.26.refs_3_ = bf16[64,2048]{1,0:T(8,128)(2,1)S(1)} collective-permute-done((bf16[64,2048]{1,0:T(8,128)(2,1)}, bf16[64,2048]{1,0:T(8,128)(2,1)S(1)}, u32[]{:S(2)}, u32[]{:S(2)}) %collective-permute-start.26) | collective-permute-done | bytes 262176 | tf_op jit(solution)/shard_map/ppermute | solution.py:680
  183.5 16.4 %feed_forward.2 = (bf16[512,4608]{1,0:T(8,128)(2,1)}, bf16[512,2048]{1,0:T(8,128)(2,1)}, bf16[512,2048]{1,0:T(8,128)(2,1)}, bf16[64,2048]{1,0:T(8,128)(2,1)}, bf...) custom-call(bf16[2048,4608]{1,0:T(8,128)(2,1)} %all-gather.3.cloned.1.call-done.gate_ref.up_ref.down_ref.r, ...), custom_call_target="tpu_custom_call" | custom-call | flops 1048576 | bytes 65536 | tf_op jit(solution)/shard_map/feed_forward/pallas_call | solution.py:503
  200.1 9.3 %collective-permute-done.29.refs_2_ = bf16[64,2048]{1,0:T(8,128)(2,1)S(1)} collective-permute-done((bf16[64,2048]{1,0:T(8,128)(2,1)S(1)}, bf16[64,2048]{1,0:T(8,128)(2,1)S(1)}, u32[]{:S(2)}, u32[]{:S(2)}) %collective-permute-start.29) | collective-permute-done | bytes 262176 | tf_op jit(solution)/shard_map/ppermute | solution.py:680
  213.3 16.4 %feed_forward.3 = (bf16[512,4608]{1,0:T(8,128)(2,1)}, bf16[512,2048]{1,0:T(8,128)(2,1)}, bf16[512,2048]{1,0:T(8,128)(2,1)}, bf16[64,2048]{1,0:T(8,128)(2,1)}, bf...) custom-call(bf16[2048,4608]{1,0:T(8,128)(2,1)} %all-gather.3.cloned., ...), custom_call_target="tpu_custom_call", output_to_operand_aliasing={{0}: (11, {}), {1}: (12, {}), {2}: (13, {})} | custom-call | flops 1048576 | bytes 65536 | tf_op jit(solution)/shard_map/feed_forward/pallas_call | solution.py:503
  229.7 17.2 %ffn_grads.1 = bf16[2048,4608]{1,0:T(8,128)(2,1)} custom-call(bf16[512,2048]{1,0:T(8,128)(2,1)} %get-tuple-element.179.refs_0_, bf16[512,2048]{1,0:T(8,128)(2,1)} %get-tuple-element.180.refs_1_, bf16[512,4608]{1,0:T(8,128)(2,1)} %get-tuple-element.182.refs_2_.refs_0_), custom_call_target="tpu_custom_call" | custom-call | flops 1048576 | bytes 65536 | tf_op jit(solution)/shard_map/ffn_grads/pallas_call | solution.py:546
  251.9 6.9 %collective-permute-done.32 = bf16[64,2048]{1,0:T(8,128)(2,1)S(1)} collective-permute-done((bf16[64,2048]{1,0:T(8,128)(2,1)S(1)}, bf16[64,2048]{1,0:T(8,128)(2,1)S(1)}, u32[]{:S(2)}, u32[]{:S(2)}) %collective-permute-start.32) | collective-permute-done | bytes 262176 | tf_op jit(solution)/shard_map/ppermute | solution.py:680
  258.8 2.8 collective-permute-done.34
  263.2 8.4 %collective-permute-done.36.refs_1_ = bf16[64,2048]{1,0:T(8,128)(2,1)S(1)} collective-permute-done((bf16[64,2048]{1,0:T(8,128)(2,1)S(1)}, bf16[64,2048]{1,0:T(8,128)(2,1)S(1)}, u32[]{:S(2)}, u32[]{:S(2)}) %collective-permute-start.36) | collective-permute-done | bytes 262176 | tf_op jit(solution)/shard_map/ppermute | solution.py:680
  271.6 2.8 collective-permute-done.35.refs_0_
  275.1 4.3 mid.1
  279.6 8.0 %ffn_out.1 = (bf16[128,2048]{1,0:T(8,128)(2,1)}, bf16[128,2048]{1,0:T(8,128)(2,1)}, bf16[128,2048]{1,0:T(8,128)(2,1)}, bf16[128,2048]{1,0:T(8,128)(2,1)}) custom-call(bf16[512,4608]{1,0:T(8,128)(2,1)} %get-tuple-element.182.refs_2_.refs_0_, bf16[2048,4608]{1,0:T(8,128)(2,1)} %all-gather.3.cloned.1.call-done.gate_ref.up_ref.down_ref.refs_1_), custom_call_target="tpu_custom_call" | custom-call | flops 1048576 | bytes 65536 | tf_op jit(solution)/shard_map/ffn_out/pallas_call | solution.py:569
  288.8 5.6 %collective-permute-done.41.refs_3_ = bf16[64,2048]{1,0:T(8,128)(2,1)S(1)} collective-permute-done((bf16[64,2048]{1,0:T(8,128)(2,1)}, bf16[64,2048]{1,0:T(8,128)(2,1)S(1)}, u32[]{:S(2)}, u32[]{:S(2)}) %collective-permute-start.41) | collective-permute-done | bytes 262176 | tf_op jit(solution)/shard_map/ppermute | solution.py:680
  294.5 5.6 %collective-permute-done.43.refs_6_ = bf16[64,2048]{1,0:T(8,128)(2,1)S(1)} collective-permute-done((bf16[64,2048]{1,0:T(8,128)(2,1)S(1)}, bf16[64,2048]{1,0:T(8,128)(2,1)S(1)}, u32[]{:S(2)}, u32[]{:S(2)}) %collective-permute-start.43) | collective-permute-done | bytes 262176 | tf_op jit(solution)/shard_map/ppermute | solution.py:680
  300.1 5.6 %collective-permute-done.42.refs_5_ = bf16[64,2048]{1,0:T(8,128)(2,1)S(1)} collective-permute-done((bf16[64,2048]{1,0:T(8,128)(2,1)S(1)}, bf16[64,2048]{1,0:T(8,128)(2,1)S(1)}, u32[]{:S(2)}, u32[]{:S(2)}) %collective-permute-start.42) | collective-permute-done | bytes 262176 | tf_op jit(solution)/shard_map/ppermute | solution.py:680
  305.7 5.3 %collective-permute-done.45.refs_8_ = bf16[64,2048]{1,0:T(8,128)(2,1)S(1)} collective-permute-done((bf16[64,2048]{1,0:T(8,128)(2,1)S(1)}, bf16[64,2048]{1,0:T(8,128)(2,1)S(1)}, u32[]{:S(2)}, u32[]{:S(2)}) %collective-permute-start.45) | collective-permute-done | bytes 262176 | tf_op jit(solution)/shard_map/ppermute | solution.py:680
  311.0 2.9 collective-permute-done.44.refs_7_
  314.6 5.1 %grad_attended.1 = (bf16[512,2048]{1,0:T(8,128)(2,1)}, bf16[512,512]{1,0:T(8,128)(2,1)}) custom-call(bf16[2048,1536]{1,0:T(8,128)(2,1)} %all-gather.5.cloned.1.call-done.w_ref.refs_1_.refs_0_.refs_2_, bf16[64,2048]{1,0:T(8,128)(2,1)} %get-tuple-element.199.refs_1_, bf16[64,2048]{1,0:T(8,128)(2,1)} %get-tuple-element.188.refs_2_, ...), custom_call_target="tpu_custom_call" | custom-call | flops 1048576 | bytes 65536 | tf_op jit(solution)/shard_map/grad_attended/pallas_call | solution.py:365
  319.6 12.0 %attn_bwd.1 = (f32[512,512]{1,0:T(8,128)}, bf16[2048,512]{1,0:T(8,128)(2,1)}, bf16[2048,512]{1,0:T(8,128)(2,1)}) custom-call(s32[8]{0:T(128)} %convert_select_fusion.1.refs_5_.flags_ref, s32[32]{0:T(128)} %add.167.refs_6_.base_ref, s32[2,1024]{1,0:T(2,128)} %copy-done.56, bf16[512,512]{1,0:T(8,128)(2,1)} %get-tuple-element.140.q_ref, ...), custom_call_target="tpu_custom_call" | custom-call | flops 1048576 | bytes 65536 | tf_op jit(solution)/shard_map/attn_bwd/pallas_call | solution.py:881
  331.9 4.2 collective-permute-done.46.refs_1_.refs_5_
  337.4 3.5 fold_blocks.1
  348.3 4.4 out_grads.1.refs_2_
  352.8 3.6 unproject_q.1
  356.3 4.3 q_grads.1.refs_9_.refs_2_
  360.6 17.4 %collective-permute-done.39.refs_2_.refs_11_ = bf16[128,2048]{1,0:T(8,128)(2,1)S(1)} collective-permute-done((bf16[128,2048]{1,0:T(8,128)(2,1)}, bf16[128,2048]{1,0:T(8,128)(2,1)S(1)}, u32[]{:S(2)}, u32[]{:S(2)}) %collective-permute-start.39) | collective-permute-done | bytes 524320 | tf_op jit(solution)/shard_map/ppermute | solution.py:874
  378.1 9.8 %collective-permute-done.49.refs_7_ = bf16[512,512]{1,0:T(8,128)(2,1)S(1)} collective-permute-done((bf16[512,512]{1,0:T(8,128)(2,1)}, bf16[512,512]{1,0:T(8,128)(2,1)S(1)}, u32[]{:S(2)}, u32[]{:S(2)}) %collective-permute-start.49) | collective-permute-done | bytes 524320 | tf_op jit(solution)/shard_map/ppermute | solution.py:697
  388.8 3.7 unproject_kv.1
  392.5 4.4 kv_grads.1.refs_12_
  396.9 6.1 %attn_back.1 = (bf16[64,2048]{1,0:T(8,128)(2,1)}, bf16[64,2048]{1,0:T(8,128)(2,1)}, bf16[64,2048]{1,0:T(8,128)(2,1)}, bf16[64,2048]{1,0:T(8,128)(2,1)}, bf16[64,...) custom-call(bf16[512,512]{1,0:T(8,128)(2,1)} %get-tuple-element.208., ...), custom_call_target="tpu_custom_call" | custom-call | flops 1048576 | bytes 65536 | tf_op jit(solution)/shard_map/attn_back/pallas_call | solution.py:332
  406.0 8.3 %collective-permute-done.51 = bf16[64,2048]{1,0:T(8,128)(2,1)S(1)} collective-permute-done((bf16[64,2048]{1,0:T(8,128)(2,1)}, bf16[64,2048]{1,0:T(8,128)(2,1)S(1)}, u32[]{:S(2)}, u32[]{:S(2)}) %collective-permute-start.51) | collective-permute-done | bytes 262176 | tf_op jit(solution)/shard_map/ppermute | solution.py:680
  414.3 4.4 collective-permute-done.52
  423.0 4.3 split_ffn.1
  427.4 4.4 collective-permute-done.54
  431.7 3.5 collective-permute-done.53
  435.5 10.0 %collective-permute-start.60 = (f32[34,128]{1,0:T(8,128)S(1)}, f32[34,128]{1,0:T(8,128)S(1)}, u32[]{:S(2)}, u32[]{:S(2)}) collective-permute-start(f32[34,128]{1,0:T(8,128)S(1)} %fusion.7), channel_id=1, source_target_pairs={{0,24},{4,28},{8,16},{12,20},{16,8},{20,12},{24,0},{28,4},{1,25},{... | collective-permute-start | bytes 52232 | tf_op jit(solution)/shard_map/ppermute | solution.py:683
  445.5 4.2 collective-permute-start.59
  453.5 3.9 collective-permute-start.63
  459.8 3.1 result.1
  462.9 3.3 last.1
  467.4 4.6 reduce-scatter.5.cloned.1.call-done.refs_0_
  (279 shorter events, 72.7 us)
Async XLA Ops:
  7.2 51.7 %all-gather.5.cloned.1.call-start = ((), (), s32[]{:S(2)}) async-start(), calls=%async_computation.3 | async-start | bytes 7077888 | tf_op jit(solution)/shard_map/all_gather | solution.py:733
  10.5 172.2 %all-gather.3.cloned.1.call-start = ((), (), s32[]{:S(2)}) async-start(), calls=%async_computation.2 | async-start | bytes 21233664 | tf_op jit(solution)/shard_map/all_gather | solution.py:734
  12.5 380.0 %reduce-scatter.3.cloned.1.call-start = ((), (), s32[]{:S(2)}) async-start(), calls=%async_computation.4 | async-start | bytes 21233664 | tf_op jit(solution)/shard_map/reduce_scatter | solution.py:858
  13.6 12.2 %collective-permute-start.1 = (bf16[64,2048]{1,0:T(8,128)(2,1)S(1)}, bf16[64,2048]{1,0:T(8,128)(2,1)S(1)}, u32[]{:S(2)}, u32[]{:S(2)}) collective-permute-start(bf16[64,2048]{1,0:T(8,128)(2,1)S(1)} %get-tuple-element.255.refs_1_.refs_5_), channel_id=1, source_target_pairs={{0,1},{1,2},{2,3},{3,0},{4,5},{5,6},{6,7},{7,4},{8,9},{9,10},{10,1... | collective-permute-start | bytes 786440 | tf_op jit(solution)/shard_map/ppermute | solution.py:680
  16.7 13.9 %collective-permute-start = (bf16[64,2048]{1,0:T(8,128)(2,1)S(1)}, bf16[64,2048]{1,0:T(8,128)(2,1)S(1)}, u32[]{:S(2)}, u32[]{:S(2)}) collective-permute-start(bf16[64,2048]{1,0:T(8,128)(2,1)S(1)} %get-tuple-element.256.refs_0_.refs_4_), channel_id=1, source_target_pairs={{0,1},{1,2},{2,3},{3,0},{4,5},{5,6},{6,7},{7,4},{8,9},{9,10},{10,1... | collective-permute-start | bytes 786440 | tf_op jit(solution)/shard_map/ppermute | solution.py:680
  30.6 11.0 %collective-permute-start.2 = (bf16[64,2048]{1,0:T(8,128)(2,1)S(1)}, bf16[64,2048]{1,0:T(8,128)(2,1)S(1)}, u32[]{:S(2)}, u32[]{:S(2)}) collective-permute-start(bf16[64,2048]{1,0:T(8,128)(2,1)S(1)} %collective-permute-done.refs_2_.refs_6_), channel_id=1, source_target_pairs={{0,1},{1,2},{2,3},{3,0},{4,5},{5,6},{6,7},{7,4},{8,9},{9,10},{10,1... | collective-permute-start | bytes 786440 | tf_op jit(solution)/shard_map/ppermute | solution.py:680
  30.6 16.7 %collective-permute-start.3 = (bf16[64,2048]{1,0:T(8,128)(2,1)S(1)}, bf16[64,2048]{1,0:T(8,128)(2,1)S(1)}, u32[]{:S(2)}, u32[]{:S(2)}) collective-permute-start(bf16[64,2048]{1,0:T(8,128)(2,1)S(1)} %collective-permute-done.1.refs_3_.refs_7_), channel_id=1, source_target_pairs={{0,1},{1,2},{2,3},{3,0},{4,5},{5,6},{6,7},{7,4},{8,9},{9,10},{10,1... | collective-permute-start | bytes 786440 | tf_op jit(solution)/shard_map/ppermute | solution.py:680
  41.7 11.2 %collective-permute-start.4 = (bf16[64,2048]{1,0:T(8,128)(2,1)S(1)}, bf16[64,2048]{1,0:T(8,128)(2,1)S(1)}, u32[]{:S(2)}, u32[]{:S(2)}) collective-permute-start(bf16[64,2048]{1,0:T(8,128)(2,1)S(1)} %collective-permute-done.2.refs_4_.refs_8_), channel_id=1, source_target_pairs={{0,1},{1,2},{2,3},{3,0},{4,5},{5,6},{6,7},{7,4},{8,9},{9,10},{10,1... | collective-permute-start | bytes 786440 | tf_op jit(solution)/shard_map/ppermute | solution.py:680
  47.3 9.5 %collective-permute-start.5 = (bf16[64,2048]{1,0:T(8,128)(2,1)S(1)}, bf16[64,2048]{1,0:T(8,128)(2,1)S(1)}, u32[]{:S(2)}, u32[]{:S(2)}) collective-permute-start(bf16[64,2048]{1,0:T(8,128)(2,1)S(1)} %collective-permute-done.3.refs_5_.refs_9_), channel_id=1, source_target_pairs={{0,1},{1,2},{2,3},{3,0},{4,5},{5,6},{6,7},{7,4},{8,9},{9,10},{10,1... | collective-permute-start | bytes 786440 | tf_op jit(solution)/shard_map/ppermute | solution.py:680
  56.8 16.7 %collective-permute-start.6 = (bf16[64,2048]{1,0:T(8,128)(2,1)S(1)}, bf16[64,2048]{1,0:T(8,128)(2,1)}, u32[]{:S(2)}, u32[]{:S(2)}) collective-permute-start(bf16[64,2048]{1,0:T(8,128)(2,1)S(1)} %get-tuple-element.134.refs_4_), channel_id=1, source_target_pairs={{0,1},{1,2},{2,3},{3,0},{4,5},{5,6},{6,7},{7,4},{8,9},{9,10},{10,1... | collective-permute-start | bytes 786440 | tf_op jit(solution)/shard_map/ppermute | solution.py:680
  56.8 16.7 %collective-permute-start.7 = (bf16[64,2048]{1,0:T(8,128)(2,1)S(1)}, bf16[64,2048]{1,0:T(8,128)(2,1)}, u32[]{:S(2)}, u32[]{:S(2)}) collective-permute-start(bf16[64,2048]{1,0:T(8,128)(2,1)S(1)} %get-tuple-element.135.refs_5_), channel_id=1, source_target_pairs={{0,1},{1,2},{2,3},{3,0},{4,5},{5,6},{6,7},{7,4},{8,9},{9,10},{10,1... | collective-permute-start | bytes 786440 | tf_op jit(solution)/shard_map/ppermute | solution.py:680
  65.5 29.5 %collective-permute-start.10 = (bf16[512,512]{1,0:T(8,128)(2,1)}, bf16[512,512]{1,0:T(8,128)(2,1)S(1)}, u32[]{:S(2)}, u32[]{:S(2)}) collective-permute-start(bf16[512,512]{1,0:T(8,128)(2,1)} %get-tuple-element.133.refs_0_), channel_id=1, source_target_pairs={{8,16},{12,20},{9,17},{13,21},{10,18},{14,22},{11,19},{15,23}} | collective-permute-start | bytes 1572872 | tf_op jit(solution)/shard_map/ppermute | solution.py:693
  66.2 37.7 %collective-permute-start.9 = (bf16[512,512]{1,0:T(8,128)(2,1)}, bf16[512,512]{1,0:T(8,128)(2,1)S(1)}, u32[]{:S(2)}, u32[]{:S(2)}) collective-permute-start(bf16[512,512]{1,0:T(8,128)(2,1)} %get-tuple-element.133.refs_0_), channel_id=1, source_target_pairs={{0,16},{4,20},{8,24},{12,28},{1,17},{5,21},{9,25},{13,29},{2,18},{... | collective-permute-start | bytes 1572872 | tf_op jit(solution)/shard_map/ppermute | solution.py:693
  70.0 33.9 %collective-permute-start.8 = (bf16[512,512]{1,0:T(8,128)(2,1)}, bf16[512,512]{1,0:T(8,128)(2,1)S(1)}, u32[]{:S(2)}, u32[]{:S(2)}) collective-permute-start(bf16[512,512]{1,0:T(8,128)(2,1)} %get-tuple-element.133.refs_0_), channel_id=1, source_target_pairs={{0,8},{4,12},{16,24},{20,28},{1,9},{5,13},{17,25},{21,29},{2,10},{... | collective-permute-start | bytes 1572872 | tf_op jit(solution)/shard_map/ppermute | solution.py:693
  79.4 11.3 %collective-permute-start.11 = (bf16[64,2048]{1,0:T(8,128)(2,1)}, bf16[64,2048]{1,0:T(8,128)(2,1)S(1)}, u32[]{:S(2)}, u32[]{:S(2)}) collective-permute-start(bf16[64,2048]{1,0:T(8,128)(2,1)} %collective-permute-done.6.refs_6_), channel_id=1, source_target_pairs={{0,1},{1,2},{2,3},{3,0},{4,5},{5,6},{6,7},{7,4},{8,9},{9,10},{10,1... | collective-permute-start | bytes 786440 | tf_op jit(solution)/shard_map/ppermute | solution.py:680
  80.8 14.2 %collective-permute-start.12 = (bf16[64,2048]{1,0:T(8,128)(2,1)}, bf16[64,2048]{1,0:T(8,128)(2,1)}, u32[]{:S(2)}, u32[]{:S(2)}) collective-permute-start(bf16[64,2048]{1,0:T(8,128)(2,1)} %collective-permute-done.7.refs_7_), channel_id=1, source_target_pairs={{0,1},{1,2},{2,3},{3,0},{4,5},{5,6},{6,7},{7,4},{8,9},{9,10},{10,1... | collective-permute-start | bytes 786440 | tf_op jit(solution)/shard_map/ppermute | solution.py:680
  90.6 15.3 %collective-permute-start.13 = (bf16[512,512]{1,0:T(8,128)(2,1)S(1)}, bf16[512,512]{1,0:T(8,128)(2,1)S(1)}, u32[]{:S(2)}, u32[]{:S(2)}) collective-permute-start(bf16[512,512]{1,0:T(8,128)(2,1)S(1)} %copy-done.8), channel_id=1, source_target_pairs={{0,4},{4,0},{8,12},{12,8},{16,20},{20,16},{24,28},{28,24},{1,5},{5... | collective-permute-start | bytes 1572872 | tf_op jit(solution)/shard_map/ppermute | solution.py:683
  104.5 12.1 %collective-permute-start.17 = (bf16[64,2048]{1,0:T(8,128)(2,1)S(1)}, bf16[64,2048]{1,0:T(8,128)(2,1)}, u32[]{:S(2)}, u32[]{:S(2)}) collective-permute-start(bf16[64,2048]{1,0:T(8,128)(2,1)S(1)} %collective-permute-done.11.refs_4_), channel_id=1, source_target_pairs={{0,1},{1,2},{2,3},{3,0},{4,5},{5,6},{6,7},{7,4},{8,9},{9,10},{10,1... | collective-permute-start | bytes 786440 | tf_op jit(solution)/shard_map/ppermute | solution.py:680
  106.0 14.6 %collective-permute-start.18 = (bf16[64,2048]{1,0:T(8,128)(2,1)}, bf16[64,2048]{1,0:T(8,128)(2,1)S(1)}, u32[]{:S(2)}, u32[]{:S(2)}) collective-permute-start(bf16[64,2048]{1,0:T(8,128)(2,1)} %collective-permute-done.12.refs_5_), channel_id=1, source_target_pairs={{0,1},{1,2},{2,3},{3,0},{4,5},{5,6},{6,7},{7,4},{8,9},{9,10},{10,1... | collective-permute-start | bytes 786440 | tf_op jit(solution)/shard_map/ppermute | solution.py:680
  124.4 11.3 %collective-permute-start.19 = (bf16[64,2048]{1,0:T(8,128)(2,1)}, bf16[64,2048]{1,0:T(8,128)(2,1)S(1)}, u32[]{:S(2)}, u32[]{:S(2)}) collective-permute-start(bf16[64,2048]{1,0:T(8,128)(2,1)} %get-tuple-element.156), channel_id=1, source_target_pairs={{0,1},{1,2},{2,3},{3,0},{4,5},{5,6},{6,7},{7,4},{8,9},{9,10},{10,1... | collective-permute-start | bytes 786440 | tf_op jit(solution)/shard_map/ppermute | solution.py:680
  124.5 16.8 %collective-permute-start.22 = (bf16[64,2048]{1,0:T(8,128)(2,1)}, bf16[64,2048]{1,0:T(8,128)(2,1)S(1)}, u32[]{:S(2)}, u32[]{:S(2)}) collective-permute-start(bf16[64,2048]{1,0:T(8,128)(2,1)} %get-tuple-element.159), channel_id=1, source_target_pairs={{0,1},{1,2},{2,3},{3,0},{4,5},{5,6},{6,7},{7,4},{8,9},{9,10},{10,1... | collective-permute-start | bytes 786440 | tf_op jit(solution)/shard_map/ppermute | solution.py:680
  136.7 10.2 %collective-permute-start.20 = (bf16[64,2048]{1,0:T(8,128)(2,1)S(1)}, bf16[64,2048]{1,0:T(8,128)(2,1)S(1)}, u32[]{:S(2)}, u32[]{:S(2)}) collective-permute-start(bf16[64,2048]{1,0:T(8,128)(2,1)S(1)} %add_convert_fusion.11), channel_id=1, source_target_pairs={{0,1},{1,2},{2,3},{3,0},{4,5},{5,6},{6,7},{7,4},{8,9},{9,10},{10,1... | collective-permute-start | bytes 786440 | tf_op jit(solution)/shard_map/ppermute | solution.py:680
  142.4 11.1 %collective-permute-start.23 = (bf16[64,2048]{1,0:T(8,128)(2,1)S(1)}, bf16[64,2048]{1,0:T(8,128)(2,1)S(1)}, u32[]{:S(2)}, u32[]{:S(2)}) collective-permute-start(bf16[64,2048]{1,0:T(8,128)(2,1)S(1)} %add_convert_fusion.9), channel_id=1, source_target_pairs={{0,1},{1,2},{2,3},{3,0},{4,5},{5,6},{6,7},{7,4},{8,9},{9,10},{10,1... | collective-permute-start | bytes 786440 | tf_op jit(solution)/shard_map/ppermute | solution.py:680
  148.0 11.1 %collective-permute-start.21 = (bf16[64,2048]{1,0:T(8,128)(2,1)S(1)}, bf16[64,2048]{1,0:T(8,128)(2,1)S(1)}, u32[]{:S(2)}, u32[]{:S(2)}) collective-permute-start(bf16[64,2048]{1,0:T(8,128)(2,1)S(1)} %add_convert_fusion.10), channel_id=1, source_target_pairs={{0,1},{1,2},{2,3},{3,0},{4,5},{5,6},{6,7},{7,4},{8,9},{9,10},{10,1... | collective-permute-start | bytes 786440 | tf_op jit(solution)/shard_map/ppermute | solution.py:680
  153.5 8.9 %collective-permute-start.24 = (bf16[64,2048]{1,0:T(8,128)(2,1)S(1)}, bf16[64,2048]{1,0:T(8,128)(2,1)S(1)}, u32[]{:S(2)}, u32[]{:S(2)}) collective-permute-start(bf16[64,2048]{1,0:T(8,128)(2,1)S(1)} %add_convert_fusion.8), channel_id=1, source_target_pairs={{0,1},{1,2},{2,3},{3,0},{4,5},{5,6},{6,7},{7,4},{8,9},{9,10},{10,1... | collective-permute-start | bytes 786440 | tf_op jit(solution)/shard_map/ppermute | solution.py:680
  165.9 11.3 %collective-permute-start.25 = (bf16[64,2048]{1,0:T(8,128)(2,1)}, bf16[64,2048]{1,0:T(8,128)(2,1)S(1)}, u32[]{:S(2)}, u32[]{:S(2)}) collective-permute-start(bf16[64,2048]{1,0:T(8,128)(2,1)} %get-tuple-element.164.refs_0_), channel_id=1, source_target_pairs={{0,1},{1,2},{2,3},{3,0},{4,5},{5,6},{6,7},{7,4},{8,9},{9,10},{10,1... | collective-permute-start | bytes 786440 | tf_op jit(solution)/shard_map/ppermute | solution.py:680
  165.9 16.9 %collective-permute-start.26 = (bf16[64,2048]{1,0:T(8,128)(2,1)}, bf16[64,2048]{1,0:T(8,128)(2,1)S(1)}, u32[]{:S(2)}, u32[]{:S(2)}) collective-permute-start(bf16[64,2048]{1,0:T(8,128)(2,1)} %get-tuple-element.165.refs_1_), channel_id=1, source_target_pairs={{0,1},{1,2},{2,3},{3,0},{4,5},{5,6},{6,7},{7,4},{8,9},{9,10},{10,1... | collective-permute-start | bytes 786440 | tf_op jit(solution)/shard_map/ppermute | solution.py:680
  177.2 22.7 %collective-permute-start.27 = (bf16[64,2048]{1,0:T(8,128)(2,1)S(1)}, bf16[64,2048]{1,0:T(8,128)(2,1)S(1)}, u32[]{:S(2)}, u32[]{:S(2)}) collective-permute-start(bf16[64,2048]{1,0:T(8,128)(2,1)S(1)} %collective-permute-done.25.refs_2_), channel_id=1, source_target_pairs={{0,1},{1,2},{2,3},{3,0},{4,5},{5,6},{6,7},{7,4},{8,9},{9,10},{10,1... | collective-permute-start | bytes 786440 | tf_op jit(solution)/shard_map/ppermute | solution.py:680
  182.8 17.1 %collective-permute-start.28 = (bf16[64,2048]{1,0:T(8,128)(2,1)S(1)}, bf16[64,2048]{1,0:T(8,128)(2,1)S(1)}, u32[]{:S(2)}, u32[]{:S(2)}) collective-permute-start(bf16[64,2048]{1,0:T(8,128)(2,1)S(1)} %collective-permute-done.26.refs_3_), channel_id=1, source_target_pairs={{0,1},{1,2},{2,3},{3,0},{4,5},{5,6},{6,7},{7,4},{8,9},{9,10},{10,1... | collective-permute-start | bytes 786440 | tf_op jit(solution)/shard_map/ppermute | solution.py:680
  199.9 9.4 %collective-permute-start.29 = (bf16[64,2048]{1,0:T(8,128)(2,1)S(1)}, bf16[64,2048]{1,0:T(8,128)(2,1)S(1)}, u32[]{:S(2)}, u32[]{:S(2)}) collective-permute-start(bf16[64,2048]{1,0:T(8,128)(2,1)S(1)} %collective-permute-done.27.refs_0_), channel_id=1, source_target_pairs={{0,1},{1,2},{2,3},{3,0},{4,5},{5,6},{6,7},{7,4},{8,9},{9,10},{10,1... | collective-permute-start | bytes 786440 | tf_op jit(solution)/shard_map/ppermute | solution.py:680
  200.0 12.2 %collective-permute-start.30 = (bf16[64,2048]{1,0:T(8,128)(2,1)S(1)}, bf16[64,2048]{1,0:T(8,128)(2,1)S(1)}, u32[]{:S(2)}, u32[]{:S(2)}) collective-permute-start(bf16[64,2048]{1,0:T(8,128)(2,1)S(1)} %collective-permute-done.28.refs_1_), channel_id=1, source_target_pairs={{0,1},{1,2},{2,3},{3,0},{4,5},{5,6},{6,7},{7,4},{8,9},{9,10},{10,1... | collective-permute-start | bytes 786440 | tf_op jit(solution)/shard_map/ppermute | solution.py:680
  212.1 17.6 %collective-permute-start.31 = (bf16[64,2048]{1,0:T(8,128)(2,1)}, bf16[64,2048]{1,0:T(8,128)(2,1)S(1)}, u32[]{:S(2)}, u32[]{:S(2)}) collective-permute-start(bf16[64,2048]{1,0:T(8,128)(2,1)} %get-tuple-element.172), channel_id=1, source_target_pairs={{0,1},{1,2},{2,3},{3,0},{4,5},{5,6},{6,7},{7,4},{8,9},{9,10},{10,1... | collective-permute-start | bytes 786440 | tf_op jit(solution)/shard_map/ppermute | solution.py:680
  212.2 17.6 %collective-permute-start.33 = (bf16[64,2048]{1,0:T(8,128)(2,1)}, bf16[64,2048]{1,0:T(8,128)(2,1)S(1)}, u32[]{:S(2)}, u32[]{:S(2)}) collective-permute-start(bf16[64,2048]{1,0:T(8,128)(2,1)} %get-tuple-element.177), channel_id=1, source_target_pairs={{0,1},{1,2},{2,3},{3,0},{4,5},{5,6},{6,7},{7,4},{8,9},{9,10},{10,1... | collective-permute-start | bytes 786440 | tf_op jit(solution)/shard_map/ppermute | solution.py:680
  247.0 225.0 %reduce-scatter.5.cloned.1.call-start = ((), (), s32[]{:S(2)}) async-start(), calls=%async_computation.5 | async-start | bytes 7077888 | tf_op jit(solution)/shard_map/reduce_scatter | solution.py:915
  248.0 10.8 %collective-permute-start.32 = (bf16[64,2048]{1,0:T(8,128)(2,1)S(1)}, bf16[64,2048]{1,0:T(8,128)(2,1)S(1)}, u32[]{:S(2)}, u32[]{:S(2)}) collective-permute-start(bf16[64,2048]{1,0:T(8,128)(2,1)S(1)} %add_convert_fusion.7), channel_id=1, source_target_pairs={{0,1},{1,2},{2,3},{3,0},{4,5},{5,6},{6,7},{7,4},{8,9},{9,10},{10,1... | collective-permute-start | bytes 786440 | tf_op jit(solution)/shard_map/ppermute | solution.py:680
  249.6 12.0 %collective-permute-start.34 = (bf16[64,2048]{1,0:T(8,128)(2,1)S(1)}, bf16[64,2048]{1,0:T(8,128)(2,1)S(1)}, u32[]{:S(2)}, u32[]{:S(2)}) collective-permute-start(bf16[64,2048]{1,0:T(8,128)(2,1)S(1)} %add_convert_fusion.6), channel_id=1, source_target_pairs={{0,1},{1,2},{2,3},{3,0},{4,5},{5,6},{6,7},{7,4},{8,9},{9,10},{10,1... | collective-permute-start | bytes 786440 | tf_op jit(solution)/shard_map/ppermute | solution.py:680
  261.7 9.9 %collective-permute-start.36 = (bf16[64,2048]{1,0:T(8,128)(2,1)S(1)}, bf16[64,2048]{1,0:T(8,128)(2,1)S(1)}, u32[]{:S(2)}, u32[]{:S(2)}) collective-permute-start(bf16[64,2048]{1,0:T(8,128)(2,1)S(1)} %add_convert_fusion.4), channel_id=1, source_target_pairs={{0,1},{1,2},{2,3},{3,0},{4,5},{5,6},{6,7},{7,4},{8,9},{9,10},{10,1... | collective-permute-start | bytes 786440 | tf_op jit(solution)/shard_map/ppermute | solution.py:680
  261.8 12.6 %collective-permute-start.35 = (bf16[64,2048]{1,0:T(8,128)(2,1)S(1)}, bf16[64,2048]{1,0:T(8,128)(2,1)S(1)}, u32[]{:S(2)}, u32[]{:S(2)}) collective-permute-start(bf16[64,2048]{1,0:T(8,128)(2,1)S(1)} %add_convert_fusion.5), channel_id=1, source_target_pairs={{0,1},{1,2},{2,3},{3,0},{4,5},{5,6},{6,7},{7,4},{8,9},{9,10},{10,1... | collective-permute-start | bytes 786440 | tf_op jit(solution)/shard_map/ppermute | solution.py:680
  279.4 9.4 %collective-permute-start.37 = (bf16[64,2048]{1,0:T(8,128)(2,1)}, bf16[64,2048]{1,0:T(8,128)(2,1)S(1)}, u32[]{:S(2)}, u32[]{:S(2)}) collective-permute-start(bf16[64,2048]{1,0:T(8,128)(2,1)} %get-tuple-element.188.refs_2_), channel_id=1, source_target_pairs={{0,1},{1,2},{2,3},{3,0},{4,5},{5,6},{6,7},{7,4},{8,9},{9,10},{10,1... | collective-permute-start | bytes 786440 | tf_op jit(solution)/shard_map/ppermute | solution.py:680
  279.4 15.0 %collective-permute-start.41 = (bf16[64,2048]{1,0:T(8,128)(2,1)}, bf16[64,2048]{1,0:T(8,128)(2,1)S(1)}, u32[]{:S(2)}, u32[]{:S(2)}) collective-permute-start(bf16[64,2048]{1,0:T(8,128)(2,1)} %get-tuple-element.199.refs_1_), channel_id=1, source_target_pairs={{0,1},{1,2},{2,3},{3,0},{4,5},{5,6},{6,7},{7,4},{8,9},{9,10},{10,1... | collective-permute-start | bytes 786440 | tf_op jit(solution)/shard_map/ppermute | solution.py:680
  288.8 11.2 %collective-permute-start.43 = (bf16[64,2048]{1,0:T(8,128)(2,1)S(1)}, bf16[64,2048]{1,0:T(8,128)(2,1)S(1)}, u32[]{:S(2)}, u32[]{:S(2)}) collective-permute-start(bf16[64,2048]{1,0:T(8,128)(2,1)S(1)} %collective-permute-done.37.refs_4_), channel_id=1, source_target_pairs={{0,1},{1,2},{2,3},{3,0},{4,5},{5,6},{6,7},{7,4},{8,9},{9,10},{10,1... | collective-permute-start | bytes 786440 | tf_op jit(solution)/shard_map/ppermute | solution.py:680
  294.5 11.2 %collective-permute-start.42 = (bf16[64,2048]{1,0:T(8,128)(2,1)S(1)}, bf16[64,2048]{1,0:T(8,128)(2,1)S(1)}, u32[]{:S(2)}, u32[]{:S(2)}) collective-permute-start(bf16[64,2048]{1,0:T(8,128)(2,1)S(1)} %collective-permute-done.41.refs_3_), channel_id=1, source_target_pairs={{0,1},{1,2},{2,3},{3,0},{4,5},{5,6},{6,7},{7,4},{8,9},{9,10},{10,1... | collective-permute-start | bytes 786440 | tf_op jit(solution)/shard_map/ppermute | solution.py:680
  300.1 10.9 %collective-permute-start.45 = (bf16[64,2048]{1,0:T(8,128)(2,1)S(1)}, bf16[64,2048]{1,0:T(8,128)(2,1)S(1)}, u32[]{:S(2)}, u32[]{:S(2)}) collective-permute-start(bf16[64,2048]{1,0:T(8,128)(2,1)S(1)} %collective-permute-done.43.refs_6_), channel_id=1, source_target_pairs={{0,1},{1,2},{2,3},{3,0},{4,5},{5,6},{6,7},{7,4},{8,9},{9,10},{10,1... | collective-permute-start | bytes 786440 | tf_op jit(solution)/shard_map/ppermute | solution.py:680
  305.7 8.2 %collective-permute-start.44 = (bf16[64,2048]{1,0:T(8,128)(2,1)S(1)}, bf16[64,2048]{1,0:T(8,128)(2,1)S(1)}, u32[]{:S(2)}, u32[]{:S(2)}) collective-permute-start(bf16[64,2048]{1,0:T(8,128)(2,1)S(1)} %collective-permute-done.42.refs_5_), channel_id=1, source_target_pairs={{0,1},{1,2},{2,3},{3,0},{4,5},{5,6},{6,7},{7,4},{8,9},{9,10},{10,1... | collective-permute-start | bytes 786440 | tf_op jit(solution)/shard_map/ppermute | solution.py:680
  331.6 4.4 collective-permute-start.46
  331.9 14.2 %collective-permute-start.38 = (bf16[128,2048]{1,0:T(8,128)(2,1)S(1)}, bf16[128,2048]{1,0:T(8,128)(2,1)S(1)}, u32[]{:S(2)}, u32[]{:S(2)}) collective-permute-start(bf16[128,2048]{1,0:T(8,128)(2,1)S(1)} %copy-done.62), channel_id=1, source_target_pairs={{0,3},{1,0},{2,1},{3,2},{4,7},{5,4},{6,5},{7,6},{8,11},{9,8},{10,9... | collective-permute-start | bytes 1572872 | tf_op jit(solution)/shard_map/ppermute | solution.py:874
  341.5 5.8 %collective-permute-start.47 = (f32[8,128]{1,0:T(8,128)}, f32[8,128]{1,0:T(8,128)S(1)}, u32[]{:S(2)}, u32[]{:S(2)}) collective-permute-start(f32[8,128]{1,0:T(8,128)} %mark.1), channel_id=1, source_target_pairs={{0,4},{4,0},{8,12},{12,8},{16,20},{20,16},{24,28},{28,24},{1,5},{5... | collective-permute-start | bytes 12296 | tf_op jit(solution)/shard_map/ppermute | solution.py:683
  341.7 36.3 %collective-permute-start.39 = (bf16[128,2048]{1,0:T(8,128)(2,1)}, bf16[128,2048]{1,0:T(8,128)(2,1)S(1)}, u32[]{:S(2)}, u32[]{:S(2)}) collective-permute-start(bf16[128,2048]{1,0:T(8,128)(2,1)} %get-tuple-element.195), channel_id=1, source_target_pairs={{0,2},{1,3},{2,0},{3,1},{4,6},{5,7},{6,4},{7,5},{8,10},{9,11},{10,... | collective-permute-start | bytes 1572872 | tf_op jit(solution)/shard_map/ppermute | solution.py:874
  341.7 36.3 %collective-permute-start.40 = (bf16[128,2048]{1,0:T(8,128)(2,1)}, bf16[128,2048]{1,0:T(8,128)(2,1)S(1)}, u32[]{:S(2)}, u32[]{:S(2)}) collective-permute-start(bf16[128,2048]{1,0:T(8,128)(2,1)} %get-tuple-element.196), channel_id=1, source_target_pairs={{0,1},{1,2},{2,3},{3,0},{4,5},{5,6},{6,7},{7,4},{8,9},{9,10},{10,1... | collective-permute-start | bytes 1572872 | tf_op jit(solution)/shard_map/ppermute | solution.py:874
  342.1 36.0 %collective-permute-start.48 = (bf16[512,512]{1,0:T(8,128)(2,1)}, bf16[512,512]{1,0:T(8,128)(2,1)S(1)}, u32[]{:S(2)}, u32[]{:S(2)}) collective-permute-start(bf16[512,512]{1,0:T(8,128)(2,1)} %get-tuple-element.205.refs_0_), channel_id=1, source_target_pairs={{8,0},{12,4},{24,16},{28,20},{9,1},{13,5},{25,17},{29,21},{10,2},{... | collective-permute-start | bytes 1572872 | tf_op jit(solution)/shard_map/ppermute | solution.py:697
  346.1 41.8 %collective-permute-start.49 = (bf16[512,512]{1,0:T(8,128)(2,1)}, bf16[512,512]{1,0:T(8,128)(2,1)S(1)}, u32[]{:S(2)}, u32[]{:S(2)}) collective-permute-start(bf16[512,512]{1,0:T(8,128)(2,1)} %get-tuple-element.206.refs_1_), channel_id=1, source_target_pairs={{16,0},{20,4},{24,8},{28,12},{17,1},{21,5},{25,9},{29,13},{18,2},{... | collective-permute-start | bytes 1572872 | tf_op jit(solution)/shard_map/ppermute | solution.py:697
  347.4 40.5 %collective-permute-start.50 = (bf16[512,512]{1,0:T(8,128)(2,1)}, bf16[512,512]{1,0:T(8,128)(2,1)S(1)}, u32[]{:S(2)}, u32[]{:S(2)}) collective-permute-start(bf16[512,512]{1,0:T(8,128)(2,1)} %get-tuple-element.207.refs_2_), channel_id=1, source_target_pairs={{16,8},{20,12},{17,9},{21,13},{18,10},{22,14},{19,11},{23,15}} | collective-permute-start | bytes 1572872 | tf_op jit(solution)/shard_map/ppermute | solution.py:697
  403.0 11.3 %collective-permute-start.51 = (bf16[64,2048]{1,0:T(8,128)(2,1)}, bf16[64,2048]{1,0:T(8,128)(2,1)S(1)}, u32[]{:S(2)}, u32[]{:S(2)}) collective-permute-start(bf16[64,2048]{1,0:T(8,128)(2,1)} %get-tuple-element.213), channel_id=1, source_target_pairs={{0,1},{1,2},{2,3},{3,0},{4,5},{5,6},{6,7},{7,4},{8,9},{9,10},{10,1... | collective-permute-start | bytes 786440 | tf_op jit(solution)/shard_map/ppermute | solution.py:680
  404.5 14.2 %collective-permute-start.52 = (bf16[64,2048]{1,0:T(8,128)(2,1)}, bf16[64,2048]{1,0:T(8,128)(2,1)S(1)}, u32[]{:S(2)}, u32[]{:S(2)}) collective-permute-start(bf16[64,2048]{1,0:T(8,128)(2,1)} %get-tuple-element.214), channel_id=1, source_target_pairs={{0,1},{1,2},{2,3},{3,0},{4,5},{5,6},{6,7},{7,4},{8,9},{9,10},{10,1... | collective-permute-start | bytes 786440 | tf_op jit(solution)/shard_map/ppermute | solution.py:680
  420.6 11.1 %collective-permute-start.54 = (bf16[64,2048]{1,0:T(8,128)(2,1)S(1)}, bf16[64,2048]{1,0:T(8,128)(2,1)S(1)}, u32[]{:S(2)}, u32[]{:S(2)}) collective-permute-start(bf16[64,2048]{1,0:T(8,128)(2,1)S(1)} %add_convert_fusion.2), channel_id=1, source_target_pairs={{0,1},{1,2},{2,3},{3,0},{4,5},{5,6},{6,7},{7,4},{8,9},{9,10},{10,1... | collective-permute-start | bytes 786440 | tf_op jit(solution)/shard_map/ppermute | solution.py:680
  421.7 13.5 %collective-permute-start.53 = (bf16[64,2048]{1,0:T(8,128)(2,1)S(1)}, bf16[64,2048]{1,0:T(8,128)(2,1)S(1)}, u32[]{:S(2)}, u32[]{:S(2)}) collective-permute-start(bf16[64,2048]{1,0:T(8,128)(2,1)S(1)} %add_convert_fusion.3), channel_id=1, source_target_pairs={{0,1},{1,2},{2,3},{3,0},{4,5},{5,6},{6,7},{7,4},{8,9},{9,10},{10,1... | collective-permute-start | bytes 786440 | tf_op jit(solution)/shard_map/ppermute | solution.py:680
  423.0 4.4 collective-permute-start.55
  435.3 18.2 %collective-permute-start.57 = (bf16[64,2048]{1,0:T(8,128)(2,1)S(1)}, bf16[64,2048]{1,0:T(8,128)(2,1)S(1)}, u32[]{:S(2)}, u32[]{:S(2)}) collective-permute-start(bf16[64,2048]{1,0:T(8,128)(2,1)S(1)} %add_convert_fusion), channel_id=1, source_target_pairs={{0,1},{1,2},{2,3},{3,0},{4,5},{5,6},{6,7},{7,4},{8,9},{9,10},{10,1... | collective-permute-start | bytes 786440 | tf_op jit(solution)/shard_map/ppermute | solution.py:680
  435.4 18.0 %collective-permute-start.56 = (bf16[64,2048]{1,0:T(8,128)(2,1)S(1)}, bf16[64,2048]{1,0:T(8,128)(2,1)S(1)}, u32[]{:S(2)}, u32[]{:S(2)}) collective-permute-start(bf16[64,2048]{1,0:T(8,128)(2,1)S(1)} %add_convert_fusion.1), channel_id=1, source_target_pairs={{0,1},{1,2},{2,3},{3,0},{4,5},{5,6},{6,7},{7,4},{8,9},{9,10},{10,1... | collective-permute-start | bytes 786440 | tf_op jit(solution)/shard_map/ppermute | solution.py:680
  435.5 14.1 %collective-permute-start.60 = (f32[34,128]{1,0:T(8,128)S(1)}, f32[34,128]{1,0:T(8,128)S(1)}, u32[]{:S(2)}, u32[]{:S(2)}) collective-permute-start(f32[34,128]{1,0:T(8,128)S(1)} %fusion.7), channel_id=1, source_target_pairs={{0,24},{4,28},{8,16},{12,20},{16,8},{20,12},{24,0},{28,4},{1,25},{... | collective-permute-start | bytes 52232 | tf_op jit(solution)/shard_map/ppermute | solution.py:683
  445.5 6.4 %collective-permute-start.59 = (f32[34,128]{1,0:T(8,128)S(1)}, f32[34,128]{1,0:T(8,128)S(1)}, u32[]{:S(2)}, u32[]{:S(2)}) collective-permute-start(f32[34,128]{1,0:T(8,128)S(1)} %fusion.7), channel_id=1, source_target_pairs={{0,16},{4,20},{8,24},{12,28},{16,0},{20,4},{24,8},{28,12},{1,17},{... | collective-permute-start | bytes 52232 | tf_op jit(solution)/shard_map/ppermute | solution.py:683
  453.5 12.8 %collective-permute-start.63 = (f32[34,128]{1,0:T(8,128)S(1)}, f32[34,128]{1,0:T(8,128)S(1)}, u32[]{:S(2)}, u32[]{:S(2)}) collective-permute-start(f32[34,128]{1,0:T(8,128)S(1)} %add_add_fusion.1), channel_id=1, source_target_pairs={{0,3},{1,0},{2,1},{3,2},{4,7},{5,4},{6,5},{7,6},{8,11},{9,8},{10,9... | collective-permute-start | bytes 52232 | tf_op jit(solution)/shard_map/ppermute | solution.py:934
  457.3 8.9 %collective-permute-start.62 = (f32[34,128]{1,0:T(8,128)S(1)}, f32[34,128]{1,0:T(8,128)S(1)}, u32[]{:S(2)}, u32[]{:S(2)}) collective-permute-start(f32[34,128]{1,0:T(8,128)S(1)} %add_add_fusion.1), channel_id=1, source_target_pairs={{0,2},{1,3},{2,0},{3,1},{4,6},{5,7},{6,4},{7,5},{8,10},{9,11},{10,... | collective-permute-start | bytes 52232 | tf_op jit(solution)/shard_map/ppermute | solution.py:934
  457.9 8.4 %collective-permute-start.61 = (f32[34,128]{1,0:T(8,128)S(1)}, f32[34,128]{1,0:T(8,128)S(1)}, u32[]{:S(2)}, u32[]{:S(2)}) collective-permute-start(f32[34,128]{1,0:T(8,128)S(1)} %add_add_fusion.1), channel_id=1, source_target_pairs={{0,1},{1,2},{2,3},{3,0},{4,5},{5,6},{6,7},{7,4},{8,9},{9,10},{10,1... | collective-permute-start | bytes 52232 | tf_op jit(solution)/shard_map/ppermute | solution.py:934
  (68 other events, 867.8 us)
Sparse Core Ops, SparseCore 0:
  10.7 48.2 all-gather.4
  60.8 118.9 all-gather.2
  247.1 145.3 reduce-scatter.2
  397.0 74.9 reduce-scatter.4
